TPU v7x, 32 devices: a whole 2x2x4 slice. The times are simulated.
32 devices in a mesh: box: 8 (over z, core), dir: 4 (over y, x).
Axes of the slice: x: 2, y: 2, z: 4, core: 2. Of those that a mesh axis runs over, the one named last changes fastest.
Arguments:
- child_out: bfloat16 [1024, 8, 512], P('box', None, 'dir'), may hold values from -6 to 6
- interp: bfloat16 [512, 2048], replicated, may hold values from -0.25 to 0.25
- shift_angle: float32 [8, 2048], replicated, may hold values from -3.140625 to 3.140625
- translators: float32 [343, 2, 2048], P(None, None, 'dir'), may hold values from -3 to 3
- nbr_index: int32 [128, 27], replicated, may hold values from 0 to 127, as said below
- nbr_trans: int32 [128, 27], replicated, may hold values from 0 to 342, as said below
Outputs:
- child_in: bfloat16 [1024, 8, 512], P('box', None, 'dir')
Inputs may be any that keep to these rules, and one draw needn't show every extreme that they name: Parents lie on a periodic slab indexed in Morton order: all index bits but the top two are taken in turn by the first two coordinates (lowest bit first), and the top two bits give the third coordinate, which thus runs over 4 layers. Row p holds 27 distinct offsets of largest component 2 or 3, and nbr_index[p, n] is the parent at that offset from p, coordinates taken periodically. nbr_trans[p, n] = (dx + 3) * 49 + (dy + 3) * 7 + (dz + 3) for the offset (dx, dy, dz) of nbr_index[p, n].
All inputs are finite; a program needn't handle non-finite values.
Results may differ from a plain program's by a relative error of at most 0.012.
Values may be sent and summed in bfloat16 or wider, within the bound.
No kernel may reach another device: no remote copies, remote signals or barrier semaphores. Data moves between devices by JAX's collectives and lax.ppermute only.
A program may use at most 64 MiB of HBM per device.

v0:
```python
import jax
import jax.numpy as jnp
from jax import lax
from jax.sharding import PartitionSpec as P

CH = 8


anterp_scale = 0.125


def cmul(field, real_part, imag_part):
    half = field.shape[-2] // 2
    left = field[..., :half, :]
    right = field[..., half:, :]
    return jnp.concatenate(
        [left * real_part - right * imag_part, left * imag_part + right * real_part], axis=-2
    )


def phases(count, table):
    octants = jnp.arange(count, dtype=jnp.int32) % table.shape[0]
    onehot = (octants[:, None] == jnp.arange(table.shape[0], dtype=jnp.int32)[None, :]).astype(
        jnp.float32
    )
    return jnp.dot(onehot, table, precision=lax.Precision.HIGHEST)


def translate(source, partners, offsets, table):

    def add_slot(slot, total):
        which = lax.dynamic_index_in_dim(partners, slot, 1, keepdims=False)
        offset_col = lax.dynamic_index_in_dim(offsets, slot, 1, keepdims=False)
        picked = jnp.take(source, which, axis=0).astype(jnp.float32)
        factors = jnp.take(table, offset_col, axis=0)
        return total + cmul(picked, factors[:, 0:1, :], factors[:, 1:2, :])

    empty = jnp.zeros((partners.shape[0], source.shape[1], source.shape[2]), jnp.float32)
    total = lax.fori_loop(0, partners.shape[1], add_slot, empty)
    return total.astype(jnp.bfloat16)


def per_device(child_out, interp, shift_angle, translators, nbr_index, nbr_trans):
    cols = child_out.shape[1]
    child_cnt = child_out.shape[0]
    par_cnt = child_cnt // CH
    ncd = interp.shape[0]
    npd = interp.shape[1]
    ndir = lax.axis_size("dir")
    box_at = lax.axis_index("box")
    per_dir = par_cnt // ndir
    cos_table = jnp.cos(shift_angle)
    sin_table = jnp.sin(shift_angle)
    grouped = child_out.reshape(par_cnt, CH, cols, child_out.shape[2])
    mine = lax.all_to_all(grouped, "dir", split_axis=0, concat_axis=3, tiled=True)
    cos_mine = phases(per_dir * CH, cos_table)[:, None, :]
    sin_mine = phases(per_dir * CH, sin_table)[:, None, :]
    interp_child = jnp.dot(
        mine.reshape(per_dir * CH * cols, ncd), interp, preferred_element_type=jnp.float32
    ).reshape(per_dir * CH, cols, npd)
    summed = (
        cmul(interp_child, cos_mine, sin_mine)
        .reshape(per_dir, CH, cols, npd)
        .sum(axis=1)
        .astype(jnp.bfloat16)
    )
    parent_out = lax.all_to_all(summed, "dir", split_axis=2, concat_axis=0, tiled=True)
    everyone = lax.all_gather(parent_out, "box", axis=0, tiled=True)
    partners = lax.dynamic_slice_in_dim(nbr_index, box_at * par_cnt, par_cnt, 0)
    offsets = lax.dynamic_slice_in_dim(nbr_trans, box_at * par_cnt, par_cnt, 0)
    parent_in = translate(everyone, partners, offsets, translators)
    whole_in = lax.all_to_all(parent_in, "dir", split_axis=0, concat_axis=2, tiled=True)
    down = (
        jnp.broadcast_to(whole_in[:, None], (per_dir, CH, cols, npd))
        .reshape(per_dir * CH, cols, npd)
        .astype(jnp.float32)
    )
    back = cmul(down, cos_mine, -sin_mine).astype(jnp.bfloat16)
    local = jnp.einsum(
        "rj,kj->rk",
        back.reshape(per_dir * CH * cols, npd),
        interp,
        preferred_element_type=jnp.float32,
    )
    local = (anterp_scale * local).reshape(per_dir * CH, cols, ncd).astype(jnp.bfloat16)
    child_in = lax.all_to_all(local, "dir", split_axis=2, concat_axis=0, tiled=True)
    return child_in


def solution(mesh):
    in_specs = (P("box", None, "dir"), P(), P(), P(None, None, "dir"), P(), P())
    out_specs = P("box", None, "dir")
    return jax.shard_map(
        per_device, mesh=mesh, in_specs=in_specs, out_specs=out_specs, check_vma=False
    )
```

profile of v0, /device:TPU:0, one launch (start us, length us, event | category | flops | bytes accessed | tf_op | source)
XLA Modules:
  0.0 209.6 jit_solution(1423788445319677335)
XLA Ops:
  6.5 5.3 %all-to-all-start = ((bf16[16,8,8,128]{3,2,1,0:T(8,128)(2,1)}), bf16[16,8,8,128]{3,2,1,0:T(8,128)(2,1)S(1)}, u32[]{:S(2)}, u32[]{:S(2)}) async-start(bf16[16,8,8,128]{3,2,1,0:T(8,128)(2,1)} %bitcast.70), calls=%async_computation | async-start | bytes 524288 | tf_op jit(solution)/shard_map/all_to_all | solution.py:55
  14.5 2.8 %all-to-all-done = bf16[16,8,8,128]{3,2,1,0:T(8,128)(2,1)S(1)} async-done(((bf16[16,8,8,128]{3,2,1,0:T(8,128)(2,1)}), bf16[16,8,8,128]{3,2,1,0:T(8,128)(2,1)S(1)}, u32[]{:S(2)}, u32[]{:S(2)}) %all-to-all-start) | async-done | bytes 262176 | tf_op jit(solution)/shard_map/all_to_all | solution.py:55
  19.1 2.4 %copy.22 = bf16[4,8,2048]{1,0,2:T(4,128)(2,1)} copy(bf16[4,8,2048]{2,1,0:T(8,128)(2,1)S(1)} %bitcast_reduce_fusion) | data formatting | bytes 262144 | tf_op jit(solution)/shard_map/convert_element_type | solution.py:65
  21.6 3.4 %reshape.76 = bf16[4,2,8192]{2,1,0:T(2,128)(2,1)S(1)} reshape(bf16[2048,4,8]{2,1,0:T(4,128)(2,1)} %bitcast.59) | data formatting | bytes 262144
  25.0 7.4 %all_to_all.60 = bf16[4,2,8192]{2,1,0:T(2,128)(2,1)S(1)} all-to-all(bf16[4,2,8192]{2,1,0:T(2,128)(2,1)S(1)} %reshape.76), channel_id=1, replica_groups=mesh['box'=8,'dir'=4] {'dir'}, dimensions={0} | all-to-all | bytes 262144 | tf_op jit(solution)/shard_map/all_to_all | solution.py:67
  32.4 3.5 %reshape.77 = bf16[2048,4,8]{2,1,0:T(4,128)(2,1)} reshape(bf16[4,2,8192]{2,1,0:T(2,128)(2,1)S(1)} %all_to_all.60) | data formatting | bytes 262144
  35.9 3.8 %copy.24 = bf16[4,4,8,512]{3,2,1,0:T(8,128)(2,1)} copy(bf16[4,4,8,512]{2,1,3,0:T(4,128)(2,1)} %bitcast.60) | data formatting | bytes 262144 | tf_op jit(solution)/shard_map/all_to_all | solution.py:67
  39.8 22.0 %all-gather.2.cloned.1.call-done = bf16[128,8,512]{2,1,0:T(8,128)(2,1)} async-done(((bf16[16,8,512]{2,1,0:T(8,128)(2,1)}), bf16[128,8,512]{2,1,0:T(8,128)(2,1)}) %all-gather.2.cloned.1.call-update) | async-done | bytes 1048592 | tf_op jit(solution)/shard_map/all_gather | solution.py:68
  61.8 116.5 %while.14 = (s32[]{:T(128)}, f32[16,8,512]{2,1,0:T(8,128)S(1)}, s32[16,27]{0,1:T(8,128)S(1)}, bf16[128,8,512]{2,1,0:T(8,128)(2,1)}, s32[16,27]{0,1:T(8,128)S(1)}...) while((s32[]{:T(128)}, f32[16,8,512]{2,1,0:T(8,128)S(1)}, s32[16,27]{0,1:T(8,128)S(1)}, ...), condition=%wide.region_2.3_spmd.clone, body=%wide.region_1.2_spmd.clone.sunk | while | flops 542915 | bytes 2564771 | solution.py:39
  66.2 2.0 gather_fusion.1
  70.5 2.0 gather_fusion.1
  83.4 2.0 gather_fusion.1
  87.8 2.0 gather_fusion.1
  105.0 2.0 gather_fusion.1
  109.3 2.0 gather_fusion.1
  113.7 2.0 gather_fusion.1
  122.3 2.0 gather_fusion.1
  130.9 2.0 gather_fusion.1
  135.2 2.0 gather_fusion.1
  148.2 2.0 gather_fusion.1
  152.5 2.0 gather_fusion.1
  156.8 2.0 gather_fusion.1
  178.4 8.5 %all_to_all.61 = bf16[16,8,512]{2,1,0:T(8,128)(2,1)S(1)} all-to-all(bf16[16,8,512]{2,1,0:T(8,128)(2,1)S(1)} %convert_element_type.43), channel_id=1, replica_groups=mesh['box'=8,'dir'=4] {'dir'}, dimensions={0} | all-to-all | bytes 262144 | tf_op jit(solution)/shard_map/all_to_all | solution.py:72
  190.7 8.8 %all_to_all.62 = bf16[4,2,16384]{2,1,0:T(2,128)(2,1)} all-to-all(bf16[4,2,16384]{2,1,0:T(2,128)(2,1)S(1)} %reshape.78), channel_id=1, replica_groups=mesh['box'=8,'dir'=4] {'dir'}, dimensions={0} | all-to-all | bytes 524288 | tf_op jit(solution)/shard_map/all_to_all | solution.py:86
  (338 shorter events, 99.6 us)
Async XLA Ops:
  6.5 10.8 %copy-start = (bf16[512,2048]{1,0:T(8,128)(2,1)S(1)}, bf16[512,2048]{1,0:T(8,128)(2,1)}, u32[]{:S(2)}) copy-start(bf16[512,2048]{1,0:T(8,128)(2,1)} %param.9) | copy-start | bytes 6291460
  6.5 10.7 %all-to-all-start = ((bf16[16,8,8,128]{3,2,1,0:T(8,128)(2,1)}), bf16[16,8,8,128]{3,2,1,0:T(8,128)(2,1)S(1)}, u32[]{:S(2)}, u32[]{:S(2)}) async-start(bf16[16,8,8,128]{3,2,1,0:T(8,128)(2,1)} %bitcast.70), calls=%async_computation | async-start | bytes 524288 | tf_op jit(solution)/shard_map/all_to_all | solution.py:55
  11.9 50.0 %all-gather.2.cloned.1.call-start = ((), (), s32[]{:S(2)}) async-start(), calls=%async_computation.4 | async-start | bytes 1179648 | tf_op jit(solution)/shard_map/all_gather | solution.py:68
  32.4 7.3 %copy-start.1 = (s32[128,27]{0,1:T(8,128)S(1)}, s32[128,27]{0,1:T(8,128)}, u32[]{:S(2)}) copy-start(s32[128,27]{0,1:T(8,128)} %param.13) | copy-start | bytes 41476
  32.4 7.4 %copy-start.2 = (s32[128,27]{0,1:T(8,128)S(1)}, s32[128,27]{0,1:T(8,128)}, u32[]{:S(2)}) copy-start(s32[128,27]{0,1:T(8,128)} %param.12) | copy-start | bytes 41476
Sparse Core Ops, SparseCore 0:
  39.8 21.9 all-gather.1
where the time goes:
time: 212 us; the launch traced here: 210 us
  local copies, waits for them, and re-layouts  122 us (58%)
  waiting for transfers between devices  24.8 us (12%)
  blocking collectives  24.7 us (12%)
  between operations  13.6 us (6%)
  other arithmetic  12.4 us (6%)
  starting transfers between devices  5.33 us (3%)
  matrix products  4.05 us (2%)
  loops' own time  2.88 us (1%)
    gather x27, local copies, waits for them, and re-layouts, add_slot(): factors = jnp.take(table, offset_col, axis=0)  53.3 us
    gather x27, local copies, waits for them, and re-layouts, add_slot(): picked = jnp.take(source, which, axis=0).astype(jnp.float32)  48.1 us
    all_gather x1, waiting for transfers between devices, per_device(): everyone = lax.all_gather(parent_out, 'box', axis=0, tiled=True)  22 us
    unnamed x10, local copies, waits for them, and re-layouts  9.79 us
    all_to_all x1, blocking collectives, per_device(): lax.all_to_all(local, 'dir', split_axis=2, concat_axis=0, tiled=True)  8.79 us
    all_to_all x1, blocking collectives, per_device(): lax.all_to_all(parent_in, 'dir', split_axis=0, concat_axis=2, tiled=True)  8.47 us
    all_to_all x1, blocking collectives, per_device(): lax.all_to_all(summed, 'dir', split_axis=2, concat_axis=0, tiled=True)  7.41 us
    all_to_all x1, starting transfers between devices, per_device(): lax.all_to_all(grouped, 'dir', split_axis=0, concat_axis=3, tiled=True)  5.32 us
  transfers between devices with their start and end apart: 2, of which 2 were waited for; matrix products, arithmetic and copies ran while one was open for 1% of the time, Pallas kernels for 0%

commit v1 on v0

v1 whole, which is shorter than its diff:
```python
import functools

import jax
import jax.numpy as jnp
from jax import lax
from jax.experimental import pallas as pl
from jax.experimental.pallas import tpu as pltpu
from jax.sharding import PartitionSpec as P

CH = 8
LANES = 128
anterp_scale = 0.125

VMEM = pl.BlockSpec(memory_space=pltpu.VMEM)
SMEM = pl.BlockSpec(memory_space=pltpu.SMEM)


def half_sign(rows, first):
    row = lax.broadcasted_iota(jnp.int32, (rows, LANES), 0)
    return jnp.where(row < rows // 2, first, -first).astype(jnp.float32)


def forward_kernel(masks, chunks, at_ref, x_ref, interp_ref, cos_ref, sin_ref, *rest):
    outs, field = rest[: len(masks)], rest[len(masks)]
    par_cnt, cols = outs[0].shape[1], outs[0].shape[2]
    width = chunks * LANES
    sign = half_sign(cols, -1.0)
    for mask, out_ref in zip(masks, outs):
        start = pl.multiple_of((at_ref[0] ^ mask) * width, width)
        field[...] = jnp.dot(
            x_ref[...], interp_ref[:, pl.ds(start, width)], preferred_element_type=jnp.float32
        )
        for chunk in range(chunks):
            lanes = pl.ds(pl.multiple_of(start + chunk * LANES, LANES), LANES)
            cosine = jnp.broadcast_to(cos_ref[:, lanes][:, None, :], (CH, cols, LANES))
            sine = jnp.broadcast_to(sin_ref[:, lanes][:, None, :], (CH, cols, LANES))

            def one(p, carry, chunk=chunk, cosine=cosine, sine=sine, out_ref=out_ref):
                rows = pl.ds(pl.multiple_of(p * CH * cols, CH * cols), CH * cols)
                part = field[rows, chunk * LANES : (chunk + 1) * LANES].reshape(CH, cols, LANES)
                same = jnp.sum(part * cosine, axis=0)
                cross = jnp.sum(part * sine, axis=0)
                total = same + sign * pltpu.roll(cross, cols // 2, 0)
                out_ref[chunk, p] = total.astype(out_ref.dtype)
                return carry

            lax.fori_loop(0, par_cnt, one, 0, unroll=4)


def forward(masks, chunks, at, x, interp, cosine, sine, cols):
    rows = x.shape[0]
    par_cnt = rows // (CH * cols)
    shape = (chunks, par_cnt, cols, LANES)
    return pl.pallas_call(
        functools.partial(forward_kernel, masks, chunks),
        out_shape=[
            jax.ShapeDtypeStruct(shape, jnp.bfloat16 if mask else jnp.float32) for mask in masks
        ],
        in_specs=[SMEM, VMEM, VMEM, VMEM, VMEM],
        out_specs=[VMEM] * len(masks),
        scratch_shapes=[pltpu.VMEM((rows, chunks * LANES), jnp.float32)],
        name="forward",
    )(at, x, interp, cosine, sine)


def translate_kernel(zc, rest, slots, at_ref, picks_ref, table_ref, *refs):
    count = len(refs) - zc - 1
    pieces, outs, source = refs[:count], refs[count : count + zc], refs[count + zc]
    par_cnt, cols = outs[0].shape[0], outs[0].shape[1]
    zi, ci = at_ref[0], at_ref[1]
    each = count // zc
    for s in range(zc):
        for t in range(each):
            box = (zi ^ s) * rest + ((ci ^ t) if each > 1 else 0)
            piece = pieces[s * each + t]
            here = piece.shape[0]
            source[pl.ds(box * par_cnt, here)] = piece[...].astype(jnp.float32)
    sign = half_sign(cols, -1.0)
    for s in range(zc):
        first = ((zi ^ s) * rest + ci) * par_cnt

        def one(p, carry, first=first, out_ref=outs[s]):
            same = jnp.zeros((cols, LANES), jnp.float32)
            cross = jnp.zeros((cols, LANES), jnp.float32)
            for slot in range(slots):
                word = picks_ref[slot, first + p]
                which, offset = word & 0xFFFF, word >> 16
                value = source[which]
                real = table_ref[pl.ds(offset, 1), :]
                imag = table_ref[pl.ds(offset + 1, 1), :]
                same += value * real
                cross += value * imag
            total = same + sign * pltpu.roll(cross, cols // 2, 0)
            out_ref[p] = total.astype(out_ref.dtype)
            return carry

        lax.fori_loop(0, par_cnt, one, 0)


def translate(zc, rest, par_cnt, at, picks, table, pieces):
    cols, lanes = pieces[0].shape[1:]
    return pl.pallas_call(
        functools.partial(translate_kernel, zc, rest, picks.shape[0]),
        out_shape=[jax.ShapeDtypeStruct((par_cnt, cols, lanes), jnp.bfloat16)] * zc,
        in_specs=[SMEM, SMEM, VMEM] + [VMEM] * len(pieces),
        out_specs=[VMEM] * zc,
        scratch_shapes=[pltpu.VMEM((zc * rest * par_cnt, cols, lanes), jnp.float32)],
        name="translate",
    )(at, picks, table, *pieces)


def backward_kernel(masks, wide, last, at_ref, interp_ref, cos_ref, sin_ref, *refs):
    quarters = refs[: len(masks)]
    held = refs[len(masks)] if len(refs) == len(masks) + 4 else None
    out_ref, left, right = refs[-3:]
    chunks, par_cnt, cols, _ = quarters[0].shape
    width = chunks * LANES
    sign = half_sign(cols, 1.0)
    total = None
    for mask, quarter in zip(masks, quarters):
        for chunk in range(chunks):
            place = (at_ref[1] ^ (chunk // wide)) * wide + chunk % wide
            start = (at_ref[0] ^ mask) * width + place * LANES
            lanes = pl.ds(pl.multiple_of(start, LANES), LANES)
            cosine = jnp.broadcast_to(cos_ref[:, lanes][:, None, :], (CH, cols, LANES))
            sine = jnp.broadcast_to(sin_ref[:, lanes][:, None, :], (CH, cols, LANES)) * sign[None]
            here = slice(chunk * LANES, (chunk + 1) * LANES)
            right[:, here] = interp_ref[:, lanes]

            def one(p, carry, chunk=chunk, cosine=cosine, sine=sine, here=here, quarter=quarter):
                field = quarter[chunk, p].astype(jnp.float32)
                turned = pltpu.roll(field, cols // 2, 0)
                moved = field[None] * cosine + turned[None] * sine
                rows = pl.ds(pl.multiple_of(p * CH * cols, CH * cols), CH * cols)
                left[rows, here] = moved.reshape(CH * cols, LANES).astype(jnp.bfloat16)
                return carry

            lax.fori_loop(0, par_cnt, one, 0, unroll=4)
        part = lax.dot_general(
            left[...], right[...], (((1,), (1,)), ((), ())), preferred_element_type=jnp.float32
        )
        total = part if total is None else total + part
    if held is not None:
        total = total + held[...]
    if last:
        total = anterp_scale * total
    out_ref[...] = total.astype(out_ref.dtype)


def backward(masks, wide, last, at, interp, cosine, sine, quarters, held):
    chunks, par_cnt, cols, _ = quarters[0].shape
    rows = par_cnt * CH * cols
    kept = [] if held is None else [held]
    return pl.pallas_call(
        functools.partial(backward_kernel, masks, wide, last),
        out_shape=jax.ShapeDtypeStruct(
            (rows, interp.shape[0]), jnp.bfloat16 if last else jnp.float32
        ),
        in_specs=[SMEM, VMEM, VMEM, VMEM] + [VMEM] * (len(masks) + len(kept)),
        out_specs=VMEM,
        scratch_shapes=[
            pltpu.VMEM((rows, chunks * LANES), jnp.bfloat16),
            pltpu.VMEM((interp.shape[0], chunks * LANES), jnp.bfloat16),
        ],
        name="backward",
    )(at, interp, cosine, sine, *quarters, *kept)


def exchange(value, axis, mask):
    size = lax.axis_size(axis)
    return lax.ppermute(value, axis, [(i, i ^ mask) for i in range(size)])


def per_device(child_out, interp, shift_angle, translators, nbr_index, nbr_trans):
    child_cnt, cols, kq = child_out.shape
    par_cnt = child_cnt // CH
    npd = interp.shape[1]
    ndir, nbox = lax.axis_size("dir"), lax.axis_size("box")
    jq = npd // ndir
    zc = 1
    while nbox % (2 * zc) == 0 and zc * 2 < nbox and jq % (2 * zc * LANES) == 0:
        zc *= 2
    rest = nbox // zc
    chunks = jq // LANES
    dir_at, box_at = lax.axis_index("dir"), lax.axis_index("box")
    zi, ci = box_at // rest, box_at % rest
    at = jnp.stack([dir_at, zi, ci]).astype(jnp.int32)

    x = child_out.reshape(child_cnt * cols, kq)
    mine = lax.dynamic_slice_in_dim(interp, dir_at * kq, kq, 0)
    cosine, sine = jnp.cos(shift_angle), jnp.sin(shift_angle)

    masks = tuple(range(1, ndir)) + (0,)
    parts = forward(masks, chunks, at, x, mine, cosine, sine, cols)
    total = parts[-1]
    for mask, part in zip(masks[:-1], parts):
        total = total + exchange(part, "dir", mask).astype(jnp.float32)
    own = total.astype(jnp.bfloat16).reshape(zc, chunks // zc, par_cnt, cols, LANES)

    wide = chunks // zc
    pieces = []
    for s in range(zc):
        piece = lax.dynamic_index_in_dim(own, zi ^ s, 0, keepdims=False)
        pieces.append(exchange(piece, "box", s * rest) if s else piece)

    table = lax.dynamic_slice_in_dim(translators, zi * wide * LANES, wide * LANES, 2)
    picks = (nbr_index | (nbr_trans * 2 << 16)).T

    if rest == 2:
        pieces = [part for piece in pieces for part in (piece, exchange(piece, "box", 1))]
    else:
        groups = [[z * rest + c for c in range(rest)] for z in range(zc)]
        pieces = [
            lax.all_gather(piece, "box", axis=1, tiled=True, axis_index_groups=groups)
            for piece in pieces
        ]
    back = []
    for w in range(wide):
        rows = table[:, :, w * LANES : (w + 1) * LANES].reshape(-1, LANES)
        parts = [piece[w] for piece in pieces]
        back.append(translate(zc, rest, par_cnt, at[1:], picks, rows, parts))
    quarter = []
    for s in range(zc):
        result = jnp.stack([b[s] for b in back])
        quarter.append(exchange(result, "box", s * rest) if s else result)
    quarter = jnp.concatenate(quarter, 0)

    quarters = [exchange(quarter, "dir", mask) for mask in range(1, ndir)]
    held = backward((0,), wide, False, at, mine, cosine, sine, [quarter], None)
    out = backward(tuple(range(1, ndir)), wide, True, at, mine, cosine, sine, quarters, held)
    return out.reshape(child_cnt, cols, kq)


def solution(mesh):
    in_specs = (P("box", None, "dir"), P(), P(), P(None, None, "dir"), P(), P())
    out_specs = P("box", None, "dir")
    return jax.shard_map(
        per_device, mesh=mesh, in_specs=in_specs, out_specs=out_specs, check_vma=False
    )
```

time: 212 us -> 61 us (0.29)
  local copies, waits for them, and re-layouts: 122 us -> 6.52 us
  blocking collectives: 24.7 us -> 0 us
  Pallas kernels: 0 us -> 19 us
  between operations: 13.6 us -> 0.16 us
  starting transfers between devices: 5.33 us -> 17.7 us
  waiting for transfers between devices: 24.8 us -> 13.7 us
  other arithmetic: 12.4 us -> 3.55 us
  matrix products: 4.05 us -> 0 us
  loops' own time: 2.88 us -> 0 us
    gather x54 -> x0, local copies, waits for them, and re-layouts: 101 us -> none  [the longest x27 53.3 us: add_slot(): factors = jnp.take(table, offset_col, axis=0)]
    all_to_all x3 -> x0, blocking collectives: 24.7 us -> none  [the longest x1 8.79 us: per_device(): lax.all_to_all(local, 'dir', split_axis=2, concat_axis=0, tiled=True)]
    all_gather x1 -> x0, waiting for transfers between devices: 22 us -> none  [per_device(): everyone = lax.all_gather(parent_out, 'box', axis=0, tiled=True)]
    pallas_call x0 -> x4, Pallas kernels: none -> 19 us  [the longest x2 7.48 us: backward(): pl.pallas_call(functools.partial(backward_kernel, masks, wide, last), out...]
    ppermute x0 -> x16, starting transfers between devices: none -> 17.7 us  [exchange(): return lax.ppermute(value, axis, [(i, i ^ mask) for i in range(size)])]
    ppermute x0 -> x16, waiting for transfers between devices: none -> 13.7 us  [exchange(): return lax.ppermute(value, axis, [(i, i ^ mask) for i in range(size)])]
    unnamed x10 -> x30, local copies, waits for them, and re-layouts: 9.79 us -> 1.82 us
    all_to_all x1 -> x0, starting transfers between devices: 5.32 us -> none  [per_device(): lax.all_to_all(grouped, 'dir', split_axis=0, concat_axis=3, tiled=True)]
  transfers between devices with their start and end apart: 2 -> 16, of which waited for: 2 -> 10; matrix products, arithmetic and copies ran while one was open for 1% -> 5% of each run, Pallas kernels for 0% -> 5%
where the time goes in v1:
time: 61 us; the launch traced here: 60.7 us
  Pallas kernels  19 us (31%)
  starting transfers between devices  17.7 us (29%)
  waiting for transfers between devices  13.7 us (22%)
  local copies, waits for them, and re-layouts  6.52 us (11%)
  other arithmetic  3.55 us (6%)
    ppermute x16, starting transfers between devices, exchange(): return lax.ppermute(value, axis, [(i, i ^ mask) for i in range(size)])  17.7 us
    ppermute x16, waiting for transfers between devices, exchange(): return lax.ppermute(value, axis, [(i, i ^ mask) for i in range(size)])  13.7 us
    pallas_call x2, Pallas kernels, backward(): pl.pallas_call(functools.partial(backward_kernel, masks, wide, last), out...  7.48 us
    pallas_call x1, Pallas kernels, translate(): pl.pallas_call(functools.partial(translate_kernel, zc, rest, picks.shape[...  6.02 us
    pallas_call x1, Pallas kernels, forward(): pl.pallas_call(functools.partial(forward_kernel, masks, chunks), out_shap...  5.5 us
    sin x1, local copies, waits for them, and re-layouts, per_device(): cosine, sine = (jnp.cos(shift_angle), jnp.sin(shift_angle))  1.87 us
    unnamed x30, local copies, waits for them, and re-layouts  1.82 us
  transfers between devices with their start and end apart: 16, of which 10 were waited for; matrix products, arithmetic and copies ran while one was open for 5% of the time, Pallas kernels for 5%

profile of v1, /device:TPU:0, one launch (start us, length us, event | category | flops | bytes accessed | tf_op | source)
XLA Modules:
  0.0 60.7 jit_solution(234941874596394516)
XLA Ops:
  0.0 1.9 %fusion = (f32[8,2048]{1,0:T(8,128)}, f32[8,2048]{1,0:T(8,128)}) fusion(f32[8,2048]{1,0:T(8,128)} %param.8), kind=kLoop, calls=%fused_computation.11 | loop fusion | bytes 196608 | tf_op jit(solution)/shard_map/sin | solution.py:191
  1.9 0.8 %constant_dynamic-slice_fusion.5.interp_ref = bf16[128,2048]{1,0:T(8,128)(2,1)} fusion(bf16[512,2048]{1,0:T(8,128)(2,1)S(1)} %copy-done, s32[]{:T(128)S(6)} %select_n.32), kind=kLoop, calls=%fused_computation.8 | loop fusion | bytes 1048580 | tf_op jit(solution)/shard_map/dynamic_slice | solution.py:190
  3.3 5.5 %forward.1 = (bf16[4,16,8,128]{3,2,1,0:T(8,128)(2,1)}, bf16[4,16,8,128]{3,2,1,0:T(8,128)(2,1)}, bf16[4,16,8,128]{3,2,1,0:T(8,128)(2,1)}, f32[4,16,8,128]{3,2,1,0:T(8,128)}) custom-call(s32[3]{0:T(128)} %pad_add_fusion.at_ref, bf16[1024,128]{1,0:T(8,128)(2,1)} %bitcast.19, bf16[128,2048]{1,0:T(8,128)(2,1)} %constant_dynamic-slice_fusion.5.interp_ref, ...), custom_call_target="tpu_custom_call" | custom-call | tf_op jit(solution)/shard_map/forward/pallas_call | solution.py:54
  8.8 3.0 %collective-permute-start = (bf16[4,16,8,128]{3,2,1,0:T(8,128)(2,1)}, bf16[4,16,8,128]{3,2,1,0:T(8,128)(2,1)S(1)}, u32[]{:S(2)}, u32[]{:S(2)}) collective-permute-start(bf16[4,16,8,128]{3,2,1,0:T(8,128)(2,1)} %get-tuple-element.14), channel_id=1, source_target_pairs={{0,1},{1,0},{2,3},{3,2},{4,5},{5,4},{6,7},{7,6},{8,9},{9,8},{10,11... | collective-permute-start | bytes 393224 | tf_op jit(solution)/shard_map/ppermute | solution.py:171
  11.8 1.5 %collective-permute-start.1 = (bf16[4,16,8,128]{3,2,1,0:T(8,128)(2,1)}, bf16[4,16,8,128]{3,2,1,0:T(8,128)(2,1)S(1)}, u32[]{:S(2)}, u32[]{:S(2)}) collective-permute-start(bf16[4,16,8,128]{3,2,1,0:T(8,128)(2,1)} %get-tuple-element.15), channel_id=1, source_target_pairs={{0,2},{1,3},{2,0},{3,1},{4,6},{5,7},{6,4},{7,5},{8,10},{9,11},{10,... | collective-permute-start | bytes 393224 | tf_op jit(solution)/shard_map/ppermute | solution.py:171
  13.9 2.1 %collective-permute-done = bf16[4,16,8,128]{3,2,1,0:T(8,128)(2,1)S(1)} collective-permute-done((bf16[4,16,8,128]{3,2,1,0:T(8,128)(2,1)}, bf16[4,16,8,128]{3,2,1,0:T(8,128)(2,1)S(1)}, u32[]{:S(2)}, u32[]{:S(2)}) %collective-permute-start) | collective-permute-done | bytes 131104 | tf_op jit(solution)/shard_map/ppermute | solution.py:171
  16.0 3.8 %collective-permute-done.1 = bf16[4,16,8,128]{3,2,1,0:T(8,128)(2,1)S(1)} collective-permute-done((bf16[4,16,8,128]{3,2,1,0:T(8,128)(2,1)}, bf16[4,16,8,128]{3,2,1,0:T(8,128)(2,1)S(1)}, u32[]{:S(2)}, u32[]{:S(2)}) %collective-permute-start.1) | collective-permute-done | bytes 131104 | tf_op jit(solution)/shard_map/ppermute | solution.py:171
  19.8 1.0 %add_convert_fusion = bf16[4,16,8,128]{3,2,1,0:T(8,128)(2,1)S(1)} fusion(bf16[4,16,8,128]{3,2,1,0:T(8,128)(2,1)S(1)} %collective-permute-done.2, bf16[4,16,8,128]{3,2,1,0:T(8,128)(2,1)S(1)} %collective-permute-done.1, f32[4,16,8,128]{3,2,1,0:T(8,128)} %get-tuple-element.13, bf16[4,16,8,128]{3,2,1,0:T(8,128)(2,1)S(1)} %collective-permute-done), kind=kLoop, calls=%fused_computation | loop fusion | flops 458752 | bytes 786432 | tf_op jit(solution)/shard_map/convert_element_type | solution.py:198
  20.8 3.7 %collective-permute-start.8 = (bf16[1,16,8,128]{3,2,1,0:T(8,128)(2,1)S(1)}, bf16[1,16,8,128]{3,2,1,0:T(8,128)(2,1)S(1)}, u32[]{:S(2)}, u32[]{:S(2)}) collective-permute-start(bf16[1,16,8,128]{3,2,1,0:T(8,128)(2,1)S(1)} %get-tuple-element.21), channel_id=1, source_target_pairs={{0,24},{4,28},{8,16},{12,20},{16,8},{20,12},{24,0},{28,4},{1,25},{... | collective-permute-start | bytes 98312 | tf_op jit(solution)/shard_map/ppermute | solution.py:171
  24.5 0.8 %collective-permute-start.4 = (bf16[1,16,8,128]{3,2,1,0:T(8,128)(2,1)S(1)}, bf16[1,16,8,128]{3,2,1,0:T(8,128)(2,1)S(1)}, u32[]{:S(2)}, u32[]{:S(2)}) collective-permute-start(bf16[1,16,8,128]{3,2,1,0:T(8,128)(2,1)S(1)} %get-tuple-element.23), channel_id=1, source_target_pairs={{0,8},{4,12},{8,0},{12,4},{16,24},{20,28},{24,16},{28,20},{1,9},{5... | collective-permute-start | bytes 98312 | tf_op jit(solution)/shard_map/ppermute | solution.py:171
  25.3 1.0 %constant_dynamic-slice_fusion.4 = f32[343,2,128]{2,1,0:T(2,128)S(1)} fusion(f32[343,2,512]{2,1,0:T(2,128)} %param.9, s32[]{:T(128)S(6)} %select_n.33), kind=kLoop, calls=%fused_computation.7 | loop fusion | bytes 702468 | tf_op jit(solution)/shard_map/dynamic_slice | solution.py:206
  26.9 2.4 %collective-permute-done.6 = bf16[1,16,8,128]{3,2,1,0:T(8,128)(2,1)S(1)} collective-permute-done((bf16[1,16,8,128]{3,2,1,0:T(8,128)(2,1)S(1)}, bf16[1,16,8,128]{3,2,1,0:T(8,128)(2,1)S(1)}, u32[]{:S(2)}, u32[]{:S(2)}) %collective-permute-start.6) | collective-permute-done | bytes 32800 | tf_op jit(solution)/shard_map/ppermute | solution.py:171
  30.4 1.0 %reshape.19.table_ref = f32[686,128]{1,0:T(8,128)} reshape(f32[343,2,128]{2,1,0:T(2,128)S(1)} %constant_dynamic-slice_fusion.4) | data formatting | bytes 702464 | tf_op jit(solution)/shard_map/reshape | solution.py:219
  32.0 6.0 %translate.1 = (bf16[16,8,128]{2,1,0:T(8,128)(2,1)}, bf16[16,8,128]{2,1,0:T(8,128)(2,1)}, bf16[16,8,128]{2,1,0:T(8,128)(2,1)}, bf16[16,8,128]{2,1,0:T(8,128)(2,1)}) custom-call(s32[2]{0:T(128)} %pad_add_fusion.1.at_ref, s32[27,128]{1,0:T(8,128)} %or_bitcast_fusion.picks_ref, f32[686,128]{1,0:T(8,128)} %reshape.19.table_ref, bf16[16,8,128]{2,1,0:T(8,128)(2,1)} %bitcast.20, ...), custom_call_target="tpu_custom_call" | custom-call | tf_op jit(solution)/shard_map/translate/pallas_call | solution.py:102
  38.1 1.7 %collective-permute-start.11 = (bf16[1,16,8,128]{3,2,1,0:T(8,128)(2,1)}, bf16[1,16,8,128]{3,2,1,0:T(8,128)(2,1)S(1)}, u32[]{:S(2)}, u32[]{:S(2)}) collective-permute-start(bf16[1,16,8,128]{3,2,1,0:T(8,128)(2,1)} %bitcast.30), channel_id=1, source_target_pairs={{0,16},{4,20},{8,24},{12,28},{16,0},{20,4},{24,8},{28,12},{1,17},{... | collective-permute-start | bytes 98312 | tf_op jit(solution)/shard_map/ppermute | solution.py:171
  39.8 2.7 %collective-permute-start.12 = (bf16[1,16,8,128]{3,2,1,0:T(8,128)(2,1)}, bf16[1,16,8,128]{3,2,1,0:T(8,128)(2,1)S(1)}, u32[]{:S(2)}, u32[]{:S(2)}) collective-permute-start(bf16[1,16,8,128]{3,2,1,0:T(8,128)(2,1)} %bitcast.29), channel_id=1, source_target_pairs={{0,24},{4,28},{8,16},{12,20},{16,8},{20,12},{24,0},{28,4},{1,25},{... | collective-permute-start | bytes 98312 | tf_op jit(solution)/shard_map/ppermute | solution.py:171
  43.3 2.4 %collective-permute-done.12 = bf16[1,16,8,128]{3,2,1,0:T(8,128)(2,1)S(1)} collective-permute-done((bf16[1,16,8,128]{3,2,1,0:T(8,128)(2,1)}, bf16[1,16,8,128]{3,2,1,0:T(8,128)(2,1)S(1)}, u32[]{:S(2)}, u32[]{:S(2)}) %collective-permute-start.12) | collective-permute-done | bytes 32800 | tf_op jit(solution)/shard_map/ppermute | solution.py:171
  45.7 0.8 %pad_maximum_fusion.refs_0_ = bf16[4,16,8,128]{3,2,1,0:T(8,128)(2,1)S(1)} fusion(bf16[1,16,8,128]{3,2,1,0:T(8,128)(2,1)S(1)} %collective-permute-done.12, bf16[1,16,8,128]{3,2,1,0:T(8,128)(2,1)S(1)} %collective-permute-done.11, bf16[1,16,8,128]{3,2,1,0:T(8,128)(2,1)S(1)} %collective-permute-done.10, bf16[1,16,8,128]{3,2,1,0:T(8,128)(2,1)} %bitcast.28), kind=kLoop, calls=%fused_computation.1 | loop fusion | flops 196608 | bytes 262144 | tf_op jit(solution)/shard_map/concatenate | solution.py:226
  46.5 1.5 %collective-permute-start.15 = (bf16[4,16,8,128]{3,2,1,0:T(8,128)(2,1)S(1)}, bf16[4,16,8,128]{3,2,1,0:T(8,128)(2,1)S(1)}, u32[]{:S(2)}, u32[]{:S(2)}) collective-permute-start(bf16[4,16,8,128]{3,2,1,0:T(8,128)(2,1)S(1)} %pad_maximum_fusion.refs_0_), channel_id=1, source_target_pairs={{0,3},{1,2},{2,1},{3,0},{4,7},{5,6},{6,5},{7,4},{8,11},{9,10},{10,... | collective-permute-start | bytes 393224 | tf_op jit(solution)/shard_map/ppermute | solution.py:171
  48.1 1.2 %collective-permute-start.14 = (bf16[4,16,8,128]{3,2,1,0:T(8,128)(2,1)S(1)}, bf16[4,16,8,128]{3,2,1,0:T(8,128)(2,1)S(1)}, u32[]{:S(2)}, u32[]{:S(2)}) collective-permute-start(bf16[4,16,8,128]{3,2,1,0:T(8,128)(2,1)S(1)} %pad_maximum_fusion.refs_0_), channel_id=1, source_target_pairs={{0,2},{1,3},{2,0},{3,1},{4,6},{5,7},{6,4},{7,5},{8,10},{9,11},{10,... | collective-permute-start | bytes 393224 | tf_op jit(solution)/shard_map/ppermute | solution.py:171
  49.3 0.8 %collective-permute-start.13 = (bf16[4,16,8,128]{3,2,1,0:T(8,128)(2,1)S(1)}, bf16[4,16,8,128]{3,2,1,0:T(8,128)(2,1)S(1)}, u32[]{:S(2)}, u32[]{:S(2)}) collective-permute-start(bf16[4,16,8,128]{3,2,1,0:T(8,128)(2,1)S(1)} %pad_maximum_fusion.refs_0_), channel_id=1, source_target_pairs={{0,1},{1,0},{2,3},{3,2},{4,5},{5,4},{6,7},{7,6},{8,9},{9,8},{10,11... | collective-permute-start | bytes 393224 | tf_op jit(solution)/shard_map/ppermute | solution.py:171
  50.1 2.8 %backward.2.refs_3_ = f32[1024,128]{1,0:T(8,128)} custom-call(s32[3]{0:T(128)} %pad_add_fusion.at_ref, bf16[128,2048]{1,0:T(8,128)(2,1)} %constant_dynamic-slice_fusion.5.interp_ref, f32[8,2048]{1,0:T(8,128)} %get-tuple-element.26.cos_ref, f32[8,2048]{1,0:T(8,128)} %get-tuple-element.25.sin_ref, bf16[4,16,8,128]{3,2,1,0:T(8,128)(2,1)} %copy-done.1), custom_call_target="tpu_custom_call" | custom-call | tf_op jit(solution)/shard_map/backward/pallas_call | solution.py:154
  53.5 1.2 %collective-permute-done.14.refs_1_ = bf16[4,16,8,128]{3,2,1,0:T(8,128)(2,1)S(1)} collective-permute-done((bf16[4,16,8,128]{3,2,1,0:T(8,128)(2,1)S(1)}, bf16[4,16,8,128]{3,2,1,0:T(8,128)(2,1)S(1)}, u32[]{:S(2)}, u32[]{:S(2)}) %collective-permute-start.14) | collective-permute-done | bytes 131104 | tf_op jit(solution)/shard_map/ppermute | solution.py:171
  56.0 4.7 %backward.3 = bf16[1024,128]{1,0:T(8,128)(2,1)} custom-call(s32[3]{0:T(128)} %pad_add_fusion.at_ref, bf16[128,2048]{1,0:T(8,128)(2,1)} %constant_dynamic-slice_fusion.5.interp_ref, f32[8,2048]{1,0:T(8,128)} %get-tuple-element.26.cos_ref, f32[8,2048]{1,0:T(8,128)} %get-tuple-element.25.sin_ref, bf16[4,16,8,128]{3,2,1,0:T(8,128)(2,1)} %copy-done.5, ...), custom_call_target="tpu_custom_call" | custom-call | tf_op jit(solution)/shard_map/backward/pallas_call | solution.py:154
  (52 shorter events, 6.2 us)
Async XLA Ops:
  0.0 1.9 %copy-start = (bf16[512,2048]{1,0:T(8,128)(2,1)S(1)}, bf16[512,2048]{1,0:T(8,128)(2,1)}, u32[]{:S(2)}) copy-start(bf16[512,2048]{1,0:T(8,128)(2,1)} %param.7) | copy-start | bytes 6291460
  0.0 13.3 %copy-start.14 = (s32[128,27]{0,1:T(8,128)S(1)}, s32[128,27]{0,1:T(8,128)}, u32[]{:S(2)}) copy-start(s32[128,27]{0,1:T(8,128)} %param.11) | copy-start | bytes 41476
  0.0 13.3 %copy-start.13 = (s32[128,27]{0,1:T(8,128)S(1)}, s32[128,27]{0,1:T(8,128)}, u32[]{:S(2)}) copy-start(s32[128,27]{0,1:T(8,128)} %param.10) | copy-start | bytes 41476
  8.8 7.2 %collective-permute-start = (bf16[4,16,8,128]{3,2,1,0:T(8,128)(2,1)}, bf16[4,16,8,128]{3,2,1,0:T(8,128)(2,1)S(1)}, u32[]{:S(2)}, u32[]{:S(2)}) collective-permute-start(bf16[4,16,8,128]{3,2,1,0:T(8,128)(2,1)} %get-tuple-element.14), channel_id=1, source_target_pairs={{0,1},{1,0},{2,3},{3,2},{4,5},{5,4},{6,7},{7,6},{8,9},{9,8},{10,11... | collective-permute-start | bytes 393224 | tf_op jit(solution)/shard_map/ppermute | solution.py:171
  11.8 8.0 %collective-permute-start.1 = (bf16[4,16,8,128]{3,2,1,0:T(8,128)(2,1)}, bf16[4,16,8,128]{3,2,1,0:T(8,128)(2,1)S(1)}, u32[]{:S(2)}, u32[]{:S(2)}) collective-permute-start(bf16[4,16,8,128]{3,2,1,0:T(8,128)(2,1)} %get-tuple-element.15), channel_id=1, source_target_pairs={{0,2},{1,3},{2,0},{3,1},{4,6},{5,7},{6,4},{7,5},{8,10},{9,11},{10,... | collective-permute-start | bytes 393224 | tf_op jit(solution)/shard_map/ppermute | solution.py:171
  13.3 6.5 %collective-permute-start.2 = (bf16[4,16,8,128]{3,2,1,0:T(8,128)(2,1)}, bf16[4,16,8,128]{3,2,1,0:T(8,128)(2,1)S(1)}, u32[]{:S(2)}, u32[]{:S(2)}) collective-permute-start(bf16[4,16,8,128]{3,2,1,0:T(8,128)(2,1)} %get-tuple-element.16), channel_id=1, source_target_pairs={{0,3},{1,2},{2,1},{3,0},{4,7},{5,6},{6,5},{7,4},{8,11},{9,10},{10,... | collective-permute-start | bytes 393224 | tf_op jit(solution)/shard_map/ppermute | solution.py:171
  20.8 10.6 %copy-start.2 = (bf16[1,16,8,128]{3,2,1,0:T(8,128)(2,1)}, bf16[1,16,8,128]{3,2,1,0:T(8,128)(2,1)S(1)}, u32[]{:S(2)}) copy-start(bf16[1,16,8,128]{3,2,1,0:T(8,128)(2,1)S(1)} %get-tuple-element.24) | copy-start | bytes 98308
  20.8 5.8 %collective-permute-start.8 = (bf16[1,16,8,128]{3,2,1,0:T(8,128)(2,1)S(1)}, bf16[1,16,8,128]{3,2,1,0:T(8,128)(2,1)S(1)}, u32[]{:S(2)}, u32[]{:S(2)}) collective-permute-start(bf16[1,16,8,128]{3,2,1,0:T(8,128)(2,1)S(1)} %get-tuple-element.21), channel_id=1, source_target_pairs={{0,24},{4,28},{8,16},{12,20},{16,8},{20,12},{24,0},{28,4},{1,25},{... | collective-permute-start | bytes 98312 | tf_op jit(solution)/shard_map/ppermute | solution.py:171
  24.5 4.8 %collective-permute-start.6 = (bf16[1,16,8,128]{3,2,1,0:T(8,128)(2,1)S(1)}, bf16[1,16,8,128]{3,2,1,0:T(8,128)(2,1)S(1)}, u32[]{:S(2)}, u32[]{:S(2)}) collective-permute-start(bf16[1,16,8,128]{3,2,1,0:T(8,128)(2,1)S(1)} %get-tuple-element.22), channel_id=1, source_target_pairs={{0,16},{4,20},{8,24},{12,28},{16,0},{20,4},{24,8},{28,12},{1,17},{... | collective-permute-start | bytes 98312 | tf_op jit(solution)/shard_map/ppermute | solution.py:171
  24.5 4.8 %collective-permute-start.4 = (bf16[1,16,8,128]{3,2,1,0:T(8,128)(2,1)S(1)}, bf16[1,16,8,128]{3,2,1,0:T(8,128)(2,1)S(1)}, u32[]{:S(2)}, u32[]{:S(2)}) collective-permute-start(bf16[1,16,8,128]{3,2,1,0:T(8,128)(2,1)S(1)} %get-tuple-element.23), channel_id=1, source_target_pairs={{0,8},{4,12},{8,0},{12,4},{16,24},{20,28},{24,16},{28,20},{1,9},{5... | collective-permute-start | bytes 98312 | tf_op jit(solution)/shard_map/ppermute | solution.py:171
  26.3 5.1 %collective-permute-start.3 = (bf16[1,16,8,128]{3,2,1,0:T(8,128)(2,1)S(1)}, bf16[1,16,8,128]{3,2,1,0:T(8,128)(2,1)S(1)}, u32[]{:S(2)}, u32[]{:S(2)}) collective-permute-start(bf16[1,16,8,128]{3,2,1,0:T(8,128)(2,1)S(1)} %get-tuple-element.24), channel_id=1, source_target_pairs={{0,4},{4,0},{8,12},{12,8},{16,20},{20,16},{24,28},{28,24},{1,5},{5... | collective-permute-start | bytes 98312 | tf_op jit(solution)/shard_map/ppermute | solution.py:171
  26.6 4.8 %copy-start.6 = (bf16[1,16,8,128]{3,2,1,0:T(8,128)(2,1)}, bf16[1,16,8,128]{3,2,1,0:T(8,128)(2,1)S(1)}, u32[]{:S(2)}) copy-start(bf16[1,16,8,128]{3,2,1,0:T(8,128)(2,1)S(1)} %collective-permute-done.8) | copy-start | bytes 98308
  26.6 4.8 %collective-permute-start.9 = (bf16[1,16,8,128]{3,2,1,0:T(8,128)(2,1)S(1)}, bf16[1,16,8,128]{3,2,1,0:T(8,128)(2,1)S(1)}, u32[]{:S(2)}, u32[]{:S(2)}) collective-permute-start(bf16[1,16,8,128]{3,2,1,0:T(8,128)(2,1)S(1)} %collective-permute-done.8), channel_id=1, source_target_pairs={{0,4},{4,0},{8,12},{12,8},{16,20},{20,16},{24,28},{28,24},{1,5},{5... | collective-permute-start | bytes 98312 | tf_op jit(solution)/shard_map/ppermute | solution.py:171
  29.3 2.2 %copy-start.7 = (bf16[1,16,8,128]{3,2,1,0:T(8,128)(2,1)}, bf16[1,16,8,128]{3,2,1,0:T(8,128)(2,1)S(1)}, u32[]{:S(2)}) copy-start(bf16[1,16,8,128]{3,2,1,0:T(8,128)(2,1)S(1)} %collective-permute-done.6) | copy-start | bytes 98308
  29.3 2.1 %collective-permute-start.7 = (bf16[1,16,8,128]{3,2,1,0:T(8,128)(2,1)S(1)}, bf16[1,16,8,128]{3,2,1,0:T(8,128)(2,1)S(1)}, u32[]{:S(2)}, u32[]{:S(2)}) collective-permute-start(bf16[1,16,8,128]{3,2,1,0:T(8,128)(2,1)S(1)} %collective-permute-done.6), channel_id=1, source_target_pairs={{0,4},{4,0},{8,12},{12,8},{16,20},{20,16},{24,28},{28,24},{1,5},{5... | collective-permute-start | bytes 98312 | tf_op jit(solution)/shard_map/ppermute | solution.py:171
  29.3 2.2 %copy-start.8 = (bf16[1,16,8,128]{3,2,1,0:T(8,128)(2,1)}, bf16[1,16,8,128]{3,2,1,0:T(8,128)(2,1)S(1)}, u32[]{:S(2)}) copy-start(bf16[1,16,8,128]{3,2,1,0:T(8,128)(2,1)S(1)} %collective-permute-done.4) | copy-start | bytes 98308
  29.3 2.1 %collective-permute-start.5 = (bf16[1,16,8,128]{3,2,1,0:T(8,128)(2,1)S(1)}, bf16[1,16,8,128]{3,2,1,0:T(8,128)(2,1)S(1)}, u32[]{:S(2)}, u32[]{:S(2)}) collective-permute-start(bf16[1,16,8,128]{3,2,1,0:T(8,128)(2,1)S(1)} %collective-permute-done.4), channel_id=1, source_target_pairs={{0,4},{4,0},{8,12},{12,8},{16,20},{20,16},{24,28},{28,24},{1,5},{5... | collective-permute-start | bytes 98312 | tf_op jit(solution)/shard_map/ppermute | solution.py:171
  38.1 4.5 %collective-permute-start.10 = (bf16[1,16,8,128]{3,2,1,0:T(8,128)(2,1)}, bf16[1,16,8,128]{3,2,1,0:T(8,128)(2,1)S(1)}, u32[]{:S(2)}, u32[]{:S(2)}) collective-permute-start(bf16[1,16,8,128]{3,2,1,0:T(8,128)(2,1)} %bitcast.31), channel_id=1, source_target_pairs={{0,8},{4,12},{8,0},{12,4},{16,24},{20,28},{24,16},{28,20},{1,9},{5... | collective-permute-start | bytes 98312 | tf_op jit(solution)/shard_map/ppermute | solution.py:171
  38.1 5.2 %collective-permute-start.11 = (bf16[1,16,8,128]{3,2,1,0:T(8,128)(2,1)}, bf16[1,16,8,128]{3,2,1,0:T(8,128)(2,1)S(1)}, u32[]{:S(2)}, u32[]{:S(2)}) collective-permute-start(bf16[1,16,8,128]{3,2,1,0:T(8,128)(2,1)} %bitcast.30), channel_id=1, source_target_pairs={{0,16},{4,20},{8,24},{12,28},{16,0},{20,4},{24,8},{28,12},{1,17},{... | collective-permute-start | bytes 98312 | tf_op jit(solution)/shard_map/ppermute | solution.py:171
  39.8 5.9 %collective-permute-start.12 = (bf16[1,16,8,128]{3,2,1,0:T(8,128)(2,1)}, bf16[1,16,8,128]{3,2,1,0:T(8,128)(2,1)S(1)}, u32[]{:S(2)}, u32[]{:S(2)}) collective-permute-start(bf16[1,16,8,128]{3,2,1,0:T(8,128)(2,1)} %bitcast.29), channel_id=1, source_target_pairs={{0,24},{4,28},{8,16},{12,20},{16,8},{20,12},{24,0},{28,4},{1,25},{... | collective-permute-start | bytes 98312 | tf_op jit(solution)/shard_map/ppermute | solution.py:171
  46.5 3.6 %copy-start.1 = (bf16[4,16,8,128]{3,2,1,0:T(8,128)(2,1)}, bf16[4,16,8,128]{3,2,1,0:T(8,128)(2,1)S(1)}, u32[]{:S(2)}) copy-start(bf16[4,16,8,128]{3,2,1,0:T(8,128)(2,1)S(1)} %pad_maximum_fusion.refs_0_) | copy-start | bytes 393220
  46.5 7.0 %collective-permute-start.15 = (bf16[4,16,8,128]{3,2,1,0:T(8,128)(2,1)S(1)}, bf16[4,16,8,128]{3,2,1,0:T(8,128)(2,1)S(1)}, u32[]{:S(2)}, u32[]{:S(2)}) collective-permute-start(bf16[4,16,8,128]{3,2,1,0:T(8,128)(2,1)S(1)} %pad_maximum_fusion.refs_0_), channel_id=1, source_target_pairs={{0,3},{1,2},{2,1},{3,0},{4,7},{5,6},{6,5},{7,4},{8,11},{9,10},{10,... | collective-permute-start | bytes 393224 | tf_op jit(solution)/shard_map/ppermute | solution.py:171
  48.1 6.6 %collective-permute-start.14 = (bf16[4,16,8,128]{3,2,1,0:T(8,128)(2,1)S(1)}, bf16[4,16,8,128]{3,2,1,0:T(8,128)(2,1)S(1)}, u32[]{:S(2)}, u32[]{:S(2)}) collective-permute-start(bf16[4,16,8,128]{3,2,1,0:T(8,128)(2,1)S(1)} %pad_maximum_fusion.refs_0_), channel_id=1, source_target_pairs={{0,2},{1,3},{2,0},{3,1},{4,6},{5,7},{6,4},{7,5},{8,10},{9,11},{10,... | collective-permute-start | bytes 393224 | tf_op jit(solution)/shard_map/ppermute | solution.py:171
  49.3 5.5 %collective-permute-start.13 = (bf16[4,16,8,128]{3,2,1,0:T(8,128)(2,1)S(1)}, bf16[4,16,8,128]{3,2,1,0:T(8,128)(2,1)S(1)}, u32[]{:S(2)}, u32[]{:S(2)}) collective-permute-start(bf16[4,16,8,128]{3,2,1,0:T(8,128)(2,1)S(1)} %pad_maximum_fusion.refs_0_), channel_id=1, source_target_pairs={{0,1},{1,0},{2,3},{3,2},{4,5},{5,4},{6,7},{7,6},{8,9},{9,8},{10,11... | collective-permute-start | bytes 393224 | tf_op jit(solution)/shard_map/ppermute | solution.py:171
  (7 other events, 5.1 us)

commit v2 on v1

v2 whole, which is shorter than its diff:
```python
import functools

import jax
import jax.numpy as jnp
from jax import lax
from jax.experimental import pallas as pl
from jax.experimental.pallas import tpu as pltpu
from jax.sharding import PartitionSpec as P


CH = 8
LANES = 128
anterp_scale = 0.125
HALF_PI = 1.5707963267948966
HALF_PI_HIGH = 1.57080078125
HALF_PI_LOW = HALF_PI - HALF_PI_HIGH

VMEM = pl.BlockSpec(memory_space=pltpu.VMEM)
SMEM = pl.BlockSpec(memory_space=pltpu.SMEM)
FAR = pl.BlockSpec(memory_space=pltpu.HBM)
GRANT = pltpu.CompilerParams(vmem_limit_bytes=12 << 20)


def half_sign(rows, first):
    row = lax.broadcasted_iota(jnp.int32, (rows, LANES), 0)
    return jnp.where(row < rows // 2, first, -first).astype(jnp.float32)


def sine_cosine(angle):
    turns = jnp.round(angle * (1.0 / HALF_PI))
    x = (angle - turns * HALF_PI_HIGH) - turns * HALF_PI_LOW
    y = x * x
    s = x * (1.0 + y * (-1.6666654611e-1 + y * (8.3321608736e-3 + y * -1.9515295891e-4)))
    c = 1.0 + y * (
        -0.5 + y * (4.166664568298827e-2 + y * (-1.388731625493765e-3 + y * 2.443315711809948e-5))
    )
    quadrant = turns.astype(jnp.int32)
    odd = (quadrant & 1) == 1
    sine = jnp.where(odd, c, s)
    cosine = jnp.where(odd, s, c)
    sine = jnp.where((quadrant & 2) == 2, -sine, sine)
    cosine = jnp.where(((quadrant + 1) & 2) == 2, -cosine, cosine)
    return sine, cosine


def add_octants(start, x_ref, interp_ref, cos_ref, sin_ref, out_ref, field):
    chunks, par_cnt, cols, _ = out_ref.shape
    width = chunks * LANES
    sign = half_sign(cols, -1.0)
    field[...] = jnp.dot(
        x_ref[...], interp_ref[:, pl.ds(start, width)], preferred_element_type=jnp.float32
    )
    for chunk in range(chunks):
        lanes = pl.ds(pl.multiple_of(start + chunk * LANES, LANES), LANES)
        cosine = jnp.broadcast_to(cos_ref[:, lanes][:, None, :], (CH, cols, LANES))
        sine = jnp.broadcast_to(sin_ref[:, lanes][:, None, :], (CH, cols, LANES))

        def one(p, carry, chunk=chunk, cosine=cosine, sine=sine):
            rows = pl.ds(pl.multiple_of(p * CH * cols, CH * cols), CH * cols)
            part = field[rows, chunk * LANES : (chunk + 1) * LANES].reshape(CH, cols, LANES)
            same = jnp.sum(part * cosine, axis=0)
            cross = jnp.sum(part * sine, axis=0)
            total = same + sign * pltpu.roll(cross, cols // 2, 0)
            out_ref[chunk, p] = total.astype(out_ref.dtype)
            return carry

        lax.fori_loop(0, par_cnt, one, 0, unroll=4)


def first_kernel(mask, at_ref, x_any, interp_any, angle_any, *refs):
    out_ref, x_ref, interp_ref, cos_ref, sin_ref, field, angle_ref, sems = refs
    load_angle = pltpu.make_async_copy(angle_any, angle_ref, sems.at[2])
    load_angle.start()
    width = out_ref.shape[0] * LANES
    rows = interp_ref.shape[0]
    dir_at = at_ref[0]
    start = pl.multiple_of((dir_at ^ mask) * width, width)
    mine = pl.ds(pl.multiple_of(dir_at * rows, rows), rows)
    load_x = pltpu.make_async_copy(x_any, x_ref, sems.at[0])
    load_interp = pltpu.make_async_copy(interp_any.at[mine], interp_ref, sems.at[1])
    load_x.start()
    load_interp.start()
    load_angle.wait()
    sine, cosine = sine_cosine(angle_ref[...])
    cos_ref[...] = cosine
    sin_ref[...] = sine
    load_x.wait()
    load_interp.wait()
    add_octants(start, x_ref, interp_ref, cos_ref, sin_ref, out_ref, field)


def first_forward(mask, chunks, cols, at, x, interp, angle):
    rows, kq = x.shape
    npd = interp.shape[1]
    par_cnt = rows // (CH * cols)
    return pl.pallas_call(
        functools.partial(first_kernel, mask),
        out_shape=[
            jax.ShapeDtypeStruct((chunks, par_cnt, cols, LANES), jnp.bfloat16),
            jax.ShapeDtypeStruct(x.shape, x.dtype),
            jax.ShapeDtypeStruct((kq, npd), interp.dtype),
            jax.ShapeDtypeStruct(angle.shape, jnp.float32),
            jax.ShapeDtypeStruct(angle.shape, jnp.float32),
        ],
        in_specs=[SMEM, FAR, FAR, FAR],
        out_specs=[VMEM] * 5,
        scratch_shapes=[
            pltpu.VMEM((rows, chunks * LANES), jnp.float32),
            pltpu.VMEM(angle.shape, jnp.float32),
            pltpu.SemaphoreType.DMA((3,)),
        ],
        compiler_params=GRANT,
        name="first_forward",
    )(at, x, interp, angle)


def forward_kernel(mask, at_ref, x_ref, interp_ref, cos_ref, sin_ref, out_ref, field):
    width = out_ref.shape[0] * LANES
    start = pl.multiple_of((at_ref[0] ^ mask) * width, width)
    add_octants(start, x_ref, interp_ref, cos_ref, sin_ref, out_ref, field)


def forward(mask, chunks, cols, at, x, interp, cosine, sine):
    rows = x.shape[0]
    shape = (chunks, rows // (CH * cols), cols, LANES)
    return pl.pallas_call(
        functools.partial(forward_kernel, mask),
        out_shape=jax.ShapeDtypeStruct(shape, jnp.bfloat16 if mask else jnp.float32),
        in_specs=[SMEM, VMEM, VMEM, VMEM, VMEM],
        out_specs=VMEM,
        scratch_shapes=[pltpu.VMEM((rows, chunks * LANES), jnp.float32)],
        compiler_params=GRANT,
        name="forward",
    )(at, x, interp, cosine, sine)


def last_forward_kernel(wide, at_ref, x_ref, interp_ref, cos_ref, sin_ref, *refs):
    tables_any, which_any, offset_any, out_ref, rows_ref, which_ref, offset_ref, field, sems = refs
    width = out_ref.shape[0] * LANES
    lanes = pl.ds(pl.multiple_of(at_ref[1] * wide * LANES, LANES), wide * LANES)
    loads = [
        pltpu.make_async_copy(tables_any.at[:, :, lanes], rows_ref, sems.at[0]),
        pltpu.make_async_copy(which_any, which_ref, sems.at[1]),
        pltpu.make_async_copy(offset_any, offset_ref, sems.at[2]),
    ]
    for load in loads:
        load.start()
    start = pl.multiple_of(at_ref[0] * width, width)
    add_octants(start, x_ref, interp_ref, cos_ref, sin_ref, out_ref, field)
    for load in loads:
        load.wait()


def last_forward(chunks, wide, cols, at, x, interp, cosine, sine, tables, which, offset):
    rows = x.shape[0]
    return pl.pallas_call(
        functools.partial(last_forward_kernel, wide),
        out_shape=[
            jax.ShapeDtypeStruct((chunks, rows // (CH * cols), cols, LANES), jnp.float32),
            jax.ShapeDtypeStruct(tables.shape[:2] + (wide * LANES,), tables.dtype),
            pltpu.SMEM(which.shape, which.dtype),
            pltpu.SMEM(offset.shape, offset.dtype),
        ],
        in_specs=[SMEM, VMEM, VMEM, VMEM, VMEM, FAR, FAR, FAR],
        out_specs=[VMEM, VMEM, SMEM, SMEM],
        scratch_shapes=[
            pltpu.VMEM((rows, chunks * LANES), jnp.float32),
            pltpu.SemaphoreType.DMA((3,)),
        ],
        compiler_params=GRANT,
        name="last_forward",
    )(at, x, interp, cosine, sine, tables, which, offset)


def gather_kernel(zc, rest, at_ref, *refs):
    pieces, source = refs[:-1], refs[-1]
    each = len(pieces) // zc
    cols = pieces[0].shape[1]
    own = pieces[0].shape[0] if each > 1 else pieces[0].shape[0] // rest
    zi, ci = at_ref[1], at_ref[2]
    for s in range(zc):
        for t in range(each):
            box = (zi ^ s) * rest + ((ci ^ t) if each > 1 else 0)
            piece = pieces[s * each + t]
            here = piece.shape[0] * cols
            rows = pl.ds(pl.multiple_of(box * own * cols, cols), here)
            source[rows, :] = piece[...].astype(jnp.float32).reshape(here, LANES)


def add_partners(targets, rest, at_ref, which_ref, offset_ref, table_ref, source, outs):
    par_cnt, cols = outs[0].shape[:2]
    total_cnt = source.shape[0] // cols
    slots = which_ref.shape[0] // total_cnt
    zi, ci = at_ref[1], at_ref[2]
    sign = half_sign(cols, -1.0)
    for s, out_ref in zip(targets, outs):
        first = ((zi ^ s) * rest + ci) * par_cnt

        def one(p, carry, first=first, out_ref=out_ref):
            same = jnp.zeros((cols, LANES), jnp.float32)
            cross = jnp.zeros((cols, LANES), jnp.float32)
            for slot in range(slots):
                place = slot * total_cnt + (first + p)
                which = pl.multiple_of(which_ref[place], cols)
                offset = offset_ref[place]
                value = source[pl.ds(which, cols), :]
                same += value * table_ref[offset, 0:1, :]
                cross += value * table_ref[offset, 1:2, :]
            total = same + sign * pltpu.roll(cross, cols // 2, 0)
            out_ref[p] = total.astype(out_ref.dtype)
            return carry

        lax.fori_loop(0, par_cnt, one, 0, unroll=2)


def first_translate_kernel(zc, rest, targets, at_ref, which_ref, offset_ref, table_ref, *refs):
    outs, source = refs[-1 - len(targets) : -1], refs[-1]
    gather_kernel(zc, rest, at_ref, *refs[: -1 - len(targets)], source)
    add_partners(targets, rest, at_ref, which_ref, offset_ref, table_ref, source, outs)


def translate_kernel(rest, targets, at_ref, which_ref, offset_ref, table_ref, source, *outs):
    add_partners(targets, rest, at_ref, which_ref, offset_ref, table_ref, source, outs)


def translate(zc, rest, par_cnt, groups, at, picks, table, pieces):
    cols, lanes = pieces[0].shape[1:]
    out = jax.ShapeDtypeStruct((par_cnt, cols, lanes), jnp.bfloat16)
    found = {}
    source = None
    for targets in groups:
        if source is None:
            result = pl.pallas_call(
                functools.partial(first_translate_kernel, zc, rest, targets),
                out_shape=[out] * len(targets)
                + [jax.ShapeDtypeStruct((zc * rest * par_cnt * cols, lanes), jnp.float32)],
                in_specs=[SMEM, SMEM, SMEM, VMEM] + [VMEM] * len(pieces),
                out_specs=[VMEM] * (len(targets) + 1),
                compiler_params=GRANT,
                name="first_translate",
            )(at, *picks, table, *pieces)
            source = result[-1]
        else:
            call = pl.pallas_call(
                functools.partial(translate_kernel, rest, targets),
                out_shape=[out] * len(targets),
                in_specs=[SMEM, SMEM, SMEM, VMEM, VMEM],
                out_specs=[VMEM] * len(targets),
                compiler_params=GRANT,
                name="translate",
            )
            result = call(at, *picks, table, source)
        for s, value in zip(targets, result):
            found[s] = value
    return [found[s] for s in range(zc)]


def backward_kernel(mask, wide, last, at_ref, interp_ref, cos_ref, sin_ref, quarter, *refs):
    held = refs[0] if len(refs) == 4 else None
    out_ref, left, right = refs[-3:]
    chunks, par_cnt, cols, _ = quarter.shape
    width = chunks * LANES
    sign = half_sign(cols, 1.0)
    for chunk in range(chunks):
        place = (at_ref[1] ^ (chunk // wide)) * wide + chunk % wide
        start = (at_ref[0] ^ mask) * width + place * LANES
        lanes = pl.ds(pl.multiple_of(start, LANES), LANES)
        cosine = jnp.broadcast_to(cos_ref[:, lanes][:, None, :], (CH, cols, LANES))
        sine = jnp.broadcast_to(sin_ref[:, lanes][:, None, :], (CH, cols, LANES)) * sign[None]
        here = slice(chunk * LANES, (chunk + 1) * LANES)
        right[:, here] = interp_ref[:, lanes]

        def one(p, carry, chunk=chunk, cosine=cosine, sine=sine, here=here):
            field = quarter[chunk, p].astype(jnp.float32)
            turned = pltpu.roll(field, cols // 2, 0)
            moved = field[None] * cosine + turned[None] * sine
            rows = pl.ds(pl.multiple_of(p * CH * cols, CH * cols), CH * cols)
            left[rows, here] = moved.reshape(CH * cols, LANES).astype(jnp.bfloat16)
            return carry

        lax.fori_loop(0, par_cnt, one, 0, unroll=4)
    total = lax.dot_general(
        left[...], right[...], (((1,), (1,)), ((), ())), preferred_element_type=jnp.float32
    )
    if held is not None:
        total = total + held[...]
    if last:
        total = anterp_scale * total
    out_ref[...] = total.astype(out_ref.dtype)


def backward(mask, wide, last, at, interp, cosine, sine, quarter, held):
    chunks, par_cnt, cols, _ = quarter.shape
    rows = par_cnt * CH * cols
    kept = [] if held is None else [held]
    return pl.pallas_call(
        functools.partial(backward_kernel, mask, wide, last),
        out_shape=jax.ShapeDtypeStruct(
            (rows, interp.shape[0]), jnp.bfloat16 if last else jnp.float32
        ),
        in_specs=[SMEM, VMEM, VMEM, VMEM, VMEM] + [VMEM] * len(kept),
        out_specs=VMEM,
        scratch_shapes=[
            pltpu.VMEM((rows, chunks * LANES), jnp.bfloat16),
            pltpu.VMEM((interp.shape[0], chunks * LANES), jnp.bfloat16),
        ],
        compiler_params=GRANT,
        name="backward",
    )(at, interp, cosine, sine, quarter, *kept)


def far(value):
    return pltpu.with_memory_space_constraint(value, pltpu.HBM)


def exchange(value, axis, mask):
    size = lax.axis_size(axis)
    return lax.ppermute(value, axis, [(i, i ^ mask) for i in range(size)])


def per_device(child_out, interp, shift_angle, translators, nbr_index, nbr_trans):
    child_cnt, cols, kq = child_out.shape
    par_cnt = child_cnt // CH
    npd = interp.shape[1]
    ndir, nbox = lax.axis_size("dir"), lax.axis_size("box")
    jq = npd // ndir
    zc = 1
    while nbox % (2 * zc) == 0 and zc * 2 < nbox and jq % (2 * zc * LANES) == 0:
        zc *= 2
    rest = nbox // zc
    chunks = jq // LANES
    wide = chunks // zc
    dir_at, box_at = lax.axis_index("dir"), lax.axis_index("box")
    zi, ci = box_at // rest, box_at % rest
    at = jnp.stack([dir_at, zi, ci]).astype(jnp.int32)
    x = child_out.reshape(child_cnt * cols, kq)
    masks = tuple(range(ndir - 1, 0, -1))

    picks = [(nbr_index * cols).T.reshape(-1), nbr_trans.T.reshape(-1)]

    part, x, mine, cosine, sine = first_forward(
        masks[0], chunks, cols, at, far(x), far(interp), far(shift_angle)
    )
    arrived = [exchange(part, "dir", masks[0])]
    for mask in masks[1:]:
        part = forward(mask, chunks, cols, at, x, mine, cosine, sine)
        arrived.append(exchange(part, "dir", mask))
    total, table, *picks = last_forward(
        chunks, wide, cols, at, x, mine, cosine, sine, far(translators), *map(far, picks)
    )
    for part in arrived:
        total = total + part.astype(jnp.float32)
    own = total.astype(jnp.bfloat16).reshape(zc, wide, par_cnt, cols, LANES)

    pieces = []
    for s in range(zc):
        piece = lax.dynamic_index_in_dim(own, zi ^ s, 0, keepdims=False)
        pieces.append(exchange(piece, "box", s * rest) if s else piece)
    if rest == 2:
        pieces = [part for piece in pieces for part in (piece, exchange(piece, "box", 1))]
    else:
        groups = [[z * rest + c for c in range(rest)] for z in range(zc)]
        pieces = [
            lax.all_gather(piece, "box", axis=1, tiled=True, axis_index_groups=groups)
            for piece in pieces
        ]

    order = [(s,) for s in range(zc - 1, -1, -1)]
    back = []
    for w in range(wide):
        rows = table[:, :, w * LANES : (w + 1) * LANES]
        parts = [piece[w] for piece in pieces]
        back.append(translate(zc, rest, par_cnt, order, at, picks, rows, parts))
    quarter = []
    for s in range(zc):
        result = jnp.stack([b[s] for b in back])
        quarter.append(exchange(result, "box", s * rest) if s else result)
    quarter = jnp.concatenate(quarter, 0)

    received = [exchange(quarter, "dir", mask) for mask in range(1, ndir)]
    out = backward(0, wide, ndir == 1, at, mine, cosine, sine, quarter, None)
    for mask, quarter in zip(range(1, ndir), received):
        out = backward(mask, wide, mask == ndir - 1, at, mine, cosine, sine, quarter, out)
    return out.reshape(child_cnt, cols, kq)


def solution(mesh):
    in_specs = (P("box", None, "dir"), P(), P(), P(None, None, "dir"), P(), P())
    out_specs = P("box", None, "dir")

    return jax.shard_map(
        per_device, mesh=mesh, in_specs=in_specs, out_specs=out_specs, check_vma=False
    )
```

time: 61 us -> 51.3 us (0.84)
  local copies, waits for them, and re-layouts: 6.52 us -> 0.03 us
  other arithmetic: 3.55 us -> 0.77 us
    sin x1 -> x0, local copies, waits for them, and re-layouts: 1.87 us -> none  [per_device(): cosine, sine = (jnp.cos(shift_angle), jnp.sin(shift_angle))]
    dynamic_slice x2 -> x0, local copies, waits for them, and re-layouts: 1.85 us -> none  [the longest x1 1 us: per_device(): lax.dynamic_slice_in_dim(translators, zi * wide * LANES, wide * LANES, 2)]
    unnamed x30 -> x2, local copies, waits for them, and re-layouts: 1.82 us -> 0.01 us
    another operation x2 -> x1, other arithmetic: 1.15 us -> 0.08 us  [per_device(): at = jnp.stack([dir_at, zi, ci]).astype(jnp.int32)]
    reshape x1 -> x0, local copies, waits for them, and re-layouts: 0.97 us -> none  [per_device(): rows = table[:, :, w * LANES:(w + 1) * LANES].reshape(-1, LANES)]
    convert_element_type x1, other arithmetic: 1.02 us -> 0.07 us  [per_device(): own = total.astype(jnp.bfloat16).reshape(zc, wide, par_cnt, cols, LANES)]
    concatenate x1, other arithmetic: 0.78 us -> 0.02 us  [per_device(): quarter = jnp.concatenate(quarter, 0)]
    pallas_call x4 -> x12, Pallas kernels: 19 us -> 19.2 us  [the longest x4 6.37 us: backward(): pl.pallas_call(functools.partial(backward_kernel, mask, wide, last), out_...]
  transfers between devices with their start and end apart: 16 -> 16, of which waited for: 10 -> 8; matrix products, arithmetic and copies ran while one was open for 5% -> 1% of each run, Pallas kernels for 5% -> 18%
where the time goes in v2:
time: 51.3 us; the launch traced here: 51.1 us
  Pallas kernels  19.2 us (37%)
  starting transfers between devices  17.6 us (34%)
  waiting for transfers between devices  13.3 us (26%)
  other arithmetic  0.77 us (2%)
    ppermute x16, starting transfers between devices, exchange(): return lax.ppermute(value, axis, [(i, i ^ mask) for i in range(size)])  17.6 us
    ppermute x16, waiting for transfers between devices, exchange(): return lax.ppermute(value, axis, [(i, i ^ mask) for i in range(size)])  13.3 us
    pallas_call x4, Pallas kernels, backward(): pl.pallas_call(functools.partial(backward_kernel, mask, wide, last), out_...  6.37 us
    pallas_call x3, Pallas kernels, translate(): result = call(at, *picks, table, source)  3.91 us
    pallas_call x2, Pallas kernels, forward(): pl.pallas_call(functools.partial(forward_kernel, mask), out_shape=jax.Sha...  2.87 us
    pallas_call x1, Pallas kernels, first_forward(): pl.pallas_call(functools.partial(first_kernel, mask), out_shape=[jax.Shap...  2.62 us
    pallas_call x1, Pallas kernels, last_forward(): pl.pallas_call(functools.partial(last_forward_kernel, wide), out_shape=[j...  2.1 us
    pallas_call x1, Pallas kernels, translate(): pl.pallas_call(functools.partial(first_translate_kernel, zc, rest, target...  1.34 us
  transfers between devices with their start and end apart: 16, of which 8 were waited for; matrix products, arithmetic and copies ran while one was open for 1% of the time, Pallas kernels for 18%

profile of v2, /device:TPU:0, one launch (start us, length us, event | category | flops | bytes accessed | tf_op | source)
XLA Modules:
  0.0 51.1 jit_solution(15879368833272024184)
XLA Ops:
  0.1 2.6 %first_forward.1 = (bf16[4,16,8,128]{3,2,1,0:T(8,128)(2,1)S(1)}, bf16[1024,128]{1,0:T(8,128)(2,1)S(1)}, bf16[128,2048]{1,0:T(8,128)(2,1)S(1)}, f32[8,2048]{1,0:T(8,128)S(1)}, f32[8,2048]{1,0:T(8,128)S(1)}) custom-call(s32[3]{0:T(128)S(1)} %pad_add_fusion.at_ref, bf16[1024,128]{1,0:T(8,128)(2,1)} %bitcast.36, bf16[512,2048]{1,0:T(8,128)(2,1)} %interp_any.1, ...), custom_call_target="tpu_custom_call" | custom-call | tf_op jit(solution)/shard_map/first_forward/pallas_call | solution.py:96
  2.7 1.4 %forward.2 = bf16[4,16,8,128]{3,2,1,0:T(8,128)(2,1)S(1)} custom-call(s32[3]{0:T(128)S(1)} %pad_add_fusion.at_ref, bf16[1024,128]{1,0:T(8,128)(2,1)S(1)} %get-tuple-element.19.x_ref, bf16[128,2048]{1,0:T(8,128)(2,1)S(1)} %get-tuple-element.16.interp_ref, f32[8,2048]{1,0:T(8,128)S(1)} %get-tuple-element.17.cos_ref, f32[8,2048]{1,0:T(8,128)S(1)} %get-tuple-element.18.sin_ref), custom_call_target="tpu_custom_call" | custom-call | tf_op jit(solution)/shard_map/forward/pallas_call | solution.py:126
  4.2 3.1 %collective-permute-start.1 = (bf16[4,16,8,128]{3,2,1,0:T(8,128)(2,1)S(1)}, bf16[4,16,8,128]{3,2,1,0:T(8,128)(2,1)S(1)}, u32[]{:S(2)}, u32[]{:S(2)}) collective-permute-start(bf16[4,16,8,128]{3,2,1,0:T(8,128)(2,1)S(1)} %forward.2), channel_id=1, source_target_pairs={{0,2},{1,3},{2,0},{3,1},{4,6},{5,7},{6,4},{7,5},{8,10},{9,11},{10,... | collective-permute-start | bytes 393224 | tf_op jit(solution)/shard_map/ppermute | solution.py:318
  7.2 1.4 %forward.3 = bf16[4,16,8,128]{3,2,1,0:T(8,128)(2,1)S(1)} custom-call(s32[3]{0:T(128)S(1)} %pad_add_fusion.at_ref, bf16[1024,128]{1,0:T(8,128)(2,1)S(1)} %get-tuple-element.19.x_ref, bf16[128,2048]{1,0:T(8,128)(2,1)S(1)} %get-tuple-element.16.interp_ref, f32[8,2048]{1,0:T(8,128)S(1)} %get-tuple-element.17.cos_ref, f32[8,2048]{1,0:T(8,128)S(1)} %get-tuple-element.18.sin_ref), custom_call_target="tpu_custom_call" | custom-call | tf_op jit(solution)/shard_map/forward/pallas_call | solution.py:126
  8.7 1.5 %collective-permute-start.2 = (bf16[4,16,8,128]{3,2,1,0:T(8,128)(2,1)S(1)}, bf16[4,16,8,128]{3,2,1,0:T(8,128)(2,1)S(1)}, u32[]{:S(2)}, u32[]{:S(2)}) collective-permute-start(bf16[4,16,8,128]{3,2,1,0:T(8,128)(2,1)S(1)} %forward.3), channel_id=1, source_target_pairs={{0,1},{1,0},{2,3},{3,2},{4,5},{5,4},{6,7},{7,6},{8,9},{9,8},{10,11... | collective-permute-start | bytes 393224 | tf_op jit(solution)/shard_map/ppermute | solution.py:318
  10.8 2.1 %last_forward.1 = (f32[4,16,8,128]{3,2,1,0:T(8,128)S(1)}, f32[343,2,128]{2,1,0:T(2,128)S(1)}, s32[3456]{0:T(1024)S(4)}, s32[3456]{0:T(1024)S(4)}) custom-call(s32[3]{0:T(128)S(1)} %pad_add_fusion.at_ref, bf16[1024,128]{1,0:T(8,128)(2,1)S(1)} %get-tuple-element.19.x_ref, bf16[128,2048]{1,0:T(8,128)(2,1)S(1)} %get-tuple-element.16.interp_ref, ...), custom_call_target="tpu_custom_call" | custom-call | tf_op jit(solution)/shard_map/last_forward/pallas_call | solution.py:156
  13.0 2.1 %collective-permute-done.2 = bf16[4,16,8,128]{3,2,1,0:T(8,128)(2,1)S(1)} collective-permute-done((bf16[4,16,8,128]{3,2,1,0:T(8,128)(2,1)S(1)}, bf16[4,16,8,128]{3,2,1,0:T(8,128)(2,1)S(1)}, u32[]{:S(2)}, u32[]{:S(2)}) %collective-permute-start.2) | collective-permute-done | bytes 131104 | tf_op jit(solution)/shard_map/ppermute | solution.py:318
  16.3 1.9 %collective-permute-start.4 = (bf16[1,16,8,128]{3,2,1,0:T(8,128)(2,1)S(1)}, bf16[1,16,8,128]{3,2,1,0:T(8,128)(2,1)S(1)}, u32[]{:S(2)}, u32[]{:S(2)}) collective-permute-start(bf16[1,16,8,128]{3,2,1,0:T(8,128)(2,1)S(1)} %get-tuple-element.29), channel_id=1, source_target_pairs={{0,8},{4,12},{8,0},{12,4},{16,24},{20,28},{24,16},{28,20},{1,9},{5... | collective-permute-start | bytes 98312 | tf_op jit(solution)/shard_map/ppermute | solution.py:318
  18.2 2.6 %collective-permute-start.6 = (bf16[1,16,8,128]{3,2,1,0:T(8,128)(2,1)S(1)}, bf16[1,16,8,128]{3,2,1,0:T(8,128)(2,1)S(1)}, u32[]{:S(2)}, u32[]{:S(2)}) collective-permute-start(bf16[1,16,8,128]{3,2,1,0:T(8,128)(2,1)S(1)} %get-tuple-element.28), channel_id=1, source_target_pairs={{0,16},{4,20},{8,24},{12,28},{16,0},{20,4},{24,8},{28,12},{1,17},{... | collective-permute-start | bytes 98312 | tf_op jit(solution)/shard_map/ppermute | solution.py:318
  21.3 2.0 %collective-permute-done.6 = bf16[1,16,8,128]{3,2,1,0:T(8,128)(2,1)S(1)} collective-permute-done((bf16[1,16,8,128]{3,2,1,0:T(8,128)(2,1)S(1)}, bf16[1,16,8,128]{3,2,1,0:T(8,128)(2,1)S(1)}, u32[]{:S(2)}, u32[]{:S(2)}) %collective-permute-start.6) | collective-permute-done | bytes 32800 | tf_op jit(solution)/shard_map/ppermute | solution.py:318
  23.3 3.2 %collective-permute-done.8 = bf16[1,16,8,128]{3,2,1,0:T(8,128)(2,1)S(1)} collective-permute-done((bf16[1,16,8,128]{3,2,1,0:T(8,128)(2,1)S(1)}, bf16[1,16,8,128]{3,2,1,0:T(8,128)(2,1)S(1)}, u32[]{:S(2)}, u32[]{:S(2)}) %collective-permute-start.8) | collective-permute-done | bytes 32800 | tf_op jit(solution)/shard_map/ppermute | solution.py:318
  27.7 1.3 %first_translate.1 = (bf16[16,8,128]{2,1,0:T(8,128)(2,1)S(1)}, f32[1024,128]{1,0:T(8,128)S(1)}) custom-call(s32[3]{0:T(128)S(1)} %pad_add_fusion.at_ref, s32[3456]{0:T(1024)S(4)} %get-tuple-element.20.which_ref, s32[3456]{0:T(1024)S(4)} %get-tuple-element.21.offset_ref, f32[343,2,128]{2,1,0:T(2,128)S(1)} %get-tuple-element.22.table_ref, ...), custom_call_target="tpu_custom_call" | custom-call | tf_op jit(solution)/shard_map/first_translate/pallas_call | solution.py:233
  29.0 1.3 %translate.4 = bf16[16,8,128]{2,1,0:T(8,128)(2,1)S(1)} custom-call(s32[3]{0:T(128)S(1)} %pad_add_fusion.at_ref, s32[3456]{0:T(1024)S(4)} %get-tuple-element.20.which_ref, s32[3456]{0:T(1024)S(4)} %get-tuple-element.21.offset_ref, f32[343,2,128]{2,1,0:T(2,128)S(1)} %get-tuple-element.22.table_ref, f32[1024,128]{1,0:T(8,128)S(1)} %get-tuple-element.25.source), custom_call_target="tpu_custom_call" | custom-call | tf_op jit(solution)/shard_map/translate/pallas_call | solution.py:252
  30.4 1.3 %translate.5 = bf16[16,8,128]{2,1,0:T(8,128)(2,1)S(1)} custom-call(s32[3]{0:T(128)S(1)} %pad_add_fusion.at_ref, s32[3456]{0:T(1024)S(4)} %get-tuple-element.20.which_ref, s32[3456]{0:T(1024)S(4)} %get-tuple-element.21.offset_ref, f32[343,2,128]{2,1,0:T(2,128)S(1)} %get-tuple-element.22.table_ref, f32[1024,128]{1,0:T(8,128)S(1)} %get-tuple-element.25.source), custom_call_target="tpu_custom_call" | custom-call | tf_op jit(solution)/shard_map/translate/pallas_call | solution.py:252
  32.6 3.5 %collective-permute-start.12 = (bf16[1,16,8,128]{3,2,1,0:T(8,128)(2,1)S(1)}, bf16[1,16,8,128]{3,2,1,0:T(8,128)(2,1)S(1)}, u32[]{:S(2)}, u32[]{:S(2)}) collective-permute-start(bf16[1,16,8,128]{3,2,1,0:T(8,128)(2,1)S(1)} %bitcast.35), channel_id=1, source_target_pairs={{0,24},{4,28},{8,16},{12,20},{16,8},{20,12},{24,0},{28,4},{1,25},{... | collective-permute-start | bytes 98312 | tf_op jit(solution)/shard_map/ppermute | solution.py:318
  36.1 1.3 %translate.3 = bf16[16,8,128]{2,1,0:T(8,128)(2,1)S(1)} custom-call(s32[3]{0:T(128)S(1)} %pad_add_fusion.at_ref, s32[3456]{0:T(1024)S(4)} %get-tuple-element.20.which_ref, s32[3456]{0:T(1024)S(4)} %get-tuple-element.21.offset_ref, f32[343,2,128]{2,1,0:T(2,128)S(1)} %get-tuple-element.22.table_ref, f32[1024,128]{1,0:T(8,128)S(1)} %get-tuple-element.25.source), custom_call_target="tpu_custom_call" | custom-call | tf_op jit(solution)/shard_map/translate/pallas_call | solution.py:252
  38.4 1.5 %collective-permute-start.15 = (bf16[4,16,8,128]{3,2,1,0:T(8,128)(2,1)S(1)}, bf16[4,16,8,128]{3,2,1,0:T(8,128)(2,1)S(1)}, u32[]{:S(2)}, u32[]{:S(2)}) collective-permute-start(bf16[4,16,8,128]{3,2,1,0:T(8,128)(2,1)S(1)} %pad_maximum_fusion.quarter), channel_id=1, source_target_pairs={{0,1},{1,0},{2,3},{3,2},{4,5},{5,4},{6,7},{7,6},{8,9},{9,8},{10,11... | collective-permute-start | bytes 393224 | tf_op jit(solution)/shard_map/ppermute | solution.py:318
  39.9 1.5 %collective-permute-start.14 = (bf16[4,16,8,128]{3,2,1,0:T(8,128)(2,1)S(1)}, bf16[4,16,8,128]{3,2,1,0:T(8,128)(2,1)S(1)}, u32[]{:S(2)}, u32[]{:S(2)}) collective-permute-start(bf16[4,16,8,128]{3,2,1,0:T(8,128)(2,1)S(1)} %pad_maximum_fusion.quarter), channel_id=1, source_target_pairs={{0,2},{1,3},{2,0},{3,1},{4,6},{5,7},{6,4},{7,5},{8,10},{9,11},{10,... | collective-permute-start | bytes 393224 | tf_op jit(solution)/shard_map/ppermute | solution.py:318
  41.9 1.4 %backward.4.refs_0_ = f32[1024,128]{1,0:T(8,128)S(1)} custom-call(s32[3]{0:T(128)S(1)} %pad_add_fusion.at_ref, bf16[128,2048]{1,0:T(8,128)(2,1)S(1)} %get-tuple-element.16.interp_ref, f32[8,2048]{1,0:T(8,128)S(1)} %get-tuple-element.17.cos_ref, f32[8,2048]{1,0:T(8,128)S(1)} %get-tuple-element.18.sin_ref, bf16[4,16,8,128]{3,2,1,0:T(8,128)(2,1)S(1)} %pad_maximum_fusion.quarter), custom_call_target="tpu_custom_call" | custom-call | tf_op jit(solution)/shard_map/backward/pallas_call | solution.py:296
  43.4 1.2 %collective-permute-done.15.quarter = bf16[4,16,8,128]{3,2,1,0:T(8,128)(2,1)S(1)} collective-permute-done((bf16[4,16,8,128]{3,2,1,0:T(8,128)(2,1)S(1)}, bf16[4,16,8,128]{3,2,1,0:T(8,128)(2,1)S(1)}, u32[]{:S(2)}, u32[]{:S(2)}) %collective-permute-start.15) | collective-permute-done | bytes 131104 | tf_op jit(solution)/shard_map/ppermute | solution.py:318
  44.6 1.4 %backward.5.refs_0_ = f32[1024,128]{1,0:T(8,128)S(1)} custom-call(s32[3]{0:T(128)S(1)} %pad_add_fusion.at_ref, bf16[128,2048]{1,0:T(8,128)(2,1)S(1)} %get-tuple-element.16.interp_ref, f32[8,2048]{1,0:T(8,128)S(1)} %get-tuple-element.17.cos_ref, f32[8,2048]{1,0:T(8,128)S(1)} %get-tuple-element.18.sin_ref, ...), custom_call_target="tpu_custom_call" | custom-call | tf_op jit(solution)/shard_map/backward/pallas_call | solution.py:296
  46.0 1.6 %collective-permute-done.14.quarter = bf16[4,16,8,128]{3,2,1,0:T(8,128)(2,1)S(1)} collective-permute-done((bf16[4,16,8,128]{3,2,1,0:T(8,128)(2,1)S(1)}, bf16[4,16,8,128]{3,2,1,0:T(8,128)(2,1)S(1)}, u32[]{:S(2)}, u32[]{:S(2)}) %collective-permute-start.14) | collective-permute-done | bytes 131104 | tf_op jit(solution)/shard_map/ppermute | solution.py:318
  47.6 1.4 %backward.6.refs_0_ = f32[1024,128]{1,0:T(8,128)S(1)} custom-call(s32[3]{0:T(128)S(1)} %pad_add_fusion.at_ref, bf16[128,2048]{1,0:T(8,128)(2,1)S(1)} %get-tuple-element.16.interp_ref, f32[8,2048]{1,0:T(8,128)S(1)} %get-tuple-element.17.cos_ref, f32[8,2048]{1,0:T(8,128)S(1)} %get-tuple-element.18.sin_ref, ...), custom_call_target="tpu_custom_call" | custom-call | tf_op jit(solution)/shard_map/backward/pallas_call | solution.py:296
  49.0 2.1 %backward.7 = bf16[1024,128]{1,0:T(8,128)(2,1)} custom-call(s32[3]{0:T(128)S(1)} %pad_add_fusion.at_ref, bf16[128,2048]{1,0:T(8,128)(2,1)S(1)} %get-tuple-element.16.interp_ref, f32[8,2048]{1,0:T(8,128)S(1)} %get-tuple-element.17.cos_ref, f32[8,2048]{1,0:T(8,128)S(1)} %get-tuple-element.18.sin_ref, ...), custom_call_target="tpu_custom_call" | custom-call | tf_op jit(solution)/shard_map/backward/pallas_call | solution.py:296
  (27 shorter events, 6.0 us)
Async XLA Ops:
  0.1 10.2 %copy-start = (s32[128,27]{0,1:T(8,128)S(1)}, s32[128,27]{0,1:T(8,128)}, u32[]{:S(2)}) copy-start(s32[128,27]{0,1:T(8,128)} %param.10) | copy-start | bytes 41476
  4.2 8.8 %collective-permute-start.1 = (bf16[4,16,8,128]{3,2,1,0:T(8,128)(2,1)S(1)}, bf16[4,16,8,128]{3,2,1,0:T(8,128)(2,1)S(1)}, u32[]{:S(2)}, u32[]{:S(2)}) collective-permute-start(bf16[4,16,8,128]{3,2,1,0:T(8,128)(2,1)S(1)} %forward.2), channel_id=1, source_target_pairs={{0,2},{1,3},{2,0},{3,1},{4,6},{5,7},{6,4},{7,5},{8,10},{9,11},{10,... | collective-permute-start | bytes 393224 | tf_op jit(solution)/shard_map/ppermute | solution.py:318
  8.7 6.4 %collective-permute-start.2 = (bf16[4,16,8,128]{3,2,1,0:T(8,128)(2,1)S(1)}, bf16[4,16,8,128]{3,2,1,0:T(8,128)(2,1)S(1)}, u32[]{:S(2)}, u32[]{:S(2)}) collective-permute-start(bf16[4,16,8,128]{3,2,1,0:T(8,128)(2,1)S(1)} %forward.3), channel_id=1, source_target_pairs={{0,1},{1,0},{2,3},{3,2},{4,5},{5,4},{6,7},{7,6},{8,9},{9,8},{10,11... | collective-permute-start | bytes 393224 | tf_op jit(solution)/shard_map/ppermute | solution.py:318
  10.2 6.0 %collective-permute-start = (bf16[4,16,8,128]{3,2,1,0:T(8,128)(2,1)S(1)}, bf16[4,16,8,128]{3,2,1,0:T(8,128)(2,1)S(1)}, u32[]{:S(2)}, u32[]{:S(2)}) collective-permute-start(bf16[4,16,8,128]{3,2,1,0:T(8,128)(2,1)S(1)} %get-tuple-element.24), channel_id=1, source_target_pairs={{0,3},{1,2},{2,1},{3,0},{4,7},{5,6},{6,5},{7,4},{8,11},{9,10},{10,... | collective-permute-start | bytes 393224 | tf_op jit(solution)/shard_map/ppermute | solution.py:318
  16.3 4.5 %collective-permute-start.4 = (bf16[1,16,8,128]{3,2,1,0:T(8,128)(2,1)S(1)}, bf16[1,16,8,128]{3,2,1,0:T(8,128)(2,1)S(1)}, u32[]{:S(2)}, u32[]{:S(2)}) collective-permute-start(bf16[1,16,8,128]{3,2,1,0:T(8,128)(2,1)S(1)} %get-tuple-element.29), channel_id=1, source_target_pairs={{0,8},{4,12},{8,0},{12,4},{16,24},{20,28},{24,16},{28,20},{1,9},{5... | collective-permute-start | bytes 98312 | tf_op jit(solution)/shard_map/ppermute | solution.py:318
  18.2 5.1 %collective-permute-start.6 = (bf16[1,16,8,128]{3,2,1,0:T(8,128)(2,1)S(1)}, bf16[1,16,8,128]{3,2,1,0:T(8,128)(2,1)S(1)}, u32[]{:S(2)}, u32[]{:S(2)}) collective-permute-start(bf16[1,16,8,128]{3,2,1,0:T(8,128)(2,1)S(1)} %get-tuple-element.28), channel_id=1, source_target_pairs={{0,16},{4,20},{8,24},{12,28},{16,0},{20,4},{24,8},{28,12},{1,17},{... | collective-permute-start | bytes 98312 | tf_op jit(solution)/shard_map/ppermute | solution.py:318
  20.8 5.7 %collective-permute-start.8 = (bf16[1,16,8,128]{3,2,1,0:T(8,128)(2,1)S(1)}, bf16[1,16,8,128]{3,2,1,0:T(8,128)(2,1)S(1)}, u32[]{:S(2)}, u32[]{:S(2)}) collective-permute-start(bf16[1,16,8,128]{3,2,1,0:T(8,128)(2,1)S(1)} %get-tuple-element.27), channel_id=1, source_target_pairs={{0,24},{4,28},{8,16},{12,20},{16,8},{20,12},{24,0},{28,4},{1,25},{... | collective-permute-start | bytes 98312 | tf_op jit(solution)/shard_map/ppermute | solution.py:318
  20.8 5.7 %collective-permute-start.3 = (bf16[1,16,8,128]{3,2,1,0:T(8,128)(2,1)S(1)}, bf16[1,16,8,128]{3,2,1,0:T(8,128)(2,1)S(1)}, u32[]{:S(2)}, u32[]{:S(2)}) collective-permute-start(bf16[1,16,8,128]{3,2,1,0:T(8,128)(2,1)S(1)} %get-tuple-element.30), channel_id=1, source_target_pairs={{0,4},{4,0},{8,12},{12,8},{16,20},{20,16},{24,28},{28,24},{1,5},{5... | collective-permute-start | bytes 98312 | tf_op jit(solution)/shard_map/ppermute | solution.py:318
  20.8 5.7 %collective-permute-start.5 = (bf16[1,16,8,128]{3,2,1,0:T(8,128)(2,1)S(1)}, bf16[1,16,8,128]{3,2,1,0:T(8,128)(2,1)S(1)}, u32[]{:S(2)}, u32[]{:S(2)}) collective-permute-start(bf16[1,16,8,128]{3,2,1,0:T(8,128)(2,1)S(1)} %collective-permute-done.4), channel_id=1, source_target_pairs={{0,4},{4,0},{8,12},{12,8},{16,20},{20,16},{24,28},{28,24},{1,5},{5... | collective-permute-start | bytes 98312 | tf_op jit(solution)/shard_map/ppermute | solution.py:318
  23.3 3.3 %collective-permute-start.7 = (bf16[1,16,8,128]{3,2,1,0:T(8,128)(2,1)S(1)}, bf16[1,16,8,128]{3,2,1,0:T(8,128)(2,1)S(1)}, u32[]{:S(2)}, u32[]{:S(2)}) collective-permute-start(bf16[1,16,8,128]{3,2,1,0:T(8,128)(2,1)S(1)} %collective-permute-done.6), channel_id=1, source_target_pairs={{0,4},{4,0},{8,12},{12,8},{16,20},{20,16},{24,28},{28,24},{1,5},{5... | collective-permute-start | bytes 98312 | tf_op jit(solution)/shard_map/ppermute | solution.py:318
  26.5 1.2 %collective-permute-start.9 = (bf16[1,16,8,128]{3,2,1,0:T(8,128)(2,1)S(1)}, bf16[1,16,8,128]{3,2,1,0:T(8,128)(2,1)S(1)}, u32[]{:S(2)}, u32[]{:S(2)}) collective-permute-start(bf16[1,16,8,128]{3,2,1,0:T(8,128)(2,1)S(1)} %collective-permute-done.8), channel_id=1, source_target_pairs={{0,4},{4,0},{8,12},{12,8},{16,20},{20,16},{24,28},{28,24},{1,5},{5... | collective-permute-start | bytes 98312 | tf_op jit(solution)/shard_map/ppermute | solution.py:318
  31.7 5.8 %collective-permute-start.10 = (bf16[1,16,8,128]{3,2,1,0:T(8,128)(2,1)S(1)}, bf16[1,16,8,128]{3,2,1,0:T(8,128)(2,1)S(1)}, u32[]{:S(2)}, u32[]{:S(2)}) collective-permute-start(bf16[1,16,8,128]{3,2,1,0:T(8,128)(2,1)S(1)} %bitcast.34), channel_id=1, source_target_pairs={{0,8},{4,12},{8,0},{12,4},{16,24},{20,28},{24,16},{28,20},{1,9},{5... | collective-permute-start | bytes 98312 | tf_op jit(solution)/shard_map/ppermute | solution.py:318
  31.7 5.7 %collective-permute-start.11 = (bf16[1,16,8,128]{3,2,1,0:T(8,128)(2,1)S(1)}, bf16[1,16,8,128]{3,2,1,0:T(8,128)(2,1)S(1)}, u32[]{:S(2)}, u32[]{:S(2)}) collective-permute-start(bf16[1,16,8,128]{3,2,1,0:T(8,128)(2,1)S(1)} %bitcast.33), channel_id=1, source_target_pairs={{0,16},{4,20},{8,24},{12,28},{16,0},{20,4},{24,8},{28,12},{1,17},{... | collective-permute-start | bytes 98312 | tf_op jit(solution)/shard_map/ppermute | solution.py:318
  32.6 5.7 %collective-permute-start.12 = (bf16[1,16,8,128]{3,2,1,0:T(8,128)(2,1)S(1)}, bf16[1,16,8,128]{3,2,1,0:T(8,128)(2,1)S(1)}, u32[]{:S(2)}, u32[]{:S(2)}) collective-permute-start(bf16[1,16,8,128]{3,2,1,0:T(8,128)(2,1)S(1)} %bitcast.35), channel_id=1, source_target_pairs={{0,24},{4,28},{8,16},{12,20},{16,8},{20,12},{24,0},{28,4},{1,25},{... | collective-permute-start | bytes 98312 | tf_op jit(solution)/shard_map/ppermute | solution.py:318
  38.4 6.2 %collective-permute-start.15 = (bf16[4,16,8,128]{3,2,1,0:T(8,128)(2,1)S(1)}, bf16[4,16,8,128]{3,2,1,0:T(8,128)(2,1)S(1)}, u32[]{:S(2)}, u32[]{:S(2)}) collective-permute-start(bf16[4,16,8,128]{3,2,1,0:T(8,128)(2,1)S(1)} %pad_maximum_fusion.quarter), channel_id=1, source_target_pairs={{0,1},{1,0},{2,3},{3,2},{4,5},{5,4},{6,7},{7,6},{8,9},{9,8},{10,11... | collective-permute-start | bytes 393224 | tf_op jit(solution)/shard_map/ppermute | solution.py:318
  39.9 7.6 %collective-permute-start.14 = (bf16[4,16,8,128]{3,2,1,0:T(8,128)(2,1)S(1)}, bf16[4,16,8,128]{3,2,1,0:T(8,128)(2,1)S(1)}, u32[]{:S(2)}, u32[]{:S(2)}) collective-permute-start(bf16[4,16,8,128]{3,2,1,0:T(8,128)(2,1)S(1)} %pad_maximum_fusion.quarter), channel_id=1, source_target_pairs={{0,2},{1,3},{2,0},{3,1},{4,6},{5,7},{6,4},{7,5},{8,10},{9,11},{10,... | collective-permute-start | bytes 393224 | tf_op jit(solution)/shard_map/ppermute | solution.py:318
  41.4 7.5 %collective-permute-start.13 = (bf16[4,16,8,128]{3,2,1,0:T(8,128)(2,1)S(1)}, bf16[4,16,8,128]{3,2,1,0:T(8,128)(2,1)S(1)}, u32[]{:S(2)}, u32[]{:S(2)}) collective-permute-start(bf16[4,16,8,128]{3,2,1,0:T(8,128)(2,1)S(1)} %pad_maximum_fusion.quarter), channel_id=1, source_target_pairs={{0,3},{1,2},{2,1},{3,0},{4,7},{5,6},{6,5},{7,4},{8,11},{9,10},{10,... | collective-permute-start | bytes 393224 | tf_op jit(solution)/shard_map/ppermute | solution.py:318

commit v3 on v2

v3 whole, which is shorter than its diff:
```python
import functools

import jax
import jax.numpy as jnp
from jax import lax
from jax.experimental import pallas as pl
from jax.experimental.pallas import tpu as pltpu
from jax.sharding import PartitionSpec as P


CH = 8
LANES = 128
anterp_scale = 0.125
HALF_PI = 1.5707963267948966
HALF_PI_HIGH = 1.57080078125
HALF_PI_LOW = HALF_PI - HALF_PI_HIGH

VMEM = pl.BlockSpec(memory_space=pltpu.VMEM)
SMEM = pl.BlockSpec(memory_space=pltpu.SMEM)
FAR = pl.BlockSpec(memory_space=pltpu.HBM)
GRANT = pltpu.CompilerParams(vmem_limit_bytes=12 << 20)


def places(rest):
    box_at = lax.axis_index("box")
    return lax.axis_index("dir"), box_at // rest, box_at % rest


def half_sign(rows, first):
    row = lax.broadcasted_iota(jnp.int32, (rows, LANES), 0)
    return jnp.where(row < rows // 2, first, -first).astype(jnp.float32)


def sine_cosine(angle):
    turns = jnp.round(angle * (1.0 / HALF_PI))
    x = (angle - turns * HALF_PI_HIGH) - turns * HALF_PI_LOW
    y = x * x
    s = x * (1.0 + y * (-1.6666654611e-1 + y * (8.3321608736e-3 + y * -1.9515295891e-4)))
    c = 1.0 + y * (
        -0.5 + y * (4.166664568298827e-2 + y * (-1.388731625493765e-3 + y * 2.443315711809948e-5))
    )
    quadrant = turns.astype(jnp.int32)
    odd = (quadrant & 1) == 1
    sine = jnp.where(odd, c, s)
    cosine = jnp.where(odd, s, c)
    sine = jnp.where((quadrant & 2) == 2, -sine, sine)
    cosine = jnp.where(((quadrant + 1) & 2) == 2, -cosine, cosine)
    return sine, cosine


def add_octants(start, x_ref, interp_ref, cos_ref, sin_ref, out_ref):
    chunks, par_cnt, cols, _ = out_ref.shape
    span = min(chunks, 2)
    sign = half_sign(cols, -1.0)
    for base in range(0, chunks, span):
        at = pl.multiple_of(start + base * LANES, LANES)
        field = jnp.dot(
            x_ref[...], interp_ref[:, pl.ds(at, span * LANES)], preferred_element_type=jnp.float32
        )
        for chunk in range(span):
            lanes = pl.ds(pl.multiple_of(at + chunk * LANES, LANES), LANES)
            cosine = [jnp.broadcast_to(cos_ref[o : o + 1, lanes], (cols, LANES)) for o in range(CH)]
            sine = [jnp.broadcast_to(sin_ref[o : o + 1, lanes], (cols, LANES)) for o in range(CH)]
            for p in range(par_cnt):
                same = cross = None
                for o in range(CH):
                    row = (p * CH + o) * cols
                    part = field[row : row + cols, chunk * LANES : (chunk + 1) * LANES]
                    same = part * cosine[o] if o == 0 else same + part * cosine[o]
                    cross = part * sine[o] if o == 0 else cross + part * sine[o]
                total = same + sign * pltpu.roll(cross, cols // 2, 0)
                out_ref[base + chunk, p] = total.astype(out_ref.dtype)


def first_kernel(mask, x_any, interp_any, angle_any, *refs):
    out_ref, x_ref, interp_ref, cos_ref, sin_ref, angle_ref, sems = refs
    load_angle = pltpu.make_async_copy(angle_any, angle_ref, sems.at[2])
    load_angle.start()
    width = out_ref.shape[0] * LANES
    rows = interp_ref.shape[0]
    dir_at = lax.axis_index("dir")
    start = pl.multiple_of((dir_at ^ mask) * width, width)
    mine = pl.ds(pl.multiple_of(dir_at * rows, rows), rows)
    load_x = pltpu.make_async_copy(x_any, x_ref, sems.at[0])
    load_interp = pltpu.make_async_copy(interp_any.at[mine], interp_ref, sems.at[1])
    load_x.start()
    load_interp.start()
    load_angle.wait()
    sine, cosine = sine_cosine(angle_ref[...])
    cos_ref[...] = cosine
    sin_ref[...] = sine
    load_x.wait()
    load_interp.wait()
    add_octants(start, x_ref, interp_ref, cos_ref, sin_ref, out_ref)


def first_forward(mask, chunks, cols, x, interp, angle):
    rows, kq = x.shape
    npd = interp.shape[1]
    par_cnt = rows // (CH * cols)
    return pl.pallas_call(
        functools.partial(first_kernel, mask),
        out_shape=[
            jax.ShapeDtypeStruct((chunks, par_cnt, cols, LANES), jnp.bfloat16),
            jax.ShapeDtypeStruct(x.shape, x.dtype),
            jax.ShapeDtypeStruct((kq, npd), interp.dtype),
            jax.ShapeDtypeStruct(angle.shape, jnp.float32),
            jax.ShapeDtypeStruct(angle.shape, jnp.float32),
        ],
        in_specs=[FAR, FAR, FAR],
        out_specs=[VMEM] * 5,
        scratch_shapes=[
            pltpu.VMEM(angle.shape, jnp.float32),
            pltpu.SemaphoreType.DMA((3,)),
        ],
        compiler_params=GRANT,
        name="first_forward",
    )(x, interp, angle)


def forward_kernel(mask, x_ref, interp_ref, cos_ref, sin_ref, out_ref):
    width = out_ref.shape[0] * LANES
    start = pl.multiple_of((lax.axis_index("dir") ^ mask) * width, width)
    add_octants(start, x_ref, interp_ref, cos_ref, sin_ref, out_ref)


def forward(mask, chunks, cols, x, interp, cosine, sine):
    rows = x.shape[0]
    shape = (chunks, rows // (CH * cols), cols, LANES)
    return pl.pallas_call(
        functools.partial(forward_kernel, mask),
        out_shape=jax.ShapeDtypeStruct(shape, jnp.bfloat16 if mask else jnp.float32),
        in_specs=[VMEM, VMEM, VMEM, VMEM],
        out_specs=VMEM,
        compiler_params=GRANT,
        name="forward",
    )(x, interp, cosine, sine)


def one_hot(column, count):
    lane = lax.broadcasted_iota(jnp.int32, (column.shape[0], count), 1)
    return jnp.where(lane == column, 1.0, 0.0).astype(jnp.bfloat16)


def prepare_kernel(zc, rest, wide, words_ref, tables_any, *refs):
    pick_ref, factor_ref, table, sems = refs
    total_cnt, slots = words_ref.shape
    par_cnt = total_cnt // (zc * rest)
    offsets, depth = tables_any.shape[0], table.shape[1]
    _, zi, ci = places(rest)
    loads = []
    table[:, offsets // 8 * 8 :, :] = jnp.zeros((2, depth - offsets // 8 * 8, wide * LANES), jnp.float32)
    lanes = pl.ds(pl.multiple_of(zi * wide * LANES, LANES), wide * LANES)
    for part in range(2):
        source = tables_any.at[:, part, lanes]
        load = pltpu.make_async_copy(source, table.at[part, pl.ds(0, offsets)], sems.at[part])
        load.start()
        loads.append(load)
    chosen = []
    for s in range(zc):
        first = pl.multiple_of(((zi ^ s) * rest + ci) * par_cnt, par_cnt)
        words = words_ref[pl.ds(first, par_cnt), :]
        which, offset = words & 0xFFFF, lax.shift_right_logical(words, 16)
        rows = []
        for slot in range(slots):
            here = slice(slot * par_cnt, (slot + 1) * par_cnt)
            pick_ref[s, here, :] = one_hot(which[:, slot : slot + 1], total_cnt)
            rows.append(one_hot(offset[:, slot : slot + 1], depth))
        chosen.append(jnp.concatenate(rows, 0))
    for load in loads:
        load.wait()
    for w in range(wide):
        here = slice(w * LANES, (w + 1) * LANES)
        both = jnp.concatenate([table[0, :, here], table[1, :, here]], 1).astype(jnp.bfloat16)
        for s in range(zc):
            factor = jnp.dot(chosen[s], both, preferred_element_type=jnp.float32)
            factor_ref[w, s, 0] = factor[:, :LANES]
            factor_ref[w, s, 1] = factor[:, LANES:]


def prepare(zc, rest, wide, words, tables):
    total_cnt, slots = words.shape
    rows = slots * total_cnt // (zc * rest)
    depth = -(-tables.shape[0] // LANES) * LANES
    return pl.pallas_call(
        functools.partial(prepare_kernel, zc, rest, wide),
        out_shape=[
            jax.ShapeDtypeStruct((zc, rows, total_cnt), jnp.bfloat16),
            jax.ShapeDtypeStruct((wide, zc, 2, rows, LANES), jnp.float32),
        ],
        in_specs=[VMEM, FAR],
        out_specs=[VMEM, VMEM],
        scratch_shapes=[
            pltpu.VMEM((2, depth, wide * LANES), jnp.float32),
            pltpu.SemaphoreType.DMA((2,)),
        ],
        compiler_params=GRANT,
        name="prepare",
    )(words, tables)


def swap_rows(outer, inner):
    rows = outer * inner
    row = lax.broadcasted_iota(jnp.int32, (rows, rows), 0)
    source = lax.broadcasted_iota(jnp.int32, (rows, rows), 1)
    wanted = row % outer * inner + row // outer
    return jnp.where(source == wanted, 1.0, 0.0).astype(jnp.bfloat16)


def add_partners(targets, w, par_cnt, pick_ref, factor_ref, source, outs):
    cols = source.shape[0]
    half = cols // 2
    slots = pick_ref.shape[1] // par_cnt
    swap = swap_rows(cols, par_cnt)
    for s, out_ref in zip(targets, outs):
        left, right = [], []
        for col in range(half):
            pair = jnp.concatenate([source[col], source[col + half]], 1)
            found = jnp.dot(pick_ref[s], pair, preferred_element_type=jnp.float32)
            for slot in range(slots):
                here = slice(slot * par_cnt, (slot + 1) * par_cnt)
                a, b = found[here, :LANES], found[here, LANES:]
                c, d = factor_ref[w, s, 0, here, :], factor_ref[w, s, 1, here, :]
                re, im = a * c - b * d, a * d + b * c
                real = re if slot == 0 else real + re
                imag = im if slot == 0 else imag + im
            left.append(real)
            right.append(imag)
        total = jnp.concatenate(left + right, 0).astype(jnp.bfloat16)
        moved = jnp.dot(swap, total, preferred_element_type=jnp.float32)
        out_ref[...] = moved.astype(jnp.bfloat16).reshape(out_ref.shape)


def first_translate_kernel(zc, rest, targets, w, pick_ref, factor_ref, *refs):
    pieces = refs[: -1 - len(targets)]
    outs, source = refs[-1 - len(targets) : -1], refs[-1]
    par_cnt, cols = outs[0].shape[:2]
    each = len(pieces) // zc
    _, zi, ci = places(rest)
    swap = swap_rows(par_cnt, cols)
    for s in range(zc):
        for t in range(each):
            box = (zi ^ s) * rest + ((ci ^ t) if each > 1 else 0)
            piece = pieces[s * each + t]

            def place(k, carry, box=box, piece=piece):
                rows = piece[pl.ds(k * par_cnt, par_cnt)].reshape(par_cnt * cols, LANES)
                moved = jnp.dot(swap, rows, preferred_element_type=jnp.float32)
                moved = moved.astype(jnp.bfloat16).reshape(cols, par_cnt, LANES)
                first = pl.multiple_of((box + k) * par_cnt, par_cnt)
                source[:, pl.ds(first, par_cnt), :] = moved
                return carry

            count = piece.shape[0] // par_cnt
            if count == 1:
                place(0, 0)
            else:
                lax.fori_loop(0, count, place, 0)
    add_partners(targets, w, par_cnt, pick_ref, factor_ref, source, outs)


def translate_kernel(targets, w, pick_ref, factor_ref, source, *outs):
    par_cnt = outs[0].shape[0]
    add_partners(targets, w, par_cnt, pick_ref, factor_ref, source, outs)


def translate(zc, rest, w, par_cnt, groups, picks, factors, pieces):
    cols, lanes = pieces[0].shape[1:]
    out = jax.ShapeDtypeStruct((par_cnt, cols, lanes), jnp.bfloat16)
    found = {}
    source = None
    for targets in groups:
        if source is None:
            result = pl.pallas_call(
                functools.partial(first_translate_kernel, zc, rest, targets, w),
                out_shape=[out] * len(targets)
                + [jax.ShapeDtypeStruct((cols, zc * rest * par_cnt, lanes), jnp.bfloat16)],
                in_specs=[VMEM, VMEM] + [VMEM] * len(pieces),
                out_specs=[VMEM] * (len(targets) + 1),
                compiler_params=GRANT,
                name="first_translate",
            )(picks, factors, *pieces)
            source = result[-1]
        else:
            call = pl.pallas_call(
                functools.partial(translate_kernel, targets, w),
                out_shape=[out] * len(targets),
                in_specs=[VMEM, VMEM, VMEM],
                out_specs=[VMEM] * len(targets),
                compiler_params=GRANT,
                name="translate",
            )
            result = call(picks, factors, source)
        for s, value in zip(targets, result):
            found[s] = value
    return [found[s] for s in range(zc)]


def backward_kernel(mask, wide, rest, last, interp_ref, cos_ref, sin_ref, quarter, *refs):
    held, out_ref = (refs[0] if len(refs) == 2 else None), refs[-1]
    chunks, par_cnt, cols, _ = quarter.shape
    width = chunks * LANES
    span, block = min(chunks, 2), min(par_cnt, 4)
    sign = half_sign(cols, 1.0)
    dir_at, zi, _ = places(rest)
    lane_sets = []
    for chunk in range(chunks):
        place = (zi ^ (chunk // wide)) * wide + chunk % wide
        start = (dir_at ^ mask) * width + place * LANES
        lane_sets.append(pl.ds(pl.multiple_of(start, LANES), LANES))
    for first in range(0, par_cnt, block):
        here = slice(first * CH * cols, (first + block) * CH * cols)
        total = None if held is None else held[here, :]
        for base in range(0, chunks, span):
            left, right = [], []
            for chunk in range(base, base + span):
                lanes = lane_sets[chunk]
                rows = []
                for p in range(first, first + block):
                    field = quarter[chunk, p].astype(jnp.float32)
                    turned = sign * pltpu.roll(field, cols // 2, 0)
                    for o in range(CH):
                        rows.append(field * cos_ref[o : o + 1, lanes] + turned * sin_ref[o : o + 1, lanes])
                left.append(jnp.concatenate(rows, 0).astype(jnp.bfloat16))
                right.append(interp_ref[:, lanes])
            part = lax.dot_general(
                jnp.concatenate(left, 1),
                jnp.concatenate(right, 1),
                (((1,), (1,)), ((), ())),
                preferred_element_type=jnp.float32,
            )
            total = part if total is None else total + part
        if last:
            total = anterp_scale * total
        out_ref[here, :] = total.astype(out_ref.dtype)


def backward(mask, wide, rest, last, interp, cosine, sine, quarter, held):
    _, par_cnt, cols, _ = quarter.shape
    rows = par_cnt * CH * cols
    kept = [] if held is None else [held]
    return pl.pallas_call(
        functools.partial(backward_kernel, mask, wide, rest, last),
        out_shape=jax.ShapeDtypeStruct(
            (rows, interp.shape[0]), jnp.bfloat16 if last else jnp.float32
        ),
        in_specs=[VMEM, VMEM, VMEM, VMEM] + [VMEM] * len(kept),
        out_specs=VMEM,
        compiler_params=GRANT,
        name="backward",
    )(interp, cosine, sine, quarter, *kept)


def far(value):
    return pltpu.with_memory_space_constraint(value, pltpu.HBM)


def exchange(value, axis, mask):
    size = lax.axis_size(axis)
    return lax.ppermute(value, axis, [(i, i ^ mask) for i in range(size)])


def per_device(child_out, interp, shift_angle, translators, nbr_index, nbr_trans):
    child_cnt, cols, kq = child_out.shape
    par_cnt = child_cnt // CH
    npd = interp.shape[1]
    ndir, nbox = lax.axis_size("dir"), lax.axis_size("box")
    jq = npd // ndir
    zc = 1
    while nbox % (2 * zc) == 0 and zc * 2 < nbox and jq % (2 * zc * LANES) == 0:
        zc *= 2
    rest = nbox // zc
    chunks = jq // LANES
    wide = chunks // zc
    zi = lax.axis_index("box") // rest
    x = child_out.reshape(child_cnt * cols, kq)
    masks = tuple(range(ndir - 1, 0, -1))

    part, x, mine, cosine, sine = first_forward(
        masks[0], chunks, cols, far(x), far(interp), far(shift_angle)
    )
    arrived = [exchange(part, "dir", masks[0])]
    for mask in masks[1:]:
        part = forward(mask, chunks, cols, x, mine, cosine, sine)
        arrived.append(exchange(part, "dir", mask))
    total = forward(0, chunks, cols, x, mine, cosine, sine)
    words = nbr_index | (nbr_trans << 16)
    picks, factors = prepare(zc, rest, wide, words, far(translators))
    for part in arrived:
        total = total + part.astype(jnp.float32)
    own = total.astype(jnp.bfloat16).reshape(zc, wide, par_cnt, cols, LANES)

    pieces = []
    for s in range(zc):
        piece = lax.dynamic_index_in_dim(own, zi ^ s, 0, keepdims=False)
        pieces.append(exchange(piece, "box", s * rest) if s else piece)
    if rest == 2:
        pieces = [part for piece in pieces for part in (piece, exchange(piece, "box", 1))]
    else:
        groups = [[z * rest + c for c in range(rest)] for z in range(zc)]
        pieces = [
            lax.all_gather(piece, "box", axis=1, tiled=True, axis_index_groups=groups)
            for piece in pieces
        ]

    order = [(s,) for s in range(zc - 1, -1, -1)]
    back = []
    for w in range(wide):
        parts = [piece[w] for piece in pieces]
        back.append(translate(zc, rest, w, par_cnt, order, picks, factors, parts))
    quarter = []
    for s in range(zc):
        result = jnp.stack([b[s] for b in back])
        quarter.append(exchange(result, "box", s * rest) if s else result)
    quarter = jnp.concatenate(quarter, 0)

    received = [exchange(quarter, "dir", mask) for mask in range(1, ndir)]
    out = backward(0, wide, rest, ndir == 1, mine, cosine, sine, quarter, None)
    for mask, quarter in zip(range(1, ndir), received):
        out = backward(mask, wide, rest, mask == ndir - 1, mine, cosine, sine, quarter, out)
    return out.reshape(child_cnt, cols, kq)


def solution(mesh):
    in_specs = (P("box", None, "dir"), P(), P(), P(None, None, "dir"), P(), P())
    out_specs = P("box", None, "dir")

    return jax.shard_map(
        per_device, mesh=mesh, in_specs=in_specs, out_specs=out_specs, check_vma=False
    )
```

time: 51.3 us -> 45.2 us (0.88)
  Pallas kernels: 19.2 us -> 10.2 us
  waiting for transfers between devices: 13.3 us -> 16.6 us
  other arithmetic: 0.77 us -> 0.09 us
    pallas_call x8, Pallas kernels: 12.4 us -> 6.45 us  [the longest x4 2.66 us: backward(): pl.pallas_call(functools.partial(backward_kernel, mask, wide, rest, last)...]
    ppermute x16, waiting for transfers between devices: 13.3 us -> 16.6 us  [exchange(): return lax.ppermute(value, axis, [(i, i ^ mask) for i in range(size)])]
    pallas_call x2 -> x3, Pallas kernels: 2.87 us -> 1.38 us  [forward(): pl.pallas_call(functools.partial(forward_kernel, mask), out_shape=jax.Sha...]
    pallas_call x1, Pallas kernels: 2.62 us -> 1.64 us  [first_forward(): pl.pallas_call(functools.partial(first_kernel, mask), out_shape=[jax.Shap...]
    reshape x1 -> x0, other arithmetic: 0.61 us -> none  [per_device(): picks = [(nbr_index * cols).T.reshape(-1), nbr_trans.T.reshape(-1)]]
    pallas_call x1, Pallas kernels: 1.34 us -> 0.73 us  [translate(): pl.pallas_call(functools.partial(first_translate_kernel, zc, rest, target...]
  transfers between devices with their start and end apart: 16 -> 16, of which waited for: 8 -> 9; matrix products, arithmetic and copies ran while one was open for 1% -> 0% of each run, Pallas kernels for 18% -> 11%
where the time goes in v3:
time: 45.2 us; the launch traced here: 45 us
  starting transfers between devices  17.7 us (39%)
  waiting for transfers between devices  16.6 us (37%)
  Pallas kernels  10.2 us (23%)
    ppermute x16, starting transfers between devices, exchange(): return lax.ppermute(value, axis, [(i, i ^ mask) for i in range(size)])  17.7 us
    ppermute x16, waiting for transfers between devices, exchange(): return lax.ppermute(value, axis, [(i, i ^ mask) for i in range(size)])  16.6 us
    pallas_call x4, Pallas kernels, backward(): pl.pallas_call(functools.partial(backward_kernel, mask, wide, rest, last)...  2.66 us
    pallas_call x1, Pallas kernels, prepare(): pl.pallas_call(functools.partial(prepare_kernel, zc, rest, wide), out_sha...  2.24 us
    pallas_call x1, Pallas kernels, first_forward(): pl.pallas_call(functools.partial(first_kernel, mask), out_shape=[jax.Shap...  1.64 us
    pallas_call x3, Pallas kernels, translate(): result = call(picks, factors, source)  1.55 us
    pallas_call x3, Pallas kernels, forward(): pl.pallas_call(functools.partial(forward_kernel, mask), out_shape=jax.Sha...  1.38 us
  transfers between devices with their start and end apart: 16, of which 9 were waited for; matrix products, arithmetic and copies ran while one was open for 0% of the time, Pallas kernels for 11%

profile of v3, /device:TPU:0, one launch (start us, length us, event | category | flops | bytes accessed | tf_op | source)
XLA Modules:
  0.0 45.0 jit_solution(13972531555466466588)
XLA Ops:
  0.0 1.6 %first_forward.1 = (bf16[4,16,8,128]{3,2,1,0:T(8,128)(2,1)S(1)}, bf16[1024,128]{1,0:T(8,128)(2,1)S(1)}, bf16[128,2048]{1,0:T(8,128)(2,1)S(1)}, f32[8,2048]{1,0:T(8,128)S(1)}, f32[8,2048]{1,0:T(8,128)S(1)}) custom-call(bf16[1024,128]{1,0:T(8,128)(2,1)} %bitcast.26, bf16[512,2048]{1,0:T(8,128)(2,1)} %interp_any.1, f32[8,2048]{1,0:T(8,128)} %angle_any.1), custom_call_target="tpu_custom_call" | custom-call | tf_op jit(solution)/shard_map/first_forward/pallas_call | solution.py:101
  2.2 3.1 %collective-permute-start.1 = (bf16[4,16,8,128]{3,2,1,0:T(8,128)(2,1)S(1)}, bf16[4,16,8,128]{3,2,1,0:T(8,128)(2,1)S(1)}, u32[]{:S(2)}, u32[]{:S(2)}) collective-permute-start(bf16[4,16,8,128]{3,2,1,0:T(8,128)(2,1)S(1)} %forward.4), channel_id=1, source_target_pairs={{0,2},{1,3},{2,0},{3,1},{4,6},{5,7},{6,4},{7,5},{8,10},{9,11},{10,... | collective-permute-start | bytes 393224 | tf_op jit(solution)/shard_map/ppermute | solution.py:360
  5.7 1.6 %collective-permute-start.2 = (bf16[4,16,8,128]{3,2,1,0:T(8,128)(2,1)S(1)}, bf16[4,16,8,128]{3,2,1,0:T(8,128)(2,1)S(1)}, u32[]{:S(2)}, u32[]{:S(2)}) collective-permute-start(bf16[4,16,8,128]{3,2,1,0:T(8,128)(2,1)S(1)} %forward.5), channel_id=1, source_target_pairs={{0,1},{1,0},{2,3},{3,2},{4,5},{5,4},{6,7},{7,6},{8,9},{9,8},{10,11... | collective-permute-start | bytes 393224 | tf_op jit(solution)/shard_map/ppermute | solution.py:360
  7.7 1.0 %collective-permute-done.1 = bf16[4,16,8,128]{3,2,1,0:T(8,128)(2,1)S(1)} collective-permute-done((bf16[4,16,8,128]{3,2,1,0:T(8,128)(2,1)S(1)}, bf16[4,16,8,128]{3,2,1,0:T(8,128)(2,1)S(1)}, u32[]{:S(2)}, u32[]{:S(2)}) %collective-permute-start.1) | collective-permute-done | bytes 131104 | tf_op jit(solution)/shard_map/ppermute | solution.py:360
  8.7 3.4 %collective-permute-done.2 = bf16[4,16,8,128]{3,2,1,0:T(8,128)(2,1)S(1)} collective-permute-done((bf16[4,16,8,128]{3,2,1,0:T(8,128)(2,1)S(1)}, bf16[4,16,8,128]{3,2,1,0:T(8,128)(2,1)S(1)}, u32[]{:S(2)}, u32[]{:S(2)}) %collective-permute-start.2) | collective-permute-done | bytes 131104 | tf_op jit(solution)/shard_map/ppermute | solution.py:360
  12.1 1.1 %collective-permute-done = bf16[4,16,8,128]{3,2,1,0:T(8,128)(2,1)S(1)} collective-permute-done((bf16[4,16,8,128]{3,2,1,0:T(8,128)(2,1)S(1)}, bf16[4,16,8,128]{3,2,1,0:T(8,128)(2,1)S(1)}, u32[]{:S(2)}, u32[]{:S(2)}) %collective-permute-start) | collective-permute-done | bytes 131104 | tf_op jit(solution)/shard_map/ppermute | solution.py:360
  13.4 3.9 %collective-permute-start.8 = (bf16[1,16,8,128]{3,2,1,0:T(8,128)(2,1)S(1)}, bf16[1,16,8,128]{3,2,1,0:T(8,128)(2,1)S(1)}, u32[]{:S(2)}, u32[]{:S(2)}) collective-permute-start(bf16[1,16,8,128]{3,2,1,0:T(8,128)(2,1)S(1)} %get-tuple-element.23), channel_id=1, source_target_pairs={{0,24},{4,28},{8,16},{12,20},{16,8},{20,12},{24,0},{28,4},{1,25},{... | collective-permute-start | bytes 98312 | tf_op jit(solution)/shard_map/ppermute | solution.py:360
  17.2 0.6 %collective-permute-start.4 = (bf16[1,16,8,128]{3,2,1,0:T(8,128)(2,1)S(1)}, bf16[1,16,8,128]{3,2,1,0:T(8,128)(2,1)S(1)}, u32[]{:S(2)}, u32[]{:S(2)}) collective-permute-start(bf16[1,16,8,128]{3,2,1,0:T(8,128)(2,1)S(1)} %get-tuple-element.25), channel_id=1, source_target_pairs={{0,8},{4,12},{8,0},{12,4},{16,24},{20,28},{24,16},{28,20},{1,9},{5... | collective-permute-start | bytes 98312 | tf_op jit(solution)/shard_map/ppermute | solution.py:360
  18.2 1.1 %collective-permute-done.8 = bf16[1,16,8,128]{3,2,1,0:T(8,128)(2,1)S(1)} collective-permute-done((bf16[1,16,8,128]{3,2,1,0:T(8,128)(2,1)S(1)}, bf16[1,16,8,128]{3,2,1,0:T(8,128)(2,1)S(1)}, u32[]{:S(2)}, u32[]{:S(2)}) %collective-permute-start.8) | collective-permute-done | bytes 32800 | tf_op jit(solution)/shard_map/ppermute | solution.py:360
  19.3 2.7 %collective-permute-done.6 = bf16[1,16,8,128]{3,2,1,0:T(8,128)(2,1)S(1)} collective-permute-done((bf16[1,16,8,128]{3,2,1,0:T(8,128)(2,1)S(1)}, bf16[1,16,8,128]{3,2,1,0:T(8,128)(2,1)S(1)}, u32[]{:S(2)}, u32[]{:S(2)}) %collective-permute-start.6) | collective-permute-done | bytes 32800 | tf_op jit(solution)/shard_map/ppermute | solution.py:360
  22.1 0.5 %collective-permute-start.5 = (bf16[1,16,8,128]{3,2,1,0:T(8,128)(2,1)S(1)}, bf16[1,16,8,128]{3,2,1,0:T(8,128)(2,1)S(1)}, u32[]{:S(2)}, u32[]{:S(2)}) collective-permute-start(bf16[1,16,8,128]{3,2,1,0:T(8,128)(2,1)S(1)} %collective-permute-done.4), channel_id=1, source_target_pairs={{0,4},{4,0},{8,12},{12,8},{16,20},{20,16},{24,28},{28,24},{1,5},{5... | collective-permute-start | bytes 98312 | tf_op jit(solution)/shard_map/ppermute | solution.py:360
  22.6 2.2 %prepare.1 = (bf16[4,432,128]{2,1,0:T(8,128)(2,1)S(1)}, f32[1,4,2,432,128]{4,3,2,1,0:T(8,128)S(1)}) custom-call(s32[128,27]{1,0:T(8,128)S(1)} %shift-left_or_fusion.words_ref, f32[343,2,512]{2,1,0:T(2,128)} %tables_any.1), custom_call_target="tpu_custom_call" | custom-call | tf_op jit(solution)/shard_map/prepare/pallas_call | solution.py:185
  24.9 0.7 %first_translate.1 = (bf16[16,8,128]{2,1,0:T(8,128)(2,1)S(1)}, bf16[8,128,128]{2,1,0:T(8,128)(2,1)S(1)}) custom-call(bf16[4,432,128]{2,1,0:T(8,128)(2,1)S(1)} %get-tuple-element.17.pick_ref, f32[1,4,2,432,128]{4,3,2,1,0:T(8,128)S(1)} %get-tuple-element.18.factor_ref, bf16[16,8,128]{2,1,0:T(8,128)(2,1)S(1)} %bitcast.14, bf16[16,8,128]{2,1,0:T(8,128)(2,1)S(1)} %bitcast.19, ...), custom_call_target="tpu_custom_call" | custom-call | tf_op jit(solution)/shard_map/first_translate/pallas_call | solution.py:274
  25.6 0.5 %translate.5 = bf16[16,8,128]{2,1,0:T(8,128)(2,1)S(1)} custom-call(bf16[4,432,128]{2,1,0:T(8,128)(2,1)S(1)} %get-tuple-element.17.pick_ref, f32[1,4,2,432,128]{4,3,2,1,0:T(8,128)S(1)} %get-tuple-element.18.factor_ref, bf16[8,128,128]{2,1,0:T(8,128)(2,1)S(1)} %get-tuple-element.21.source), custom_call_target="tpu_custom_call" | custom-call | tf_op jit(solution)/shard_map/translate/pallas_call | solution.py:293
  26.1 0.5 %translate.4 = bf16[16,8,128]{2,1,0:T(8,128)(2,1)S(1)} custom-call(bf16[4,432,128]{2,1,0:T(8,128)(2,1)S(1)} %get-tuple-element.17.pick_ref, f32[1,4,2,432,128]{4,3,2,1,0:T(8,128)S(1)} %get-tuple-element.18.factor_ref, bf16[8,128,128]{2,1,0:T(8,128)(2,1)S(1)} %get-tuple-element.21.source), custom_call_target="tpu_custom_call" | custom-call | tf_op jit(solution)/shard_map/translate/pallas_call | solution.py:293
  26.7 1.6 %collective-permute-start.11 = (bf16[1,16,8,128]{3,2,1,0:T(8,128)(2,1)S(1)}, bf16[1,16,8,128]{3,2,1,0:T(8,128)(2,1)S(1)}, u32[]{:S(2)}, u32[]{:S(2)}) collective-permute-start(bf16[1,16,8,128]{3,2,1,0:T(8,128)(2,1)S(1)} %bitcast.23), channel_id=1, source_target_pairs={{0,16},{4,20},{8,24},{12,28},{16,0},{20,4},{24,8},{28,12},{1,17},{... | collective-permute-start | bytes 98312 | tf_op jit(solution)/shard_map/ppermute | solution.py:360
  28.2 2.8 %collective-permute-start.12 = (bf16[1,16,8,128]{3,2,1,0:T(8,128)(2,1)S(1)}, bf16[1,16,8,128]{3,2,1,0:T(8,128)(2,1)S(1)}, u32[]{:S(2)}, u32[]{:S(2)}) collective-permute-start(bf16[1,16,8,128]{3,2,1,0:T(8,128)(2,1)S(1)} %bitcast.25), channel_id=1, source_target_pairs={{0,24},{4,28},{8,16},{12,20},{16,8},{20,12},{24,0},{28,4},{1,25},{... | collective-permute-start | bytes 98312 | tf_op jit(solution)/shard_map/ppermute | solution.py:360
  31.0 0.5 %translate.3 = bf16[16,8,128]{2,1,0:T(8,128)(2,1)S(1)} custom-call(bf16[4,432,128]{2,1,0:T(8,128)(2,1)S(1)} %get-tuple-element.17.pick_ref, f32[1,4,2,432,128]{4,3,2,1,0:T(8,128)S(1)} %get-tuple-element.18.factor_ref, bf16[8,128,128]{2,1,0:T(8,128)(2,1)S(1)} %get-tuple-element.21.source), custom_call_target="tpu_custom_call" | custom-call | tf_op jit(solution)/shard_map/translate/pallas_call | solution.py:293
  31.7 2.2 %collective-permute-done.12 = bf16[1,16,8,128]{3,2,1,0:T(8,128)(2,1)S(1)} collective-permute-done((bf16[1,16,8,128]{3,2,1,0:T(8,128)(2,1)S(1)}, bf16[1,16,8,128]{3,2,1,0:T(8,128)(2,1)S(1)}, u32[]{:S(2)}, u32[]{:S(2)}) %collective-permute-start.12) | collective-permute-done | bytes 32800 | tf_op jit(solution)/shard_map/ppermute | solution.py:360
  34.0 1.5 %collective-permute-start.15 = (bf16[4,16,8,128]{3,2,1,0:T(8,128)(2,1)S(1)}, bf16[4,16,8,128]{3,2,1,0:T(8,128)(2,1)S(1)}, u32[]{:S(2)}, u32[]{:S(2)}) collective-permute-start(bf16[4,16,8,128]{3,2,1,0:T(8,128)(2,1)S(1)} %pad_maximum_fusion.quarter), channel_id=1, source_target_pairs={{0,1},{1,0},{2,3},{3,2},{4,5},{5,4},{6,7},{7,6},{8,9},{9,8},{10,11... | collective-permute-start | bytes 393224 | tf_op jit(solution)/shard_map/ppermute | solution.py:360
  35.5 1.5 %collective-permute-start.14 = (bf16[4,16,8,128]{3,2,1,0:T(8,128)(2,1)S(1)}, bf16[4,16,8,128]{3,2,1,0:T(8,128)(2,1)S(1)}, u32[]{:S(2)}, u32[]{:S(2)}) collective-permute-start(bf16[4,16,8,128]{3,2,1,0:T(8,128)(2,1)S(1)} %pad_maximum_fusion.quarter), channel_id=1, source_target_pairs={{0,2},{1,3},{2,0},{3,1},{4,6},{5,7},{6,4},{7,5},{8,10},{9,11},{10,... | collective-permute-start | bytes 393224 | tf_op jit(solution)/shard_map/ppermute | solution.py:360
  38.0 1.8 %collective-permute-done.15.quarter = bf16[4,16,8,128]{3,2,1,0:T(8,128)(2,1)S(1)} collective-permute-done((bf16[4,16,8,128]{3,2,1,0:T(8,128)(2,1)S(1)}, bf16[4,16,8,128]{3,2,1,0:T(8,128)(2,1)S(1)}, u32[]{:S(2)}, u32[]{:S(2)}) %collective-permute-start.15) | collective-permute-done | bytes 131104 | tf_op jit(solution)/shard_map/ppermute | solution.py:360
  40.3 3.0 %collective-permute-done.14.quarter = bf16[4,16,8,128]{3,2,1,0:T(8,128)(2,1)S(1)} collective-permute-done((bf16[4,16,8,128]{3,2,1,0:T(8,128)(2,1)S(1)}, bf16[4,16,8,128]{3,2,1,0:T(8,128)(2,1)S(1)}, u32[]{:S(2)}, u32[]{:S(2)}) %collective-permute-start.14) | collective-permute-done | bytes 131104 | tf_op jit(solution)/shard_map/ppermute | solution.py:360
  43.8 1.2 %backward.7 = bf16[1024,128]{1,0:T(8,128)(2,1)} custom-call(bf16[128,2048]{1,0:T(8,128)(2,1)S(1)} %get-tuple-element.14.interp_ref, f32[8,2048]{1,0:T(8,128)S(1)} %get-tuple-element.15.cos_ref, f32[8,2048]{1,0:T(8,128)S(1)} %get-tuple-element.16.sin_ref, bf16[4,16,8,128]{3,2,1,0:T(8,128)(2,1)S(1)} %collective-permute-done.13.quarter, ...), custom_call_target="tpu_custom_call" | custom-call | tf_op jit(solution)/shard_map/backward/pallas_call | solution.py:342
  (31 shorter events, 3.9 us)
Async XLA Ops:
  2.1 15.7 %copy-start = (s32[128,27]{0,1:T(8,128)S(1)}, s32[128,27]{0,1:T(8,128)}, u32[]{:S(2)}) copy-start(s32[128,27]{0,1:T(8,128)} %param.10) | copy-start | bytes 41476
  2.1 15.8 %copy-start.1 = (s32[128,27]{0,1:T(8,128)S(1)}, s32[128,27]{0,1:T(8,128)}, u32[]{:S(2)}) copy-start(s32[128,27]{0,1:T(8,128)} %param.11) | copy-start | bytes 41476
  2.2 6.6 %collective-permute-start.1 = (bf16[4,16,8,128]{3,2,1,0:T(8,128)(2,1)S(1)}, bf16[4,16,8,128]{3,2,1,0:T(8,128)(2,1)S(1)}, u32[]{:S(2)}, u32[]{:S(2)}) collective-permute-start(bf16[4,16,8,128]{3,2,1,0:T(8,128)(2,1)S(1)} %forward.4), channel_id=1, source_target_pairs={{0,2},{1,3},{2,0},{3,1},{4,6},{5,7},{6,4},{7,5},{8,10},{9,11},{10,... | collective-permute-start | bytes 393224 | tf_op jit(solution)/shard_map/ppermute | solution.py:360
  5.7 6.4 %collective-permute-start.2 = (bf16[4,16,8,128]{3,2,1,0:T(8,128)(2,1)S(1)}, bf16[4,16,8,128]{3,2,1,0:T(8,128)(2,1)S(1)}, u32[]{:S(2)}, u32[]{:S(2)}) collective-permute-start(bf16[4,16,8,128]{3,2,1,0:T(8,128)(2,1)S(1)} %forward.5), channel_id=1, source_target_pairs={{0,1},{1,0},{2,3},{3,2},{4,5},{5,4},{6,7},{7,6},{8,9},{9,8},{10,11... | collective-permute-start | bytes 393224 | tf_op jit(solution)/shard_map/ppermute | solution.py:360
  7.2 6.0 %collective-permute-start = (bf16[4,16,8,128]{3,2,1,0:T(8,128)(2,1)S(1)}, bf16[4,16,8,128]{3,2,1,0:T(8,128)(2,1)S(1)}, u32[]{:S(2)}, u32[]{:S(2)}) collective-permute-start(bf16[4,16,8,128]{3,2,1,0:T(8,128)(2,1)S(1)} %get-tuple-element.20), channel_id=1, source_target_pairs={{0,3},{1,2},{2,1},{3,0},{4,7},{5,6},{6,5},{7,4},{8,11},{9,10},{10,... | collective-permute-start | bytes 393224 | tf_op jit(solution)/shard_map/ppermute | solution.py:360
  13.4 6.0 %collective-permute-start.8 = (bf16[1,16,8,128]{3,2,1,0:T(8,128)(2,1)S(1)}, bf16[1,16,8,128]{3,2,1,0:T(8,128)(2,1)S(1)}, u32[]{:S(2)}, u32[]{:S(2)}) collective-permute-start(bf16[1,16,8,128]{3,2,1,0:T(8,128)(2,1)S(1)} %get-tuple-element.23), channel_id=1, source_target_pairs={{0,24},{4,28},{8,16},{12,20},{16,8},{20,12},{24,0},{28,4},{1,25},{... | collective-permute-start | bytes 98312 | tf_op jit(solution)/shard_map/ppermute | solution.py:360
  17.2 4.8 %collective-permute-start.6 = (bf16[1,16,8,128]{3,2,1,0:T(8,128)(2,1)S(1)}, bf16[1,16,8,128]{3,2,1,0:T(8,128)(2,1)S(1)}, u32[]{:S(2)}, u32[]{:S(2)}) collective-permute-start(bf16[1,16,8,128]{3,2,1,0:T(8,128)(2,1)S(1)} %get-tuple-element.24), channel_id=1, source_target_pairs={{0,16},{4,20},{8,24},{12,28},{16,0},{20,4},{24,8},{28,12},{1,17},{... | collective-permute-start | bytes 98312 | tf_op jit(solution)/shard_map/ppermute | solution.py:360
  17.2 4.8 %collective-permute-start.4 = (bf16[1,16,8,128]{3,2,1,0:T(8,128)(2,1)S(1)}, bf16[1,16,8,128]{3,2,1,0:T(8,128)(2,1)S(1)}, u32[]{:S(2)}, u32[]{:S(2)}) collective-permute-start(bf16[1,16,8,128]{3,2,1,0:T(8,128)(2,1)S(1)} %get-tuple-element.25), channel_id=1, source_target_pairs={{0,8},{4,12},{8,0},{12,4},{16,24},{20,28},{24,16},{28,20},{1,9},{5... | collective-permute-start | bytes 98312 | tf_op jit(solution)/shard_map/ppermute | solution.py:360
  18.1 6.7 %collective-permute-start.3 = (bf16[1,16,8,128]{3,2,1,0:T(8,128)(2,1)S(1)}, bf16[1,16,8,128]{3,2,1,0:T(8,128)(2,1)S(1)}, u32[]{:S(2)}, u32[]{:S(2)}) collective-permute-start(bf16[1,16,8,128]{3,2,1,0:T(8,128)(2,1)S(1)} %get-tuple-element.26), channel_id=1, source_target_pairs={{0,4},{4,0},{8,12},{12,8},{16,20},{20,16},{24,28},{28,24},{1,5},{5... | collective-permute-start | bytes 98312 | tf_op jit(solution)/shard_map/ppermute | solution.py:360
  19.3 5.5 %collective-permute-start.9 = (bf16[1,16,8,128]{3,2,1,0:T(8,128)(2,1)S(1)}, bf16[1,16,8,128]{3,2,1,0:T(8,128)(2,1)S(1)}, u32[]{:S(2)}, u32[]{:S(2)}) collective-permute-start(bf16[1,16,8,128]{3,2,1,0:T(8,128)(2,1)S(1)} %collective-permute-done.8), channel_id=1, source_target_pairs={{0,4},{4,0},{8,12},{12,8},{16,20},{20,16},{24,28},{28,24},{1,5},{5... | collective-permute-start | bytes 98312 | tf_op jit(solution)/shard_map/ppermute | solution.py:360
  22.1 2.8 %collective-permute-start.7 = (bf16[1,16,8,128]{3,2,1,0:T(8,128)(2,1)S(1)}, bf16[1,16,8,128]{3,2,1,0:T(8,128)(2,1)S(1)}, u32[]{:S(2)}, u32[]{:S(2)}) collective-permute-start(bf16[1,16,8,128]{3,2,1,0:T(8,128)(2,1)S(1)} %collective-permute-done.6), channel_id=1, source_target_pairs={{0,4},{4,0},{8,12},{12,8},{16,20},{20,16},{24,28},{28,24},{1,5},{5... | collective-permute-start | bytes 98312 | tf_op jit(solution)/shard_map/ppermute | solution.py:360
  22.1 2.8 %collective-permute-start.5 = (bf16[1,16,8,128]{3,2,1,0:T(8,128)(2,1)S(1)}, bf16[1,16,8,128]{3,2,1,0:T(8,128)(2,1)S(1)}, u32[]{:S(2)}, u32[]{:S(2)}) collective-permute-start(bf16[1,16,8,128]{3,2,1,0:T(8,128)(2,1)S(1)} %collective-permute-done.4), channel_id=1, source_target_pairs={{0,4},{4,0},{8,12},{12,8},{16,20},{20,16},{24,28},{28,24},{1,5},{5... | collective-permute-start | bytes 98312 | tf_op jit(solution)/shard_map/ppermute | solution.py:360
  26.6 4.9 %collective-permute-start.10 = (bf16[1,16,8,128]{3,2,1,0:T(8,128)(2,1)S(1)}, bf16[1,16,8,128]{3,2,1,0:T(8,128)(2,1)S(1)}, u32[]{:S(2)}, u32[]{:S(2)}) collective-permute-start(bf16[1,16,8,128]{3,2,1,0:T(8,128)(2,1)S(1)} %bitcast.24), channel_id=1, source_target_pairs={{0,8},{4,12},{8,0},{12,4},{16,24},{20,28},{24,16},{28,20},{1,9},{5... | collective-permute-start | bytes 98312 | tf_op jit(solution)/shard_map/ppermute | solution.py:360
  26.7 5.1 %collective-permute-start.11 = (bf16[1,16,8,128]{3,2,1,0:T(8,128)(2,1)S(1)}, bf16[1,16,8,128]{3,2,1,0:T(8,128)(2,1)S(1)}, u32[]{:S(2)}, u32[]{:S(2)}) collective-permute-start(bf16[1,16,8,128]{3,2,1,0:T(8,128)(2,1)S(1)} %bitcast.23), channel_id=1, source_target_pairs={{0,16},{4,20},{8,24},{12,28},{16,0},{20,4},{24,8},{28,12},{1,17},{... | collective-permute-start | bytes 98312 | tf_op jit(solution)/shard_map/ppermute | solution.py:360
  28.2 5.7 %collective-permute-start.12 = (bf16[1,16,8,128]{3,2,1,0:T(8,128)(2,1)S(1)}, bf16[1,16,8,128]{3,2,1,0:T(8,128)(2,1)S(1)}, u32[]{:S(2)}, u32[]{:S(2)}) collective-permute-start(bf16[1,16,8,128]{3,2,1,0:T(8,128)(2,1)S(1)} %bitcast.25), channel_id=1, source_target_pairs={{0,24},{4,28},{8,16},{12,20},{16,8},{20,12},{24,0},{28,4},{1,25},{... | collective-permute-start | bytes 98312 | tf_op jit(solution)/shard_map/ppermute | solution.py:360
  34.0 5.9 %collective-permute-start.15 = (bf16[4,16,8,128]{3,2,1,0:T(8,128)(2,1)S(1)}, bf16[4,16,8,128]{3,2,1,0:T(8,128)(2,1)S(1)}, u32[]{:S(2)}, u32[]{:S(2)}) collective-permute-start(bf16[4,16,8,128]{3,2,1,0:T(8,128)(2,1)S(1)} %pad_maximum_fusion.quarter), channel_id=1, source_target_pairs={{0,1},{1,0},{2,3},{3,2},{4,5},{5,4},{6,7},{7,6},{8,9},{9,8},{10,11... | collective-permute-start | bytes 393224 | tf_op jit(solution)/shard_map/ppermute | solution.py:360
  35.5 7.8 %collective-permute-start.14 = (bf16[4,16,8,128]{3,2,1,0:T(8,128)(2,1)S(1)}, bf16[4,16,8,128]{3,2,1,0:T(8,128)(2,1)S(1)}, u32[]{:S(2)}, u32[]{:S(2)}) collective-permute-start(bf16[4,16,8,128]{3,2,1,0:T(8,128)(2,1)S(1)} %pad_maximum_fusion.quarter), channel_id=1, source_target_pairs={{0,2},{1,3},{2,0},{3,1},{4,6},{5,7},{6,4},{7,5},{8,10},{9,11},{10,... | collective-permute-start | bytes 393224 | tf_op jit(solution)/shard_map/ppermute | solution.py:360
  37.0 6.8 %collective-permute-start.13 = (bf16[4,16,8,128]{3,2,1,0:T(8,128)(2,1)S(1)}, bf16[4,16,8,128]{3,2,1,0:T(8,128)(2,1)S(1)}, u32[]{:S(2)}, u32[]{:S(2)}) collective-permute-start(bf16[4,16,8,128]{3,2,1,0:T(8,128)(2,1)S(1)} %pad_maximum_fusion.quarter), channel_id=1, source_target_pairs={{0,3},{1,2},{2,1},{3,0},{4,7},{5,6},{6,5},{7,4},{8,11},{9,10},{10,... | collective-permute-start | bytes 393224 | tf_op jit(solution)/shard_map/ppermute | solution.py:360

commit v4 on v3

--- a/solution.py
+++ b/solution.py
@@ -48,19 +48,23 @@
     return sine, cosine
 
 
-def add_octants(start, x_ref, interp_ref, cos_ref, sin_ref, out_ref):
+def add_octants(x_ref, interp_ref, angle_ref, start, out_ref, cos_ref, sin_ref):
     chunks, par_cnt, cols, _ = out_ref.shape
+    width = chunks * LANES
     span = min(chunks, 2)
     sign = half_sign(cols, -1.0)
+    sine_all, cosine_all = sine_cosine(angle_ref[:, pl.ds(start, width)])
+    cos_ref[...] = cosine_all
+    sin_ref[...] = sine_all
     for base in range(0, chunks, span):
         at = pl.multiple_of(start + base * LANES, LANES)
         field = jnp.dot(
             x_ref[...], interp_ref[:, pl.ds(at, span * LANES)], preferred_element_type=jnp.float32
         )
         for chunk in range(span):
-            lanes = pl.ds(pl.multiple_of(at + chunk * LANES, LANES), LANES)
-            cosine = [jnp.broadcast_to(cos_ref[o : o + 1, lanes], (cols, LANES)) for o in range(CH)]
-            sine = [jnp.broadcast_to(sin_ref[o : o + 1, lanes], (cols, LANES)) for o in range(CH)]
+            here = slice((base + chunk) * LANES, (base + chunk + 1) * LANES)
+            cosine = [jnp.broadcast_to(cos_ref[o : o + 1, here], (cols, LANES)) for o in range(CH)]
+            sine = [jnp.broadcast_to(sin_ref[o : o + 1, here], (cols, LANES)) for o in range(CH)]
             for p in range(par_cnt):
                 same = cross = None
                 for o in range(CH):
@@ -73,25 +77,34 @@
 
 
 def first_kernel(mask, x_any, interp_any, angle_any, *refs):
-    out_ref, x_ref, interp_ref, cos_ref, sin_ref, angle_ref, sems = refs
-    load_angle = pltpu.make_async_copy(angle_any, angle_ref, sems.at[2])
-    load_angle.start()
+    out_ref, cos_ref, sin_ref, x_ref, interp_ref, angle_ref, sems = refs
     width = out_ref.shape[0] * LANES
     rows = interp_ref.shape[0]
     dir_at = lax.axis_index("dir")
     start = pl.multiple_of((dir_at ^ mask) * width, width)
     mine = pl.ds(pl.multiple_of(dir_at * rows, rows), rows)
-    load_x = pltpu.make_async_copy(x_any, x_ref, sems.at[0])
-    load_interp = pltpu.make_async_copy(interp_any.at[mine], interp_ref, sems.at[1])
-    load_x.start()
-    load_interp.start()
-    load_angle.wait()
-    sine, cosine = sine_cosine(angle_ref[...])
-    cos_ref[...] = cosine
-    sin_ref[...] = sine
-    load_x.wait()
-    load_interp.wait()
-    add_octants(start, x_ref, interp_ref, cos_ref, sin_ref, out_ref)
+    loads = [
+        pltpu.make_async_copy(angle_any, angle_ref, sems.at[0]),
+        pltpu.make_async_copy(x_any, x_ref, sems.at[1]),
+    ]
+    for step in range(interp_ref.shape[1] // width):
+        at = pl.multiple_of((dir_at ^ mask ^ step) * width, width)
+        here = interp_ref.at[:, pl.ds(at, width)]
+        loads.append(
+            pltpu.make_async_copy(interp_any.at[mine, pl.ds(at, width)], here, sems.at[2 + step])
+        )
+    for load in loads:
+        load.start()
+    for load in loads[:3]:
+        load.wait()
+    add_octants(x_ref, interp_ref, angle_ref, start, out_ref, cos_ref, sin_ref)
+    for load in loads[3:]:
+        load.wait()
+
+
+def quarter_shapes(chunks, par_cnt, cols, kind):
+    table = jax.ShapeDtypeStruct((CH, chunks * LANES), jnp.float32)
+    return [jax.ShapeDtypeStruct((chunks, par_cnt, cols, LANES), kind), table, table]
 
 
 def first_forward(mask, chunks, cols, x, interp, angle):
@@ -100,41 +113,37 @@
     par_cnt = rows // (CH * cols)
     return pl.pallas_call(
         functools.partial(first_kernel, mask),
-        out_shape=[
-            jax.ShapeDtypeStruct((chunks, par_cnt, cols, LANES), jnp.bfloat16),
+        out_shape=quarter_shapes(chunks, par_cnt, cols, jnp.bfloat16)
+        + [
             jax.ShapeDtypeStruct(x.shape, x.dtype),
             jax.ShapeDtypeStruct((kq, npd), interp.dtype),
             jax.ShapeDtypeStruct(angle.shape, jnp.float32),
-            jax.ShapeDtypeStruct(angle.shape, jnp.float32),
         ],
         in_specs=[FAR, FAR, FAR],
-        out_specs=[VMEM] * 5,
-        scratch_shapes=[
-            pltpu.VMEM(angle.shape, jnp.float32),
-            pltpu.SemaphoreType.DMA((3,)),
-        ],
+        out_specs=[VMEM] * 6,
+        scratch_shapes=[pltpu.SemaphoreType.DMA((2 + npd // (chunks * LANES),))],
         compiler_params=GRANT,
         name="first_forward",
     )(x, interp, angle)
 
 
-def forward_kernel(mask, x_ref, interp_ref, cos_ref, sin_ref, out_ref):
+def forward_kernel(mask, x_ref, interp_ref, angle_ref, out_ref, cos_ref, sin_ref):
     width = out_ref.shape[0] * LANES
     start = pl.multiple_of((lax.axis_index("dir") ^ mask) * width, width)
-    add_octants(start, x_ref, interp_ref, cos_ref, sin_ref, out_ref)
-
-
-def forward(mask, chunks, cols, x, interp, cosine, sine):
-    rows = x.shape[0]
-    shape = (chunks, rows // (CH * cols), cols, LANES)
+    add_octants(x_ref, interp_ref, angle_ref, start, out_ref, cos_ref, sin_ref)
+
+
+def forward(mask, chunks, cols, x, interp, angle):
+    par_cnt = x.shape[0] // (CH * cols)
+    kind = jnp.bfloat16 if mask else jnp.float32
     return pl.pallas_call(
         functools.partial(forward_kernel, mask),
-        out_shape=jax.ShapeDtypeStruct(shape, jnp.bfloat16 if mask else jnp.float32),
-        in_specs=[VMEM, VMEM, VMEM, VMEM],
-        out_specs=VMEM,
+        out_shape=quarter_shapes(chunks, par_cnt, cols, kind),
+        in_specs=[VMEM, VMEM, VMEM],
+        out_specs=[VMEM] * 3,
         compiler_params=GRANT,
         name="forward",
-    )(x, interp, cosine, sine)
+    )(x, interp, angle)
 
 
 def one_hot(column, count):
@@ -297,24 +306,29 @@
 
 
 def backward_kernel(mask, wide, rest, last, interp_ref, cos_ref, sin_ref, quarter, *refs):
-    held, out_ref = (refs[0] if len(refs) == 2 else None), refs[-1]
+    refs = list(refs)
+    sems = refs.pop() if last else None
+    kept = refs.pop() if last else None
+    out_ref = refs.pop()
+    held = refs.pop() if refs else None
     chunks, par_cnt, cols, _ = quarter.shape
     width = chunks * LANES
     span, block = min(chunks, 2), min(par_cnt, 4)
     sign = half_sign(cols, 1.0)
     dir_at, zi, _ = places(rest)
-    lane_sets = []
+    near, far_sets = [], []
     for chunk in range(chunks):
-        place = (zi ^ (chunk // wide)) * wide + chunk % wide
-        start = (dir_at ^ mask) * width + place * LANES
-        lane_sets.append(pl.ds(pl.multiple_of(start, LANES), LANES))
+        place = ((zi ^ (chunk // wide)) * wide + chunk % wide) * LANES
+        near.append(pl.ds(pl.multiple_of(place, LANES), LANES))
+        far_sets.append(pl.ds(pl.multiple_of((dir_at ^ mask) * width + place, LANES), LANES))
+    stores = []
     for first in range(0, par_cnt, block):
         here = slice(first * CH * cols, (first + block) * CH * cols)
         total = None if held is None else held[here, :]
         for base in range(0, chunks, span):
             left, right = [], []
             for chunk in range(base, base + span):
-                lanes = lane_sets[chunk]
+                lanes = near[chunk]
                 rows = []
                 for p in range(first, first + block):
                     field = quarter[chunk, p].astype(jnp.float32)
@@ -322,7 +336,7 @@
                     for o in range(CH):
                         rows.append(field * cos_ref[o : o + 1, lanes] + turned * sin_ref[o : o + 1, lanes])
                 left.append(jnp.concatenate(rows, 0).astype(jnp.bfloat16))
-                right.append(interp_ref[:, lanes])
+                right.append(interp_ref[:, far_sets[chunk]])
             part = lax.dot_general(
                 jnp.concatenate(left, 1),
                 jnp.concatenate(right, 1),
@@ -331,24 +345,36 @@
             )
             total = part if total is None else total + part
         if last:
-            total = anterp_scale * total
-        out_ref[here, :] = total.astype(out_ref.dtype)
-
-
-def backward(mask, wide, rest, last, interp, cosine, sine, quarter, held):
+            kept[here, :] = (anterp_scale * total).astype(kept.dtype)
+            store = pltpu.make_async_copy(
+                kept.at[here, :], out_ref.at[here, :], sems.at[first // block]
+            )
+            store.start()
+            stores.append(store)
+        else:
+            out_ref[here, :] = total
+    for store in stores:
+        store.wait()
+
+
+def backward(mask, wide, rest, last, interp, tables, quarter, held):
     _, par_cnt, cols, _ = quarter.shape
-    rows = par_cnt * CH * cols
+    shape = (par_cnt * CH * cols, interp.shape[0])
     kept = [] if held is None else [held]
+    if last:
+        out_shape = jax.ShapeDtypeStruct(shape, jnp.bfloat16)
+        scratch = [pltpu.VMEM(shape, jnp.bfloat16), pltpu.SemaphoreType.DMA((-(-par_cnt // 4),))]
+    else:
+        out_shape, scratch = jax.ShapeDtypeStruct(shape, jnp.float32), []
     return pl.pallas_call(
         functools.partial(backward_kernel, mask, wide, rest, last),
-        out_shape=jax.ShapeDtypeStruct(
-            (rows, interp.shape[0]), jnp.bfloat16 if last else jnp.float32
-        ),
+        out_shape=out_shape,
         in_specs=[VMEM, VMEM, VMEM, VMEM] + [VMEM] * len(kept),
-        out_specs=VMEM,
+        out_specs=FAR if last else VMEM,
+        scratch_shapes=scratch,
         compiler_params=GRANT,
         name="backward",
-    )(interp, cosine, sine, quarter, *kept)
+    )(interp, *tables, quarter, *kept)
 
 
 def far(value):
@@ -365,25 +391,21 @@
     par_cnt = child_cnt // CH
     npd = interp.shape[1]
     ndir, nbox = lax.axis_size("dir"), lax.axis_size("box")
-    jq = npd // ndir
-    zc = 1
-    while nbox % (2 * zc) == 0 and zc * 2 < nbox and jq % (2 * zc * LANES) == 0:
-        zc *= 2
-    rest = nbox // zc
-    chunks = jq // LANES
+    chunks, zc, rest = splits(npd, ndir, nbox)
     wide = chunks // zc
     zi = lax.axis_index("box") // rest
     x = child_out.reshape(child_cnt * cols, kq)
     masks = tuple(range(ndir - 1, 0, -1))
 
-    part, x, mine, cosine, sine = first_forward(
+    part, *turns, x, mine, angle = first_forward(
         masks[0], chunks, cols, far(x), far(interp), far(shift_angle)
     )
+    tables = {masks[0]: turns}
     arrived = [exchange(part, "dir", masks[0])]
     for mask in masks[1:]:
-        part = forward(mask, chunks, cols, x, mine, cosine, sine)
+        part, *tables[mask] = forward(mask, chunks, cols, x, mine, angle)
         arrived.append(exchange(part, "dir", mask))
-    total = forward(0, chunks, cols, x, mine, cosine, sine)
+    total, *tables[0] = forward(0, chunks, cols, x, mine, angle)
     words = nbr_index | (nbr_trans << 16)
     picks, factors = prepare(zc, rest, wide, words, far(translators))
     for part in arrived:
@@ -403,7 +425,7 @@
             for piece in pieces
         ]
 
-    order = [(s,) for s in range(zc - 1, -1, -1)]
+    order = [(s,) for s in home_order(zc)]
     back = []
     for w in range(wide):
         parts = [piece[w] for piece in pieces]
@@ -415,16 +437,33 @@
     quarter = jnp.concatenate(quarter, 0)
 
     received = [exchange(quarter, "dir", mask) for mask in range(1, ndir)]
-    out = backward(0, wide, rest, ndir == 1, mine, cosine, sine, quarter, None)
+    out = backward(0, wide, rest, ndir == 1, mine, tables[0], quarter, None)
     for mask, quarter in zip(range(1, ndir), received):
-        out = backward(mask, wide, rest, mask == ndir - 1, mine, cosine, sine, quarter, out)
+        out = backward(mask, wide, rest, mask == ndir - 1, mine, tables[mask], quarter, out)
     return out.reshape(child_cnt, cols, kq)
+
+
+def splits(npd, ndir, nbox):
+    jq, zc = npd // ndir, 1
+    while nbox % (2 * zc) == 0 and zc * 2 < nbox and jq % (2 * zc * LANES) == 0:
+        zc *= 2
+    return jq // LANES, zc, nbox // zc
+
+
+def home_order(zc):
+    return ((zc - 1,) + tuple(range(1, zc - 1)) if zc > 1 else ()) + (0,)
 
 
 def solution(mesh):
     in_specs = (P("box", None, "dir"), P(), P(), P(None, None, "dir"), P(), P())
     out_specs = P("box", None, "dir")
 
-    return jax.shard_map(
-        per_device, mesh=mesh, in_specs=in_specs, out_specs=out_specs, check_vma=False
-    )
+    def run(*args):
+        ndir, nbox = mesh.shape["dir"], mesh.shape["box"]
+        _, _, _ = splits(args[1].shape[1], ndir, nbox)
+        step = jax.shard_map(
+            per_device, mesh=mesh, in_specs=in_specs, out_specs=out_specs, check_vma=False
+        )
+        return step(*args)
+
+    return run

time: 45.2 us -> 44 us (0.973)
  waiting for transfers between devices: 16.6 us -> 15.5 us
    ppermute x16, waiting for transfers between devices: 16.6 us -> 15.5 us  [exchange(): return lax.ppermute(value, axis, [(i, i ^ mask) for i in range(size)])]
  transfers between devices with their start and end apart: 16 -> 16, of which waited for: 9 -> 9; matrix products, arithmetic and copies ran while one was open for 0% -> 1% of each run, Pallas kernels for 11% -> 13%
where the time goes in v4:
time: 44 us; the launch traced here: 43.8 us
  starting transfers between devices  17.7 us (40%)
  waiting for transfers between devices  15.5 us (35%)
  Pallas kernels  10 us (23%)
    ppermute x16, starting transfers between devices, exchange(): return lax.ppermute(value, axis, [(i, i ^ mask) for i in range(size)])  17.7 us
    ppermute x16, waiting for transfers between devices, exchange(): return lax.ppermute(value, axis, [(i, i ^ mask) for i in range(size)])  15.5 us
    pallas_call x4, Pallas kernels, backward(): pl.pallas_call(functools.partial(backward_kernel, mask, wide, rest, last)...  2.61 us
    pallas_call x1, Pallas kernels, prepare(): pl.pallas_call(functools.partial(prepare_kernel, zc, rest, wide), out_sha...  2.24 us
    pallas_call x1, Pallas kernels, first_forward(): pl.pallas_call(functools.partial(first_kernel, mask), out_shape=quarter_s...  1.54 us
    pallas_call x3, Pallas kernels, translate(): result = call(picks, factors, source)  1.54 us
    pallas_call x3, Pallas kernels, forward(): pl.pallas_call(functools.partial(forward_kernel, mask), out_shape=quarter...  1.37 us
  transfers between devices with their start and end apart: 16, of which 9 were waited for; matrix products, arithmetic and copies ran while one was open for 1% of the time, Pallas kernels for 13%

profile of v4, /device:TPU:0, one launch (start us, length us, event | category | flops | bytes accessed | tf_op | source)
XLA Modules:
  0.0 43.8 jit_solution(4963858402637449388)
XLA Ops:
  0.0 1.5 %first_forward.1 = (bf16[4,16,8,128]{3,2,1,0:T(8,128)(2,1)S(1)}, f32[8,512]{1,0:T(8,128)S(1)}, f32[8,512]{1,0:T(8,128)S(1)}, bf16[1024,128]{1,0:T(8,128)(2,1)S(1...) custom-call(bf16[1024,128]{1,0:T(8,128)(2,1)} %bitcast.26, bf16[512,2048]{1,0:T(8,128)(2,1)} %interp_any.1, ...), custom_call_target="tpu_custom_call" | custom-call | tf_op jit(solution)/shard_map/first_forward/pallas_call | solution.py:114
  1.6 4.0 %collective-permute-start = (bf16[4,16,8,128]{3,2,1,0:T(8,128)(2,1)S(1)}, bf16[4,16,8,128]{3,2,1,0:T(8,128)(2,1)S(1)}, u32[]{:S(2)}, u32[]{:S(2)}) collective-permute-start(bf16[4,16,8,128]{3,2,1,0:T(8,128)(2,1)S(1)} %get-tuple-element.32), channel_id=1, source_target_pairs={{0,3},{1,2},{2,1},{3,0},{4,7},{5,6},{6,5},{7,4},{8,11},{9,10},{10,... | collective-permute-start | bytes 393224 | tf_op jit(solution)/shard_map/ppermute | solution.py:386
  6.0 0.6 %collective-permute-start.2 = (bf16[4,16,8,128]{3,2,1,0:T(8,128)(2,1)S(1)}, bf16[4,16,8,128]{3,2,1,0:T(8,128)(2,1)S(1)}, u32[]{:S(2)}, u32[]{:S(2)}) collective-permute-start(bf16[4,16,8,128]{3,2,1,0:T(8,128)(2,1)S(1)} %get-tuple-element.34), channel_id=1, source_target_pairs={{0,1},{1,0},{2,3},{3,2},{4,5},{5,4},{6,7},{7,6},{8,9},{9,8},{10,11... | collective-permute-start | bytes 393224 | tf_op jit(solution)/shard_map/ppermute | solution.py:386
  7.7 2.2 %collective-permute-done = bf16[4,16,8,128]{3,2,1,0:T(8,128)(2,1)S(1)} collective-permute-done((bf16[4,16,8,128]{3,2,1,0:T(8,128)(2,1)S(1)}, bf16[4,16,8,128]{3,2,1,0:T(8,128)(2,1)S(1)}, u32[]{:S(2)}, u32[]{:S(2)}) %collective-permute-start) | collective-permute-done | bytes 131104 | tf_op jit(solution)/shard_map/ppermute | solution.py:386
  9.9 2.2 %collective-permute-done.2 = bf16[4,16,8,128]{3,2,1,0:T(8,128)(2,1)S(1)} collective-permute-done((bf16[4,16,8,128]{3,2,1,0:T(8,128)(2,1)S(1)}, bf16[4,16,8,128]{3,2,1,0:T(8,128)(2,1)S(1)}, u32[]{:S(2)}, u32[]{:S(2)}) %collective-permute-start.2) | collective-permute-done | bytes 131104 | tf_op jit(solution)/shard_map/ppermute | solution.py:386
  12.4 3.9 %collective-permute-start.8 = (bf16[1,16,8,128]{3,2,1,0:T(8,128)(2,1)S(1)}, bf16[1,16,8,128]{3,2,1,0:T(8,128)(2,1)S(1)}, u32[]{:S(2)}, u32[]{:S(2)}) collective-permute-start(bf16[1,16,8,128]{3,2,1,0:T(8,128)(2,1)S(1)} %get-tuple-element.43), channel_id=1, source_target_pairs={{0,24},{4,28},{8,16},{12,20},{16,8},{20,12},{24,0},{28,4},{1,25},{... | collective-permute-start | bytes 98312 | tf_op jit(solution)/shard_map/ppermute | solution.py:386
  16.2 0.6 %collective-permute-start.4 = (bf16[1,16,8,128]{3,2,1,0:T(8,128)(2,1)S(1)}, bf16[1,16,8,128]{3,2,1,0:T(8,128)(2,1)S(1)}, u32[]{:S(2)}, u32[]{:S(2)}) collective-permute-start(bf16[1,16,8,128]{3,2,1,0:T(8,128)(2,1)S(1)} %get-tuple-element.45), channel_id=1, source_target_pairs={{0,8},{4,12},{8,0},{12,4},{16,24},{20,28},{24,16},{28,20},{1,9},{5... | collective-permute-start | bytes 98312 | tf_op jit(solution)/shard_map/ppermute | solution.py:386
  17.1 1.1 %collective-permute-done.8 = bf16[1,16,8,128]{3,2,1,0:T(8,128)(2,1)S(1)} collective-permute-done((bf16[1,16,8,128]{3,2,1,0:T(8,128)(2,1)S(1)}, bf16[1,16,8,128]{3,2,1,0:T(8,128)(2,1)S(1)}, u32[]{:S(2)}, u32[]{:S(2)}) %collective-permute-start.8) | collective-permute-done | bytes 32800 | tf_op jit(solution)/shard_map/ppermute | solution.py:386
  18.3 2.7 %collective-permute-done.6 = bf16[1,16,8,128]{3,2,1,0:T(8,128)(2,1)S(1)} collective-permute-done((bf16[1,16,8,128]{3,2,1,0:T(8,128)(2,1)S(1)}, bf16[1,16,8,128]{3,2,1,0:T(8,128)(2,1)S(1)}, u32[]{:S(2)}, u32[]{:S(2)}) %collective-permute-start.6) | collective-permute-done | bytes 32800 | tf_op jit(solution)/shard_map/ppermute | solution.py:386
  21.0 0.5 %collective-permute-start.5 = (bf16[1,16,8,128]{3,2,1,0:T(8,128)(2,1)S(1)}, bf16[1,16,8,128]{3,2,1,0:T(8,128)(2,1)S(1)}, u32[]{:S(2)}, u32[]{:S(2)}) collective-permute-start(bf16[1,16,8,128]{3,2,1,0:T(8,128)(2,1)S(1)} %collective-permute-done.4), channel_id=1, source_target_pairs={{0,4},{4,0},{8,12},{12,8},{16,20},{20,16},{24,28},{28,24},{1,5},{5... | collective-permute-start | bytes 98312 | tf_op jit(solution)/shard_map/ppermute | solution.py:386
  21.6 2.2 %prepare.1 = (bf16[4,432,128]{2,1,0:T(8,128)(2,1)S(1)}, f32[1,4,2,432,128]{4,3,2,1,0:T(8,128)S(1)}) custom-call(s32[128,27]{1,0:T(8,128)S(1)} %shift-left_or_fusion.words_ref, f32[343,2,512]{2,1,0:T(2,128)} %tables_any.1), custom_call_target="tpu_custom_call" | custom-call | tf_op jit(solution)/shard_map/prepare/pallas_call | solution.py:194
  23.8 0.7 %first_translate.1 = (bf16[16,8,128]{2,1,0:T(8,128)(2,1)S(1)}, bf16[8,128,128]{2,1,0:T(8,128)(2,1)S(1)}) custom-call(bf16[4,432,128]{2,1,0:T(8,128)(2,1)S(1)} %get-tuple-element.27.pick_ref, f32[1,4,2,432,128]{4,3,2,1,0:T(8,128)S(1)} %get-tuple-element.28.factor_ref, bf16[16,8,128]{2,1,0:T(8,128)(2,1)S(1)} %bitcast.14, bf16[16,8,128]{2,1,0:T(8,128)(2,1)S(1)} %bitcast.19, ...), custom_call_target="tpu_custom_call" | custom-call | tf_op jit(solution)/shard_map/first_translate/pallas_call | solution.py:283
  24.6 0.5 %translate.5 = bf16[16,8,128]{2,1,0:T(8,128)(2,1)S(1)} custom-call(bf16[4,432,128]{2,1,0:T(8,128)(2,1)S(1)} %get-tuple-element.27.pick_ref, f32[1,4,2,432,128]{4,3,2,1,0:T(8,128)S(1)} %get-tuple-element.28.factor_ref, bf16[8,128,128]{2,1,0:T(8,128)(2,1)S(1)} %get-tuple-element.35.source), custom_call_target="tpu_custom_call" | custom-call | tf_op jit(solution)/shard_map/translate/pallas_call | solution.py:302
  25.1 0.5 %translate.4 = bf16[16,8,128]{2,1,0:T(8,128)(2,1)S(1)} custom-call(bf16[4,432,128]{2,1,0:T(8,128)(2,1)S(1)} %get-tuple-element.27.pick_ref, f32[1,4,2,432,128]{4,3,2,1,0:T(8,128)S(1)} %get-tuple-element.28.factor_ref, bf16[8,128,128]{2,1,0:T(8,128)(2,1)S(1)} %get-tuple-element.35.source), custom_call_target="tpu_custom_call" | custom-call | tf_op jit(solution)/shard_map/translate/pallas_call | solution.py:302
  25.6 1.6 %collective-permute-start.11 = (bf16[1,16,8,128]{3,2,1,0:T(8,128)(2,1)S(1)}, bf16[1,16,8,128]{3,2,1,0:T(8,128)(2,1)S(1)}, u32[]{:S(2)}, u32[]{:S(2)}) collective-permute-start(bf16[1,16,8,128]{3,2,1,0:T(8,128)(2,1)S(1)} %bitcast.23), channel_id=1, source_target_pairs={{0,16},{4,20},{8,24},{12,28},{16,0},{20,4},{24,8},{28,12},{1,17},{... | collective-permute-start | bytes 98312 | tf_op jit(solution)/shard_map/ppermute | solution.py:386
  27.2 2.8 %collective-permute-start.12 = (bf16[1,16,8,128]{3,2,1,0:T(8,128)(2,1)S(1)}, bf16[1,16,8,128]{3,2,1,0:T(8,128)(2,1)S(1)}, u32[]{:S(2)}, u32[]{:S(2)}) collective-permute-start(bf16[1,16,8,128]{3,2,1,0:T(8,128)(2,1)S(1)} %bitcast.25), channel_id=1, source_target_pairs={{0,24},{4,28},{8,16},{12,20},{16,8},{20,12},{24,0},{28,4},{1,25},{... | collective-permute-start | bytes 98312 | tf_op jit(solution)/shard_map/ppermute | solution.py:386
  30.0 0.5 %translate.3 = bf16[16,8,128]{2,1,0:T(8,128)(2,1)S(1)} custom-call(bf16[4,432,128]{2,1,0:T(8,128)(2,1)S(1)} %get-tuple-element.27.pick_ref, f32[1,4,2,432,128]{4,3,2,1,0:T(8,128)S(1)} %get-tuple-element.28.factor_ref, bf16[8,128,128]{2,1,0:T(8,128)(2,1)S(1)} %get-tuple-element.35.source), custom_call_target="tpu_custom_call" | custom-call | tf_op jit(solution)/shard_map/translate/pallas_call | solution.py:302
  30.7 2.2 %collective-permute-done.12 = bf16[1,16,8,128]{3,2,1,0:T(8,128)(2,1)S(1)} collective-permute-done((bf16[1,16,8,128]{3,2,1,0:T(8,128)(2,1)S(1)}, bf16[1,16,8,128]{3,2,1,0:T(8,128)(2,1)S(1)}, u32[]{:S(2)}, u32[]{:S(2)}) %collective-permute-start.12) | collective-permute-done | bytes 32800 | tf_op jit(solution)/shard_map/ppermute | solution.py:386
  33.0 1.6 %collective-permute-start.15 = (bf16[4,16,8,128]{3,2,1,0:T(8,128)(2,1)S(1)}, bf16[4,16,8,128]{3,2,1,0:T(8,128)(2,1)S(1)}, u32[]{:S(2)}, u32[]{:S(2)}) collective-permute-start(bf16[4,16,8,128]{3,2,1,0:T(8,128)(2,1)S(1)} %pad_maximum_fusion.quarter), channel_id=1, source_target_pairs={{0,1},{1,0},{2,3},{3,2},{4,5},{5,4},{6,7},{7,6},{8,9},{9,8},{10,11... | collective-permute-start | bytes 393224 | tf_op jit(solution)/shard_map/ppermute | solution.py:386
  34.6 1.1 %collective-permute-start.14 = (bf16[4,16,8,128]{3,2,1,0:T(8,128)(2,1)S(1)}, bf16[4,16,8,128]{3,2,1,0:T(8,128)(2,1)S(1)}, u32[]{:S(2)}, u32[]{:S(2)}) collective-permute-start(bf16[4,16,8,128]{3,2,1,0:T(8,128)(2,1)S(1)} %pad_maximum_fusion.quarter), channel_id=1, source_target_pairs={{0,2},{1,3},{2,0},{3,1},{4,6},{5,7},{6,4},{7,5},{8,10},{9,11},{10,... | collective-permute-start | bytes 393224 | tf_op jit(solution)/shard_map/ppermute | solution.py:386
  35.6 0.9 %collective-permute-start.13 = (bf16[4,16,8,128]{3,2,1,0:T(8,128)(2,1)S(1)}, bf16[4,16,8,128]{3,2,1,0:T(8,128)(2,1)S(1)}, u32[]{:S(2)}, u32[]{:S(2)}) collective-permute-start(bf16[4,16,8,128]{3,2,1,0:T(8,128)(2,1)S(1)} %pad_maximum_fusion.quarter), channel_id=1, source_target_pairs={{0,3},{1,2},{2,1},{3,0},{4,7},{5,6},{6,5},{7,4},{8,11},{9,10},{10,... | collective-permute-start | bytes 393224 | tf_op jit(solution)/shard_map/ppermute | solution.py:386
  37.0 1.8 %collective-permute-done.15.quarter = bf16[4,16,8,128]{3,2,1,0:T(8,128)(2,1)S(1)} collective-permute-done((bf16[4,16,8,128]{3,2,1,0:T(8,128)(2,1)S(1)}, bf16[4,16,8,128]{3,2,1,0:T(8,128)(2,1)S(1)}, u32[]{:S(2)}, u32[]{:S(2)}) %collective-permute-start.15) | collective-permute-done | bytes 131104 | tf_op jit(solution)/shard_map/ppermute | solution.py:386
  39.3 2.9 %collective-permute-done.14.quarter = bf16[4,16,8,128]{3,2,1,0:T(8,128)(2,1)S(1)} collective-permute-done((bf16[4,16,8,128]{3,2,1,0:T(8,128)(2,1)S(1)}, bf16[4,16,8,128]{3,2,1,0:T(8,128)(2,1)S(1)}, u32[]{:S(2)}, u32[]{:S(2)}) %collective-permute-start.14) | collective-permute-done | bytes 131104 | tf_op jit(solution)/shard_map/ppermute | solution.py:386
  42.6 1.2 %backward.7 = bf16[1024,128]{1,0:T(8,128)(2,1)} custom-call(bf16[128,2048]{1,0:T(8,128)(2,1)S(1)} %get-tuple-element.24.interp_ref, f32[8,512]{1,0:T(8,128)S(1)} %get-tuple-element.25.cos_ref, f32[8,512]{1,0:T(8,128)S(1)} %get-tuple-element.26.sin_ref, bf16[4,16,8,128]{3,2,1,0:T(8,128)(2,1)S(1)} %collective-permute-done.13.quarter, ...), custom_call_target="tpu_custom_call" | custom-call | tf_op jit(solution)/shard_map/backward/pallas_call | solution.py:369
  (31 shorter events, 3.7 us)
Async XLA Ops:
  1.6 8.3 %collective-permute-start = (bf16[4,16,8,128]{3,2,1,0:T(8,128)(2,1)S(1)}, bf16[4,16,8,128]{3,2,1,0:T(8,128)(2,1)S(1)}, u32[]{:S(2)}, u32[]{:S(2)}) collective-permute-start(bf16[4,16,8,128]{3,2,1,0:T(8,128)(2,1)S(1)} %get-tuple-element.32), channel_id=1, source_target_pairs={{0,3},{1,2},{2,1},{3,0},{4,7},{5,6},{6,5},{7,4},{8,11},{9,10},{10,... | collective-permute-start | bytes 393224 | tf_op jit(solution)/shard_map/ppermute | solution.py:386
  5.5 11.3 %copy-start = (s32[128,27]{0,1:T(8,128)S(1)}, s32[128,27]{0,1:T(8,128)}, u32[]{:S(2)}) copy-start(s32[128,27]{0,1:T(8,128)} %param.10) | copy-start | bytes 41476
  5.5 11.4 %copy-start.1 = (s32[128,27]{0,1:T(8,128)S(1)}, s32[128,27]{0,1:T(8,128)}, u32[]{:S(2)}) copy-start(s32[128,27]{0,1:T(8,128)} %param.11) | copy-start | bytes 41476
  6.0 6.1 %collective-permute-start.2 = (bf16[4,16,8,128]{3,2,1,0:T(8,128)(2,1)S(1)}, bf16[4,16,8,128]{3,2,1,0:T(8,128)(2,1)S(1)}, u32[]{:S(2)}, u32[]{:S(2)}) collective-permute-start(bf16[4,16,8,128]{3,2,1,0:T(8,128)(2,1)S(1)} %get-tuple-element.34), channel_id=1, source_target_pairs={{0,1},{1,0},{2,3},{3,2},{4,5},{5,4},{6,7},{7,6},{8,9},{9,8},{10,11... | collective-permute-start | bytes 393224 | tf_op jit(solution)/shard_map/ppermute | solution.py:386
  7.1 5.2 %collective-permute-start.1 = (bf16[4,16,8,128]{3,2,1,0:T(8,128)(2,1)S(1)}, bf16[4,16,8,128]{3,2,1,0:T(8,128)(2,1)S(1)}, u32[]{:S(2)}, u32[]{:S(2)}) collective-permute-start(bf16[4,16,8,128]{3,2,1,0:T(8,128)(2,1)S(1)} %get-tuple-element.33), channel_id=1, source_target_pairs={{0,2},{1,3},{2,0},{3,1},{4,6},{5,7},{6,4},{7,5},{8,10},{9,11},{10,... | collective-permute-start | bytes 393224 | tf_op jit(solution)/shard_map/ppermute | solution.py:386
  12.4 5.9 %collective-permute-start.8 = (bf16[1,16,8,128]{3,2,1,0:T(8,128)(2,1)S(1)}, bf16[1,16,8,128]{3,2,1,0:T(8,128)(2,1)S(1)}, u32[]{:S(2)}, u32[]{:S(2)}) collective-permute-start(bf16[1,16,8,128]{3,2,1,0:T(8,128)(2,1)S(1)} %get-tuple-element.43), channel_id=1, source_target_pairs={{0,24},{4,28},{8,16},{12,20},{16,8},{20,12},{24,0},{28,4},{1,25},{... | collective-permute-start | bytes 98312 | tf_op jit(solution)/shard_map/ppermute | solution.py:386
  16.2 4.8 %collective-permute-start.6 = (bf16[1,16,8,128]{3,2,1,0:T(8,128)(2,1)S(1)}, bf16[1,16,8,128]{3,2,1,0:T(8,128)(2,1)S(1)}, u32[]{:S(2)}, u32[]{:S(2)}) collective-permute-start(bf16[1,16,8,128]{3,2,1,0:T(8,128)(2,1)S(1)} %get-tuple-element.44), channel_id=1, source_target_pairs={{0,16},{4,20},{8,24},{12,28},{16,0},{20,4},{24,8},{28,12},{1,17},{... | collective-permute-start | bytes 98312 | tf_op jit(solution)/shard_map/ppermute | solution.py:386
  16.2 4.8 %collective-permute-start.4 = (bf16[1,16,8,128]{3,2,1,0:T(8,128)(2,1)S(1)}, bf16[1,16,8,128]{3,2,1,0:T(8,128)(2,1)S(1)}, u32[]{:S(2)}, u32[]{:S(2)}) collective-permute-start(bf16[1,16,8,128]{3,2,1,0:T(8,128)(2,1)S(1)} %get-tuple-element.45), channel_id=1, source_target_pairs={{0,8},{4,12},{8,0},{12,4},{16,24},{20,28},{24,16},{28,20},{1,9},{5... | collective-permute-start | bytes 98312 | tf_op jit(solution)/shard_map/ppermute | solution.py:386
  17.1 6.7 %collective-permute-start.3 = (bf16[1,16,8,128]{3,2,1,0:T(8,128)(2,1)S(1)}, bf16[1,16,8,128]{3,2,1,0:T(8,128)(2,1)S(1)}, u32[]{:S(2)}, u32[]{:S(2)}) collective-permute-start(bf16[1,16,8,128]{3,2,1,0:T(8,128)(2,1)S(1)} %get-tuple-element.46), channel_id=1, source_target_pairs={{0,4},{4,0},{8,12},{12,8},{16,20},{20,16},{24,28},{28,24},{1,5},{5... | collective-permute-start | bytes 98312 | tf_op jit(solution)/shard_map/ppermute | solution.py:386
  18.3 5.5 %collective-permute-start.9 = (bf16[1,16,8,128]{3,2,1,0:T(8,128)(2,1)S(1)}, bf16[1,16,8,128]{3,2,1,0:T(8,128)(2,1)S(1)}, u32[]{:S(2)}, u32[]{:S(2)}) collective-permute-start(bf16[1,16,8,128]{3,2,1,0:T(8,128)(2,1)S(1)} %collective-permute-done.8), channel_id=1, source_target_pairs={{0,4},{4,0},{8,12},{12,8},{16,20},{20,16},{24,28},{28,24},{1,5},{5... | collective-permute-start | bytes 98312 | tf_op jit(solution)/shard_map/ppermute | solution.py:386
  21.0 2.8 %collective-permute-start.7 = (bf16[1,16,8,128]{3,2,1,0:T(8,128)(2,1)S(1)}, bf16[1,16,8,128]{3,2,1,0:T(8,128)(2,1)S(1)}, u32[]{:S(2)}, u32[]{:S(2)}) collective-permute-start(bf16[1,16,8,128]{3,2,1,0:T(8,128)(2,1)S(1)} %collective-permute-done.6), channel_id=1, source_target_pairs={{0,4},{4,0},{8,12},{12,8},{16,20},{20,16},{24,28},{28,24},{1,5},{5... | collective-permute-start | bytes 98312 | tf_op jit(solution)/shard_map/ppermute | solution.py:386
  21.0 2.8 %collective-permute-start.5 = (bf16[1,16,8,128]{3,2,1,0:T(8,128)(2,1)S(1)}, bf16[1,16,8,128]{3,2,1,0:T(8,128)(2,1)S(1)}, u32[]{:S(2)}, u32[]{:S(2)}) collective-permute-start(bf16[1,16,8,128]{3,2,1,0:T(8,128)(2,1)S(1)} %collective-permute-done.4), channel_id=1, source_target_pairs={{0,4},{4,0},{8,12},{12,8},{16,20},{20,16},{24,28},{28,24},{1,5},{5... | collective-permute-start | bytes 98312 | tf_op jit(solution)/shard_map/ppermute | solution.py:386
  25.6 4.9 %collective-permute-start.10 = (bf16[1,16,8,128]{3,2,1,0:T(8,128)(2,1)S(1)}, bf16[1,16,8,128]{3,2,1,0:T(8,128)(2,1)S(1)}, u32[]{:S(2)}, u32[]{:S(2)}) collective-permute-start(bf16[1,16,8,128]{3,2,1,0:T(8,128)(2,1)S(1)} %bitcast.24), channel_id=1, source_target_pairs={{0,8},{4,12},{8,0},{12,4},{16,24},{20,28},{24,16},{28,20},{1,9},{5... | collective-permute-start | bytes 98312 | tf_op jit(solution)/shard_map/ppermute | solution.py:386
  25.6 5.1 %collective-permute-start.11 = (bf16[1,16,8,128]{3,2,1,0:T(8,128)(2,1)S(1)}, bf16[1,16,8,128]{3,2,1,0:T(8,128)(2,1)S(1)}, u32[]{:S(2)}, u32[]{:S(2)}) collective-permute-start(bf16[1,16,8,128]{3,2,1,0:T(8,128)(2,1)S(1)} %bitcast.23), channel_id=1, source_target_pairs={{0,16},{4,20},{8,24},{12,28},{16,0},{20,4},{24,8},{28,12},{1,17},{... | collective-permute-start | bytes 98312 | tf_op jit(solution)/shard_map/ppermute | solution.py:386
  27.2 5.7 %collective-permute-start.12 = (bf16[1,16,8,128]{3,2,1,0:T(8,128)(2,1)S(1)}, bf16[1,16,8,128]{3,2,1,0:T(8,128)(2,1)S(1)}, u32[]{:S(2)}, u32[]{:S(2)}) collective-permute-start(bf16[1,16,8,128]{3,2,1,0:T(8,128)(2,1)S(1)} %bitcast.25), channel_id=1, source_target_pairs={{0,24},{4,28},{8,16},{12,20},{16,8},{20,12},{24,0},{28,4},{1,25},{... | collective-permute-start | bytes 98312 | tf_op jit(solution)/shard_map/ppermute | solution.py:386
  33.0 5.8 %collective-permute-start.15 = (bf16[4,16,8,128]{3,2,1,0:T(8,128)(2,1)S(1)}, bf16[4,16,8,128]{3,2,1,0:T(8,128)(2,1)S(1)}, u32[]{:S(2)}, u32[]{:S(2)}) collective-permute-start(bf16[4,16,8,128]{3,2,1,0:T(8,128)(2,1)S(1)} %pad_maximum_fusion.quarter), channel_id=1, source_target_pairs={{0,1},{1,0},{2,3},{3,2},{4,5},{5,4},{6,7},{7,6},{8,9},{9,8},{10,11... | collective-permute-start | bytes 393224 | tf_op jit(solution)/shard_map/ppermute | solution.py:386
  34.6 7.6 %collective-permute-start.14 = (bf16[4,16,8,128]{3,2,1,0:T(8,128)(2,1)S(1)}, bf16[4,16,8,128]{3,2,1,0:T(8,128)(2,1)S(1)}, u32[]{:S(2)}, u32[]{:S(2)}) collective-permute-start(bf16[4,16,8,128]{3,2,1,0:T(8,128)(2,1)S(1)} %pad_maximum_fusion.quarter), channel_id=1, source_target_pairs={{0,2},{1,3},{2,0},{3,1},{4,6},{5,7},{6,4},{7,5},{8,10},{9,11},{10,... | collective-permute-start | bytes 393224 | tf_op jit(solution)/shard_map/ppermute | solution.py:386
  35.6 7.0 %collective-permute-start.13 = (bf16[4,16,8,128]{3,2,1,0:T(8,128)(2,1)S(1)}, bf16[4,16,8,128]{3,2,1,0:T(8,128)(2,1)S(1)}, u32[]{:S(2)}, u32[]{:S(2)}) collective-permute-start(bf16[4,16,8,128]{3,2,1,0:T(8,128)(2,1)S(1)} %pad_maximum_fusion.quarter), channel_id=1, source_target_pairs={{0,3},{1,2},{2,1},{3,0},{4,7},{5,6},{6,5},{7,4},{8,11},{9,10},{10,... | collective-permute-start | bytes 393224 | tf_op jit(solution)/shard_map/ppermute | solution.py:386

commit v5 on v4

--- a/solution.py
+++ b/solution.py
@@ -19,6 +19,10 @@
 SMEM = pl.BlockSpec(memory_space=pltpu.SMEM)
 FAR = pl.BlockSpec(memory_space=pltpu.HBM)
 GRANT = pltpu.CompilerParams(vmem_limit_bytes=12 << 20)
+
+
+def side(rest, s):
+    return 1 if s and rest == 2 else 0
 
 
 def places(rest):
@@ -167,7 +171,8 @@
         loads.append(load)
     chosen = []
     for s in range(zc):
-        first = pl.multiple_of(((zi ^ s) * rest + ci) * par_cnt, par_cnt)
+        first = ((zi ^ s) * rest + ci) * par_cnt
+        first = pl.multiple_of(first, par_cnt)
         words = words_ref[pl.ds(first, par_cnt), :]
         which, offset = words & 0xFFFF, lax.shift_right_logical(words, 16)
         rows = []
@@ -249,7 +254,7 @@
     swap = swap_rows(par_cnt, cols)
     for s in range(zc):
         for t in range(each):
-            box = (zi ^ s) * rest + ((ci ^ t) if each > 1 else 0)
+            box = (zi ^ s) * rest + ((ci ^ t ^ side(rest, s)) if each > 1 else 0)
             piece = pieces[s * each + t]
 
             def place(k, carry, box=box, piece=piece):
@@ -395,7 +400,7 @@
     wide = chunks // zc
     zi = lax.axis_index("box") // rest
     x = child_out.reshape(child_cnt * cols, kq)
-    masks = tuple(range(ndir - 1, 0, -1))
+    masks = down_order(ndir)
 
     part, *turns, x, mine, angle = first_forward(
         masks[0], chunks, cols, far(x), far(interp), far(shift_angle)
@@ -415,7 +420,7 @@
     pieces = []
     for s in range(zc):
         piece = lax.dynamic_index_in_dim(own, zi ^ s, 0, keepdims=False)
-        pieces.append(exchange(piece, "box", s * rest) if s else piece)
+        pieces.append(exchange(piece, "box", s * rest + side(rest, s)) if s else piece)
     if rest == 2:
         pieces = [part for piece in pieces for part in (piece, exchange(piece, "box", 1))]
     else:
@@ -436,10 +441,11 @@
         quarter.append(exchange(result, "box", s * rest) if s else result)
     quarter = jnp.concatenate(quarter, 0)
 
-    received = [exchange(quarter, "dir", mask) for mask in range(1, ndir)]
+    down = down_order(ndir)
+    received = [exchange(quarter, "dir", mask) for mask in down]
     out = backward(0, wide, rest, ndir == 1, mine, tables[0], quarter, None)
-    for mask, quarter in zip(range(1, ndir), received):
-        out = backward(mask, wide, rest, mask == ndir - 1, mine, tables[mask], quarter, out)
+    for mask, quarter in zip(down, received):
+        out = backward(mask, wide, rest, mask == down[-1], mine, tables[mask], quarter, out)
     return out.reshape(child_cnt, cols, kq)
 
 
@@ -451,7 +457,11 @@
 
 
 def home_order(zc):
-    return ((zc - 1,) + tuple(range(1, zc - 1)) if zc > 1 else ()) + (0,)
+    return tuple(range(zc - 1, 0, -1)) + (0,)
+
+
+def down_order(ndir):
+    return (ndir - 1,) + tuple(range(1, ndir - 1))
 
 
 def solution(mesh):

time: 44 us -> 42.1 us (0.957)
  waiting for transfers between devices: 15.5 us -> 12.3 us
  starting transfers between devices: 17.7 us -> 19.1 us
    ppermute x16, waiting for transfers between devices: 15.5 us -> 12.3 us  [exchange(): return lax.ppermute(value, axis, [(i, i ^ mask) for i in range(size)])]
    ppermute x16, starting transfers between devices: 17.7 us -> 19.1 us  [exchange(): return lax.ppermute(value, axis, [(i, i ^ mask) for i in range(size)])]
  transfers between devices with their start and end apart: 16 -> 16, of which waited for: 9 -> 8; matrix products, arithmetic and copies ran while one was open for 1% -> 1% of each run, Pallas kernels for 13% -> 13%
where the time goes in v5:
time: 42.1 us; the launch traced here: 41.9 us
  starting transfers between devices  19.1 us (45%)
  waiting for transfers between devices  12.3 us (29%)
  Pallas kernels  10 us (24%)
    ppermute x16, starting transfers between devices, exchange(): return lax.ppermute(value, axis, [(i, i ^ mask) for i in range(size)])  19.1 us
    ppermute x16, waiting for transfers between devices, exchange(): return lax.ppermute(value, axis, [(i, i ^ mask) for i in range(size)])  12.3 us
    pallas_call x4, Pallas kernels, backward(): pl.pallas_call(functools.partial(backward_kernel, mask, wide, rest, last)...  2.6 us
    pallas_call x1, Pallas kernels, prepare(): pl.pallas_call(functools.partial(prepare_kernel, zc, rest, wide), out_sha...  2.24 us
    pallas_call x3, Pallas kernels, translate(): result = call(picks, factors, source)  1.55 us
    pallas_call x1, Pallas kernels, first_forward(): pl.pallas_call(functools.partial(first_kernel, mask), out_shape=quarter_s...  1.54 us
    pallas_call x3, Pallas kernels, forward(): pl.pallas_call(functools.partial(forward_kernel, mask), out_shape=quarter...  1.37 us
  transfers between devices with their start and end apart: 16, of which 8 were waited for; matrix products, arithmetic and copies ran while one was open for 1% of the time, Pallas kernels for 13%

profile of v5, /device:TPU:0, one launch (start us, length us, event | category | flops | bytes accessed | tf_op | source)
XLA Modules:
  0.0 41.9 jit_solution(3188144147955288473)
XLA Ops:
  0.0 1.5 %first_forward.1 = (bf16[4,16,8,128]{3,2,1,0:T(8,128)(2,1)S(1)}, f32[8,512]{1,0:T(8,128)S(1)}, f32[8,512]{1,0:T(8,128)S(1)}, bf16[1024,128]{1,0:T(8,128)(2,1)S(1...) custom-call(bf16[1024,128]{1,0:T(8,128)(2,1)} %bitcast.26, bf16[512,2048]{1,0:T(8,128)(2,1)} %interp_any.1, ...), custom_call_target="tpu_custom_call" | custom-call | tf_op jit(solution)/shard_map/first_forward/pallas_call | solution.py:118
  1.6 4.0 %collective-permute-start = (bf16[4,16,8,128]{3,2,1,0:T(8,128)(2,1)S(1)}, bf16[4,16,8,128]{3,2,1,0:T(8,128)(2,1)S(1)}, u32[]{:S(2)}, u32[]{:S(2)}) collective-permute-start(bf16[4,16,8,128]{3,2,1,0:T(8,128)(2,1)S(1)} %get-tuple-element.32), channel_id=1, source_target_pairs={{0,3},{1,2},{2,1},{3,0},{4,7},{5,6},{6,5},{7,4},{8,11},{9,10},{10,... | collective-permute-start | bytes 393224 | tf_op jit(solution)/shard_map/ppermute | solution.py:391
  6.0 0.6 %collective-permute-start.1 = (bf16[4,16,8,128]{3,2,1,0:T(8,128)(2,1)S(1)}, bf16[4,16,8,128]{3,2,1,0:T(8,128)(2,1)S(1)}, u32[]{:S(2)}, u32[]{:S(2)}) collective-permute-start(bf16[4,16,8,128]{3,2,1,0:T(8,128)(2,1)S(1)} %get-tuple-element.33), channel_id=1, source_target_pairs={{0,1},{1,0},{2,3},{3,2},{4,5},{5,4},{6,7},{7,6},{8,9},{9,8},{10,11... | collective-permute-start | bytes 393224 | tf_op jit(solution)/shard_map/ppermute | solution.py:391
  7.7 2.2 %collective-permute-done = bf16[4,16,8,128]{3,2,1,0:T(8,128)(2,1)S(1)} collective-permute-done((bf16[4,16,8,128]{3,2,1,0:T(8,128)(2,1)S(1)}, bf16[4,16,8,128]{3,2,1,0:T(8,128)(2,1)S(1)}, u32[]{:S(2)}, u32[]{:S(2)}) %collective-permute-start) | collective-permute-done | bytes 131104 | tf_op jit(solution)/shard_map/ppermute | solution.py:391
  9.9 2.2 %collective-permute-done.1 = bf16[4,16,8,128]{3,2,1,0:T(8,128)(2,1)S(1)} collective-permute-done((bf16[4,16,8,128]{3,2,1,0:T(8,128)(2,1)S(1)}, bf16[4,16,8,128]{3,2,1,0:T(8,128)(2,1)S(1)}, u32[]{:S(2)}, u32[]{:S(2)}) %collective-permute-start.1) | collective-permute-done | bytes 131104 | tf_op jit(solution)/shard_map/ppermute | solution.py:391
  12.4 2.5 %collective-permute-start.8 = (bf16[1,16,8,128]{3,2,1,0:T(8,128)(2,1)S(1)}, bf16[1,16,8,128]{3,2,1,0:T(8,128)(2,1)S(1)}, u32[]{:S(2)}, u32[]{:S(2)}) collective-permute-start(bf16[1,16,8,128]{3,2,1,0:T(8,128)(2,1)S(1)} %get-tuple-element.43), channel_id=1, source_target_pairs={{0,28},{4,24},{8,20},{12,16},{16,12},{20,8},{24,4},{28,0},{1,29},{... | collective-permute-start | bytes 98312 | tf_op jit(solution)/shard_map/ppermute | solution.py:391
  14.9 0.5 %collective-permute-start.6 = (bf16[1,16,8,128]{3,2,1,0:T(8,128)(2,1)S(1)}, bf16[1,16,8,128]{3,2,1,0:T(8,128)(2,1)S(1)}, u32[]{:S(2)}, u32[]{:S(2)}) collective-permute-start(bf16[1,16,8,128]{3,2,1,0:T(8,128)(2,1)S(1)} %get-tuple-element.44), channel_id=1, source_target_pairs={{0,20},{4,16},{8,28},{12,24},{16,4},{20,0},{24,12},{28,8},{1,21},{... | collective-permute-start | bytes 98312 | tf_op jit(solution)/shard_map/ppermute | solution.py:391
  15.4 1.2 %collective-permute-start.4 = (bf16[1,16,8,128]{3,2,1,0:T(8,128)(2,1)S(1)}, bf16[1,16,8,128]{3,2,1,0:T(8,128)(2,1)S(1)}, u32[]{:S(2)}, u32[]{:S(2)}) collective-permute-start(bf16[1,16,8,128]{3,2,1,0:T(8,128)(2,1)S(1)} %get-tuple-element.45), channel_id=1, source_target_pairs={{0,12},{4,8},{8,4},{12,0},{16,28},{20,24},{24,20},{28,16},{1,13},{... | collective-permute-start | bytes 98312 | tf_op jit(solution)/shard_map/ppermute | solution.py:391
  16.9 0.7 %collective-permute-done.8 = bf16[1,16,8,128]{3,2,1,0:T(8,128)(2,1)S(1)} collective-permute-done((bf16[1,16,8,128]{3,2,1,0:T(8,128)(2,1)S(1)}, bf16[1,16,8,128]{3,2,1,0:T(8,128)(2,1)S(1)}, u32[]{:S(2)}, u32[]{:S(2)}) %collective-permute-start.8) | collective-permute-done | bytes 32800 | tf_op jit(solution)/shard_map/ppermute | solution.py:391
  17.7 0.6 %collective-permute-start.9 = (bf16[1,16,8,128]{3,2,1,0:T(8,128)(2,1)S(1)}, bf16[1,16,8,128]{3,2,1,0:T(8,128)(2,1)S(1)}, u32[]{:S(2)}, u32[]{:S(2)}) collective-permute-start(bf16[1,16,8,128]{3,2,1,0:T(8,128)(2,1)S(1)} %collective-permute-done.8), channel_id=1, source_target_pairs={{0,4},{4,0},{8,12},{12,8},{16,20},{20,16},{24,28},{28,24},{1,5},{5... | collective-permute-start | bytes 98312 | tf_op jit(solution)/shard_map/ppermute | solution.py:391
  18.3 0.8 %collective-permute-done.6 = bf16[1,16,8,128]{3,2,1,0:T(8,128)(2,1)S(1)} collective-permute-done((bf16[1,16,8,128]{3,2,1,0:T(8,128)(2,1)S(1)}, bf16[1,16,8,128]{3,2,1,0:T(8,128)(2,1)S(1)}, u32[]{:S(2)}, u32[]{:S(2)}) %collective-permute-start.6) | collective-permute-done | bytes 32800 | tf_op jit(solution)/shard_map/ppermute | solution.py:391
  19.1 1.4 %collective-permute-start.7 = (bf16[1,16,8,128]{3,2,1,0:T(8,128)(2,1)S(1)}, bf16[1,16,8,128]{3,2,1,0:T(8,128)(2,1)S(1)}, u32[]{:S(2)}, u32[]{:S(2)}) collective-permute-start(bf16[1,16,8,128]{3,2,1,0:T(8,128)(2,1)S(1)} %collective-permute-done.6), channel_id=1, source_target_pairs={{0,4},{4,0},{8,12},{12,8},{16,20},{20,16},{24,28},{28,24},{1,5},{5... | collective-permute-start | bytes 98312 | tf_op jit(solution)/shard_map/ppermute | solution.py:391
  20.6 2.2 %prepare.1 = (bf16[4,432,128]{2,1,0:T(8,128)(2,1)S(1)}, f32[1,4,2,432,128]{4,3,2,1,0:T(8,128)S(1)}) custom-call(s32[128,27]{1,0:T(8,128)S(1)} %shift-left_or_fusion.words_ref, f32[343,2,512]{2,1,0:T(2,128)} %tables_any.1), custom_call_target="tpu_custom_call" | custom-call | tf_op jit(solution)/shard_map/prepare/pallas_call | solution.py:199
  22.9 0.7 %first_translate.1 = (bf16[16,8,128]{2,1,0:T(8,128)(2,1)S(1)}, bf16[8,128,128]{2,1,0:T(8,128)(2,1)S(1)}) custom-call(bf16[4,432,128]{2,1,0:T(8,128)(2,1)S(1)} %get-tuple-element.29.pick_ref, f32[1,4,2,432,128]{4,3,2,1,0:T(8,128)S(1)} %get-tuple-element.30.factor_ref, bf16[16,8,128]{2,1,0:T(8,128)(2,1)S(1)} %bitcast.14, bf16[16,8,128]{2,1,0:T(8,128)(2,1)S(1)} %bitcast.19, ...), custom_call_target="tpu_custom_call" | custom-call | tf_op jit(solution)/shard_map/first_translate/pallas_call | solution.py:288
  23.6 0.5 %translate.5 = bf16[16,8,128]{2,1,0:T(8,128)(2,1)S(1)} custom-call(bf16[4,432,128]{2,1,0:T(8,128)(2,1)S(1)} %get-tuple-element.29.pick_ref, f32[1,4,2,432,128]{4,3,2,1,0:T(8,128)S(1)} %get-tuple-element.30.factor_ref, bf16[8,128,128]{2,1,0:T(8,128)(2,1)S(1)} %get-tuple-element.35.source), custom_call_target="tpu_custom_call" | custom-call | tf_op jit(solution)/shard_map/translate/pallas_call | solution.py:307
  24.1 0.5 %translate.4 = bf16[16,8,128]{2,1,0:T(8,128)(2,1)S(1)} custom-call(bf16[4,432,128]{2,1,0:T(8,128)(2,1)S(1)} %get-tuple-element.29.pick_ref, f32[1,4,2,432,128]{4,3,2,1,0:T(8,128)S(1)} %get-tuple-element.30.factor_ref, bf16[8,128,128]{2,1,0:T(8,128)(2,1)S(1)} %get-tuple-element.35.source), custom_call_target="tpu_custom_call" | custom-call | tf_op jit(solution)/shard_map/translate/pallas_call | solution.py:307
  24.8 2.6 %collective-permute-start.11 = (bf16[1,16,8,128]{3,2,1,0:T(8,128)(2,1)S(1)}, bf16[1,16,8,128]{3,2,1,0:T(8,128)(2,1)S(1)}, u32[]{:S(2)}, u32[]{:S(2)}) collective-permute-start(bf16[1,16,8,128]{3,2,1,0:T(8,128)(2,1)S(1)} %bitcast.23), channel_id=1, source_target_pairs={{0,16},{4,20},{8,24},{12,28},{16,0},{20,4},{24,8},{28,12},{1,17},{... | collective-permute-start | bytes 98312 | tf_op jit(solution)/shard_map/ppermute | solution.py:391
  27.3 1.7 %collective-permute-start.12 = (bf16[1,16,8,128]{3,2,1,0:T(8,128)(2,1)S(1)}, bf16[1,16,8,128]{3,2,1,0:T(8,128)(2,1)S(1)}, u32[]{:S(2)}, u32[]{:S(2)}) collective-permute-start(bf16[1,16,8,128]{3,2,1,0:T(8,128)(2,1)S(1)} %bitcast.25), channel_id=1, source_target_pairs={{0,24},{4,28},{8,16},{12,20},{16,8},{20,12},{24,0},{28,4},{1,25},{... | collective-permute-start | bytes 98312 | tf_op jit(solution)/shard_map/ppermute | solution.py:391
  29.0 0.5 %translate.3 = bf16[16,8,128]{2,1,0:T(8,128)(2,1)S(1)} custom-call(bf16[4,432,128]{2,1,0:T(8,128)(2,1)S(1)} %get-tuple-element.29.pick_ref, f32[1,4,2,432,128]{4,3,2,1,0:T(8,128)S(1)} %get-tuple-element.30.factor_ref, bf16[8,128,128]{2,1,0:T(8,128)(2,1)S(1)} %get-tuple-element.35.source), custom_call_target="tpu_custom_call" | custom-call | tf_op jit(solution)/shard_map/translate/pallas_call | solution.py:307
  29.6 3.5 %collective-permute-done.12 = bf16[1,16,8,128]{3,2,1,0:T(8,128)(2,1)S(1)} collective-permute-done((bf16[1,16,8,128]{3,2,1,0:T(8,128)(2,1)S(1)}, bf16[1,16,8,128]{3,2,1,0:T(8,128)(2,1)S(1)}, u32[]{:S(2)}, u32[]{:S(2)}) %collective-permute-start.12) | collective-permute-done | bytes 32800 | tf_op jit(solution)/shard_map/ppermute | solution.py:391
  33.1 1.8 %collective-permute-start.15 = (bf16[4,16,8,128]{3,2,1,0:T(8,128)(2,1)S(1)}, bf16[4,16,8,128]{3,2,1,0:T(8,128)(2,1)S(1)}, u32[]{:S(2)}, u32[]{:S(2)}) collective-permute-start(bf16[4,16,8,128]{3,2,1,0:T(8,128)(2,1)S(1)} %pad_maximum_fusion.quarter), channel_id=1, source_target_pairs={{0,3},{1,2},{2,1},{3,0},{4,7},{5,6},{6,5},{7,4},{8,11},{9,10},{10,... | collective-permute-start | bytes 393224 | tf_op jit(solution)/shard_map/ppermute | solution.py:391
  35.3 1.3 %collective-permute-start.13 = (bf16[4,16,8,128]{3,2,1,0:T(8,128)(2,1)S(1)}, bf16[4,16,8,128]{3,2,1,0:T(8,128)(2,1)S(1)}, u32[]{:S(2)}, u32[]{:S(2)}) collective-permute-start(bf16[4,16,8,128]{3,2,1,0:T(8,128)(2,1)S(1)} %pad_maximum_fusion.quarter), channel_id=1, source_target_pairs={{0,2},{1,3},{2,0},{3,1},{4,6},{5,7},{6,4},{7,5},{8,10},{9,11},{10,... | collective-permute-start | bytes 393224 | tf_op jit(solution)/shard_map/ppermute | solution.py:391
  37.1 2.2 %collective-permute-done.15.quarter = bf16[4,16,8,128]{3,2,1,0:T(8,128)(2,1)S(1)} collective-permute-done((bf16[4,16,8,128]{3,2,1,0:T(8,128)(2,1)S(1)}, bf16[4,16,8,128]{3,2,1,0:T(8,128)(2,1)S(1)}, u32[]{:S(2)}, u32[]{:S(2)}) %collective-permute-start.15) | collective-permute-done | bytes 131104 | tf_op jit(solution)/shard_map/ppermute | solution.py:391
  40.7 1.2 %backward.7 = bf16[1024,128]{1,0:T(8,128)(2,1)} custom-call(bf16[128,2048]{1,0:T(8,128)(2,1)S(1)} %get-tuple-element.24.interp_ref, f32[8,512]{1,0:T(8,128)S(1)} %get-tuple-element.27.cos_ref, f32[8,512]{1,0:T(8,128)S(1)} %get-tuple-element.28.sin_ref, bf16[4,16,8,128]{3,2,1,0:T(8,128)(2,1)S(1)} %collective-permute-done.13.quarter, ...), custom_call_target="tpu_custom_call" | custom-call | tf_op jit(solution)/shard_map/backward/pallas_call | solution.py:374
  (31 shorter events, 4.6 us)
Async XLA Ops:
  1.6 8.3 %collective-permute-start = (bf16[4,16,8,128]{3,2,1,0:T(8,128)(2,1)S(1)}, bf16[4,16,8,128]{3,2,1,0:T(8,128)(2,1)S(1)}, u32[]{:S(2)}, u32[]{:S(2)}) collective-permute-start(bf16[4,16,8,128]{3,2,1,0:T(8,128)(2,1)S(1)} %get-tuple-element.32), channel_id=1, source_target_pairs={{0,3},{1,2},{2,1},{3,0},{4,7},{5,6},{6,5},{7,4},{8,11},{9,10},{10,... | collective-permute-start | bytes 393224 | tf_op jit(solution)/shard_map/ppermute | solution.py:391
  5.5 11.0 %copy-start = (s32[128,27]{0,1:T(8,128)S(1)}, s32[128,27]{0,1:T(8,128)}, u32[]{:S(2)}) copy-start(s32[128,27]{0,1:T(8,128)} %param.10) | copy-start | bytes 41476
  5.5 11.2 %copy-start.1 = (s32[128,27]{0,1:T(8,128)S(1)}, s32[128,27]{0,1:T(8,128)}, u32[]{:S(2)}) copy-start(s32[128,27]{0,1:T(8,128)} %param.11) | copy-start | bytes 41476
  6.0 6.1 %collective-permute-start.1 = (bf16[4,16,8,128]{3,2,1,0:T(8,128)(2,1)S(1)}, bf16[4,16,8,128]{3,2,1,0:T(8,128)(2,1)S(1)}, u32[]{:S(2)}, u32[]{:S(2)}) collective-permute-start(bf16[4,16,8,128]{3,2,1,0:T(8,128)(2,1)S(1)} %get-tuple-element.33), channel_id=1, source_target_pairs={{0,1},{1,0},{2,3},{3,2},{4,5},{5,4},{6,7},{7,6},{8,9},{9,8},{10,11... | collective-permute-start | bytes 393224 | tf_op jit(solution)/shard_map/ppermute | solution.py:391
  7.1 5.2 %collective-permute-start.2 = (bf16[4,16,8,128]{3,2,1,0:T(8,128)(2,1)S(1)}, bf16[4,16,8,128]{3,2,1,0:T(8,128)(2,1)S(1)}, u32[]{:S(2)}, u32[]{:S(2)}) collective-permute-start(bf16[4,16,8,128]{3,2,1,0:T(8,128)(2,1)S(1)} %get-tuple-element.34), channel_id=1, source_target_pairs={{0,2},{1,3},{2,0},{3,1},{4,6},{5,7},{6,4},{7,5},{8,10},{9,11},{10,... | collective-permute-start | bytes 393224 | tf_op jit(solution)/shard_map/ppermute | solution.py:391
  12.4 5.3 %collective-permute-start.8 = (bf16[1,16,8,128]{3,2,1,0:T(8,128)(2,1)S(1)}, bf16[1,16,8,128]{3,2,1,0:T(8,128)(2,1)S(1)}, u32[]{:S(2)}, u32[]{:S(2)}) collective-permute-start(bf16[1,16,8,128]{3,2,1,0:T(8,128)(2,1)S(1)} %get-tuple-element.43), channel_id=1, source_target_pairs={{0,28},{4,24},{8,20},{12,16},{16,12},{20,8},{24,4},{28,0},{1,29},{... | collective-permute-start | bytes 98312 | tf_op jit(solution)/shard_map/ppermute | solution.py:391
  14.9 4.3 %collective-permute-start.6 = (bf16[1,16,8,128]{3,2,1,0:T(8,128)(2,1)S(1)}, bf16[1,16,8,128]{3,2,1,0:T(8,128)(2,1)S(1)}, u32[]{:S(2)}, u32[]{:S(2)}) collective-permute-start(bf16[1,16,8,128]{3,2,1,0:T(8,128)(2,1)S(1)} %get-tuple-element.44), channel_id=1, source_target_pairs={{0,20},{4,16},{8,28},{12,24},{16,4},{20,0},{24,12},{28,8},{1,21},{... | collective-permute-start | bytes 98312 | tf_op jit(solution)/shard_map/ppermute | solution.py:391
  15.4 5.2 %collective-permute-start.4 = (bf16[1,16,8,128]{3,2,1,0:T(8,128)(2,1)S(1)}, bf16[1,16,8,128]{3,2,1,0:T(8,128)(2,1)S(1)}, u32[]{:S(2)}, u32[]{:S(2)}) collective-permute-start(bf16[1,16,8,128]{3,2,1,0:T(8,128)(2,1)S(1)} %get-tuple-element.45), channel_id=1, source_target_pairs={{0,12},{4,8},{8,4},{12,0},{16,28},{20,24},{24,20},{28,16},{1,13},{... | collective-permute-start | bytes 98312 | tf_op jit(solution)/shard_map/ppermute | solution.py:391
  16.8 6.0 %collective-permute-start.3 = (bf16[1,16,8,128]{3,2,1,0:T(8,128)(2,1)S(1)}, bf16[1,16,8,128]{3,2,1,0:T(8,128)(2,1)S(1)}, u32[]{:S(2)}, u32[]{:S(2)}) collective-permute-start(bf16[1,16,8,128]{3,2,1,0:T(8,128)(2,1)S(1)} %get-tuple-element.46), channel_id=1, source_target_pairs={{0,4},{4,0},{8,12},{12,8},{16,20},{20,16},{24,28},{28,24},{1,5},{5... | collective-permute-start | bytes 98312 | tf_op jit(solution)/shard_map/ppermute | solution.py:391
  17.7 5.2 %collective-permute-start.9 = (bf16[1,16,8,128]{3,2,1,0:T(8,128)(2,1)S(1)}, bf16[1,16,8,128]{3,2,1,0:T(8,128)(2,1)S(1)}, u32[]{:S(2)}, u32[]{:S(2)}) collective-permute-start(bf16[1,16,8,128]{3,2,1,0:T(8,128)(2,1)S(1)} %collective-permute-done.8), channel_id=1, source_target_pairs={{0,4},{4,0},{8,12},{12,8},{16,20},{20,16},{24,28},{28,24},{1,5},{5... | collective-permute-start | bytes 98312 | tf_op jit(solution)/shard_map/ppermute | solution.py:391
  19.1 3.7 %collective-permute-start.7 = (bf16[1,16,8,128]{3,2,1,0:T(8,128)(2,1)S(1)}, bf16[1,16,8,128]{3,2,1,0:T(8,128)(2,1)S(1)}, u32[]{:S(2)}, u32[]{:S(2)}) collective-permute-start(bf16[1,16,8,128]{3,2,1,0:T(8,128)(2,1)S(1)} %collective-permute-done.6), channel_id=1, source_target_pairs={{0,4},{4,0},{8,12},{12,8},{16,20},{20,16},{24,28},{28,24},{1,5},{5... | collective-permute-start | bytes 98312 | tf_op jit(solution)/shard_map/ppermute | solution.py:391
  20.6 2.3 %collective-permute-start.5 = (bf16[1,16,8,128]{3,2,1,0:T(8,128)(2,1)S(1)}, bf16[1,16,8,128]{3,2,1,0:T(8,128)(2,1)S(1)}, u32[]{:S(2)}, u32[]{:S(2)}) collective-permute-start(bf16[1,16,8,128]{3,2,1,0:T(8,128)(2,1)S(1)} %collective-permute-done.4), channel_id=1, source_target_pairs={{0,4},{4,0},{8,12},{12,8},{16,20},{20,16},{24,28},{28,24},{1,5},{5... | collective-permute-start | bytes 98312 | tf_op jit(solution)/shard_map/ppermute | solution.py:391
  24.7 4.9 %collective-permute-start.10 = (bf16[1,16,8,128]{3,2,1,0:T(8,128)(2,1)S(1)}, bf16[1,16,8,128]{3,2,1,0:T(8,128)(2,1)S(1)}, u32[]{:S(2)}, u32[]{:S(2)}) collective-permute-start(bf16[1,16,8,128]{3,2,1,0:T(8,128)(2,1)S(1)} %bitcast.24), channel_id=1, source_target_pairs={{0,8},{4,12},{8,0},{12,4},{16,24},{20,28},{24,16},{28,20},{1,9},{5... | collective-permute-start | bytes 98312 | tf_op jit(solution)/shard_map/ppermute | solution.py:391
  24.8 4.8 %collective-permute-start.11 = (bf16[1,16,8,128]{3,2,1,0:T(8,128)(2,1)S(1)}, bf16[1,16,8,128]{3,2,1,0:T(8,128)(2,1)S(1)}, u32[]{:S(2)}, u32[]{:S(2)}) collective-permute-start(bf16[1,16,8,128]{3,2,1,0:T(8,128)(2,1)S(1)} %bitcast.23), channel_id=1, source_target_pairs={{0,16},{4,20},{8,24},{12,28},{16,0},{20,4},{24,8},{28,12},{1,17},{... | collective-permute-start | bytes 98312 | tf_op jit(solution)/shard_map/ppermute | solution.py:391
  27.3 5.7 %collective-permute-start.12 = (bf16[1,16,8,128]{3,2,1,0:T(8,128)(2,1)S(1)}, bf16[1,16,8,128]{3,2,1,0:T(8,128)(2,1)S(1)}, u32[]{:S(2)}, u32[]{:S(2)}) collective-permute-start(bf16[1,16,8,128]{3,2,1,0:T(8,128)(2,1)S(1)} %bitcast.25), channel_id=1, source_target_pairs={{0,24},{4,28},{8,16},{12,20},{16,8},{20,12},{24,0},{28,4},{1,25},{... | collective-permute-start | bytes 98312 | tf_op jit(solution)/shard_map/ppermute | solution.py:391
  33.1 6.2 %collective-permute-start.15 = (bf16[4,16,8,128]{3,2,1,0:T(8,128)(2,1)S(1)}, bf16[4,16,8,128]{3,2,1,0:T(8,128)(2,1)S(1)}, u32[]{:S(2)}, u32[]{:S(2)}) collective-permute-start(bf16[4,16,8,128]{3,2,1,0:T(8,128)(2,1)S(1)} %pad_maximum_fusion.quarter), channel_id=1, source_target_pairs={{0,3},{1,2},{2,1},{3,0},{4,7},{5,6},{6,5},{7,4},{8,11},{9,10},{10,... | collective-permute-start | bytes 393224 | tf_op jit(solution)/shard_map/ppermute | solution.py:391
  34.8 5.4 %collective-permute-start.14 = (bf16[4,16,8,128]{3,2,1,0:T(8,128)(2,1)S(1)}, bf16[4,16,8,128]{3,2,1,0:T(8,128)(2,1)S(1)}, u32[]{:S(2)}, u32[]{:S(2)}) collective-permute-start(bf16[4,16,8,128]{3,2,1,0:T(8,128)(2,1)S(1)} %pad_maximum_fusion.quarter), channel_id=1, source_target_pairs={{0,1},{1,0},{2,3},{3,2},{4,5},{5,4},{6,7},{7,6},{8,9},{9,8},{10,11... | collective-permute-start | bytes 393224 | tf_op jit(solution)/shard_map/ppermute | solution.py:391
  35.3 5.4 %collective-permute-start.13 = (bf16[4,16,8,128]{3,2,1,0:T(8,128)(2,1)S(1)}, bf16[4,16,8,128]{3,2,1,0:T(8,128)(2,1)S(1)}, u32[]{:S(2)}, u32[]{:S(2)}) collective-permute-start(bf16[4,16,8,128]{3,2,1,0:T(8,128)(2,1)S(1)} %pad_maximum_fusion.quarter), channel_id=1, source_target_pairs={{0,2},{1,3},{2,0},{3,1},{4,6},{5,7},{6,4},{7,5},{8,10},{9,11},{10,... | collective-permute-start | bytes 393224 | tf_op jit(solution)/shard_map/ppermute | solution.py:391
